TPU v7x, 32 devices: a whole 2x2x4 slice. The times are simulated.
32 devices in a mesh: row: 8 (over z, y), leaf: 4 (over x, core).
Axes of the slice: x: 2, y: 2, z: 4, core: 2. Of those that a mesh axis runs over, the one named last changes fastest.
Arguments:
- leaf_index: int32 [8192, 256], P('row', 'leaf'), may hold values from 0 to 63
- targets: float32 [8192, 64], P('row'), may hold values from -6 to 6
Outputs:
- solution: float32 [16384, 64], P('leaf')
- residual: float32 [16384, 64], P('leaf')
All inputs are finite; a program needn't handle non-finite values.
Results may differ from a plain program's by a relative error of at most 0.0003.
Values sent between devices are 32-bit elements; how exact they have to be, the bound alone decides.
No kernel may reach another device: no remote copies, remote signals or barrier semaphores. Data moves between devices by JAX's collectives and lax.ppermute only.
A program may use at most 64 MiB of HBM per device.

v0:
```python
import math

import jax
import jax.numpy as jnp
from jax import lax
from jax.sharding import PartitionSpec as P

LEAVES = 64
ITERS = 2


ridge_weight = 1.0


def indicator(leaf_index, start, count):
    columns = start + jnp.arange(count, dtype=jnp.int32)
    trees = columns // LEAVES
    which = columns % LEAVES
    picked = jnp.take(leaf_index, trees, axis=1)
    return (picked == which[None, :]).astype(jnp.float32)


def forward_local(leaf_index, vector):
    columns = vector.shape[0]
    block_cols = math.gcd(512, columns)

    def step(index, running):
        start = index * block_cols
        marks = indicator(leaf_index, start, block_cols)
        piece = lax.dynamic_slice_in_dim(vector, start, block_cols, 0)
        return running + jnp.dot(
            marks, piece, precision=lax.Precision.HIGHEST, preferred_element_type=jnp.float32
        )

    running = jnp.zeros((leaf_index.shape[0], vector.shape[1]), jnp.float32)
    return lax.fori_loop(0, columns // block_cols, step, running)


def backward_range(leaf_index, values, start, count):
    block_cols = math.gcd(512, count)

    def block(index):
        marks = indicator(leaf_index, start + index * block_cols, block_cols)
        return lax.dot_general(
            marks,
            values,
            (((0,), (0,)), ((), ())),
            precision=lax.Precision.HIGHEST,
            preferred_element_type=jnp.float32,
        )

    blocks = lax.map(block, jnp.arange(count // block_cols, dtype=jnp.int32))
    return blocks.reshape(count, values.shape[1])


def per_device(leaf_index, targets):
    rows_dev = leaf_index.shape[0]
    columns = leaf_index.shape[1] * LEAVES
    scale = (LEAVES / (rows_dev * lax.axis_size("row"))) ** 0.5

    def normal(values):
        local_term = backward_range(leaf_index, values, 0, columns)
        return scale * lax.psum(local_term, "row")

    def total(value):
        return lax.psum(value, "leaf")

    residual = normal(targets)
    solution = jnp.zeros_like(residual)
    direction = residual
    norm_now = total(jnp.sum(residual * residual))
    for step in range(ITERS):
        image = (
            normal(scale * lax.psum(forward_local(leaf_index, direction), "leaf"))
            + ridge_weight * direction
        )
        alpha = norm_now / total(jnp.sum(direction * image))
        solution = solution + alpha * direction
        residual = residual - alpha * image
        norm_next = total(jnp.sum(residual * residual))
        direction = residual + norm_next / norm_now * direction
        norm_now = norm_next
    return (solution, residual)


def solution(mesh):
    return jax.shard_map(
        per_device,
        mesh=mesh,
        in_specs=(P("row", "leaf"), P("row", None)),
        out_specs=(P("leaf", None), P("leaf", None)),
        check_vma=False,
    )
```

profile of v0, /device:TPU:0, one launch (start us, length us, event | category | flops | bytes accessed | tf_op | source)
XLA Modules:
  0.0 664.0 jit_solution(8274413344973260972)
XLA Ops:
  8.3 83.5 %while.68 = (s32[]{:T(128)}, f32[8,512,64]{1,0,2:T(8,128)}, s32[8]{0:T(128)S(1)}, s32[1024,64]{0,1:T(8,128)}, f32[1024,64]{0,1:T(8,128)}, /*index=5*/s32[]{:T(128)}, s32[1]{0:T(128)}, s32[]{:T(128)}) while((s32[]{:T(128)}, f32[8,512,64]{1,0,2:T(8,128)}, s32[8]{0:T(128)S(1)}, s32[1024,64]{0,1:T(8,128)}, f32[1024,64]{0,1:T(8,128)}, ...), condition=%wide.region_1.3_spmd, body=%wide.region_0.2_spmd.sunk | while | flops 403725824 | bytes 8273045 | solution.py:52
  9.7 3.8 gather_fusion
  20.2 3.8 gather_fusion
  25.5 3.7 dynamic_update_slice.22
  30.6 3.8 gather_fusion
  35.9 3.7 dynamic_update_slice.22
  41.0 3.8 gather_fusion
  51.5 3.8 gather_fusion
  56.8 3.7 dynamic_update_slice.22
  61.9 3.8 gather_fusion
  67.2 3.7 dynamic_update_slice.22
  72.4 3.8 gather_fusion
  77.7 3.7 dynamic_update_slice.22
  82.8 3.8 gather_fusion
  94.7 81.2 %all-reduce.7.cloned.1.call-done = f32[4096,64]{0,1:T(8,128)} async-done(((f32[4096,64]{0,1:T(8,128)}), f32[4096,64]{0,1:T(8,128)}) %all-reduce.7.cloned.1.call-update) | async-done | bytes 1048592 | tf_op jit(solution)/shard_map/psum | solution.py:63
  178.2 31.5 %while.71 = (s32[]{:T(128)}, f32[1024,64]{0,1:T(8,128)S(1)}, s32[1024,64]{0,1:T(8,128)S(1)}, f32[4096,64]{0,1:T(8,128)}, s32[]{:T(128)}, /*index=5*/s32[]{:T(128)}, s32[]{:T(128)}, s32[]{:T(128)}) while((s32[]{:T(128)}, f32[1024,64]{0,1:T(8,128)S(1)}, s32[1024,64]{0,1:T(8,128)S(1)}, f32[4096,64]{0,1:T(8,128)}, s32[]{:T(128)}, ...), condition=%wide.region_6.8_spmd.clone, body=%wide.region_5.7_spmd.clone.sunk | while | flops 403856896 | bytes 6962329 | solution.py:36
  210.5 32.0 %all-reduce.9.cloned.1.call-done = f32[1024,64]{0,1:T(8,128)} async-done(((f32[1024,64]{0,1:T(8,128)}), f32[1024,64]{0,1:T(8,128)}) %all-reduce.9.cloned.1.call-update) | async-done | bytes 262160 | tf_op jit(solution)/shard_map/psum | solution.py:74
  244.8 68.2 %while.69 = (s32[]{:T(128)}, f32[8,512,64]{1,0,2:T(8,128)}, s32[8]{0:T(128)S(1)}, s32[1024,64]{0,1:T(8,128)S(1)}, f32[1024,64]{1,0:T(8,128)S(1)}, /*index=5*/s32[]{:T(128)}, s32[1]{0:T(128)}, s32[]{:T(128)}) while((s32[]{:T(128)}, f32[8,512,64]{1,0,2:T(8,128)}, s32[8]{0:T(128)S(1)}, s32[1024,64]{0,1:T(8,128)S(1)}, f32[1024,64]{1,0:T(8,128)S(1)}, ...), condition=%wide.region_9.11_spmd, body=%wide.region_8.10_spmd.sunk | while | flops 403725824 | bytes 7224441 | solution.py:52
  249.6 3.7 dynamic_update_slice.23
  258.1 3.7 dynamic_update_slice.23
  266.6 3.7 dynamic_update_slice.23
  283.7 3.7 dynamic_update_slice.23
  292.2 3.7 dynamic_update_slice.23
  300.7 3.7 dynamic_update_slice.23
  315.9 78.3 %all-reduce.11.cloned.1.call-done = f32[4096,64]{0,1:T(8,128)} async-done(((f32[4096,64]{0,1:T(8,128)}), f32[4096,64]{0,1:T(8,128)}) %all-reduce.11.cloned.1.call-update) | async-done | bytes 1048592 | tf_op jit(solution)/shard_map/psum | solution.py:63
  396.5 7.1 %all-reduce = (f32[]{:T(128)}, f32[]{:T(128)}) all-reduce(f32[]{:T(128)} %get-tuple-element.487, f32[]{:T(128)} %get-tuple-element.486), channel_id=1, replica_groups=mesh['row'=8,'leaf'=4] {'leaf'}, use_global_device_ids=true, to_apply=%region_4.6 | all-reduce | flops 2 | bytes 16 | tf_op jit(solution)/shard_map/psum | solution.py:66
  405.7 6.3 psum.68
  414.4 37.6 %while.72 = (s32[]{:T(128)}, f32[1024,64]{0,1:T(8,128)}, s32[1024,64]{0,1:T(8,128)S(1)}, f32[4096,64]{0,1:T(8,128)}, s32[]{:T(128)}, /*index=5*/s32[]{:T(128)}, s32[]{:T(128)}, s32[]{:T(128)}) while((s32[]{:T(128)}, f32[1024,64]{0,1:T(8,128)}, s32[1024,64]{0,1:T(8,128)S(1)}, f32[4096,64]{0,1:T(8,128)}, s32[]{:T(128)}, ...), condition=%wide.region_16.18_spmd.clone, body=%wide.region_15.17_spmd.clone.sunk | while | flops 403856896 | bytes 6962329 | solution.py:36
  452.3 31.4 %all-reduce.13.cloned.1.call-done = f32[1024,64]{0,1:T(8,128)} async-done(((f32[1024,64]{0,1:T(8,128)}), f32[1024,64]{0,1:T(8,128)}) %all-reduce.13.cloned.1.call-update) | async-done | bytes 262160 | tf_op jit(solution)/shard_map/psum | solution.py:74
  486.7 75.9 %while.70 = (s32[]{:T(128)}, f32[8,512,64]{1,0,2:T(8,128)}, s32[8]{0:T(128)S(1)}, s32[1024,64]{0,1:T(8,128)S(1)}, f32[1024,64]{1,0:T(8,128)}, /*index=5*/s32[]{:T(128)}, s32[1]{0:T(128)}, s32[]{:T(128)}) while((s32[]{:T(128)}, f32[8,512,64]{1,0,2:T(8,128)}, s32[8]{0:T(128)S(1)}, s32[1024,64]{0,1:T(8,128)S(1)}, f32[1024,64]{1,0:T(8,128)}, ...), condition=%wide.region_19.21_spmd, body=%wide.region_18.20_spmd.sunk | while | flops 403725824 | bytes 7224441 | solution.py:52
  565.6 78.5 %all-reduce.15.cloned.1.call-done = f32[4096,64]{0,1:T(8,128)} async-done(((f32[4096,64]{0,1:T(8,128)}), f32[4096,64]{0,1:T(8,128)}) %all-reduce.15.cloned.1.call-update) | async-done | bytes 1048592 | tf_op jit(solution)/shard_map/psum | solution.py:63
  646.2 7.1 %psum.71 = f32[]{:T(128)} all-reduce(f32[]{:T(128)} %multiply_reduce_fusion), channel_id=1, replica_groups=mesh['row'=8,'leaf'=4] {'leaf'}, use_global_device_ids=true, to_apply=%region_22.24 | all-reduce | flops 1 | bytes 8 | tf_op jit(solution)/shard_map/psum | solution.py:66
  (312 shorter events, 235.1 us)
Async XLA Ops:
  7.2 168.8 %all-reduce.7.cloned.1.call-start = ((), (), s32[]{:S(2)}) async-start(), calls=%async_computation | async-start | bytes 2097152 | tf_op jit(solution)/shard_map/psum | solution.py:63
  9.7 3.9 copy-start.6
  20.2 3.9 copy-start.6
  30.6 3.9 copy-start.6
  41.0 3.9 copy-start.6
  51.5 3.9 copy-start.6
  61.9 3.9 copy-start.6
  72.4 3.9 copy-start.6
  82.8 3.9 copy-start.6
  94.7 83.6 %copy-start = (s32[1024,64]{0,1:T(8,128)S(1)}, s32[1024,64]{0,1:T(8,128)}, u32[]{:S(2)}) copy-start(s32[1024,64]{0,1:T(8,128)} %get-tuple-element.836) | copy-start | bytes 786436
  94.7 147.8 %all-reduce.9.cloned.1.call-start = ((), (), s32[]{:S(2)}) async-start(), calls=%async_computation.1 | async-start | bytes 524288 | tf_op jit(solution)/shard_map/psum | solution.py:74
  209.7 0.7 copy-start.5
  210.5 183.8 %all-reduce.11.cloned.1.call-start = ((), (), s32[]{:S(2)}) async-start(), calls=%async_computation.2 | async-start | bytes 2097152 | tf_op jit(solution)/shard_map/psum | solution.py:63
  313.0 81.3 %copy-start.1 = (f32[4096,64]{0,1:T(8,128)S(1)}, f32[4096,64]{0,1:T(8,128)}, u32[]{:S(2)}) copy-start(f32[4096,64]{0,1:T(8,128)} %all-reduce.7.cloned.1.call-done) | copy-start | bytes 3145732
  315.9 167.7 %all-reduce.13.cloned.1.call-start = ((), (), s32[]{:S(2)}) async-start(), calls=%async_computation.3 | async-start | bytes 524288 | tf_op jit(solution)/shard_map/psum | solution.py:74
  394.3 10.6 %copy-start.2 = (f32[4096,64]{0,1:T(8,128)S(1)}, f32[4096,64]{0,1:T(8,128)}, u32[]{:S(2)}) copy-start(f32[4096,64]{0,1:T(8,128)} %all-reduce.11.cloned.1.call-done) | copy-start | bytes 3145732
  452.0 192.0 %all-reduce.15.cloned.1.call-start = ((), (), s32[]{:S(2)}) async-start(), calls=%async_computation.4 | async-start | bytes 2097152 | tf_op jit(solution)/shard_map/psum | solution.py:63
  562.7 81.4 %copy-start.4 = (f32[4096,64]{0,1:T(8,128)S(1)}, f32[4096,64]{0,1:T(8,128)}, u32[]{:S(2)}) copy-start(f32[4096,64]{0,1:T(8,128)} %get-tuple-element.842) | copy-start | bytes 3145732
  565.6 88.9 %copy-start.3 = (f32[4096,64]{0,1:T(8,128)S(1)}, f32[4096,64]{0,1:T(8,128)}, u32[]{:S(2)}) copy-start(f32[4096,64]{0,1:T(8,128)} %all-reduce.11.cloned.1.call-done) | copy-start | bytes 3145732
Sparse Core Ops, SparseCore 0:
  94.8 81.0 all-reduce.6
  210.6 31.8 all-reduce.8
  316.0 78.2 all-reduce.10
  452.2 31.4 all-reduce.12
  565.7 78.3 all-reduce.14
where the time goes:
time: 667 us; the launch traced here: 664 us
  waiting for transfers between devices  301 us (45%)
  local copies, waits for them, and re-layouts  215 us (32%)
  matrix products  76.4 us (11%)
  blocking collectives  20.5 us (3%)
  loops' own time  17.9 us (3%)
  between operations  17.5 us (3%)
  other arithmetic  15.1 us (2%)
    psum x3, waiting for transfers between devices, normal(): return scale * lax.psum(local_term, 'row')  238 us
    dynamic_update_slice x48, local copies, waits for them, and re-layouts, backward_range(): blocks = lax.map(block, jnp.arange(count // block_cols, dtype=jnp.int32))  93.2 us
    gather x40, local copies, waits for them, and re-layouts, indicator(): picked = jnp.take(leaf_index, trees, axis=1)  92 us
    psum x2, waiting for transfers between devices, per_device(): lax.psum(forward_local(leaf_index, direction), 'leaf')  63.3 us
    dot_general x24, matrix products, block(): lax.dot_general(marks, values, (((0,), (0,)), ((), ())), precision=lax.Pr...  39.2 us
    dot_general x16, matrix products, step(): jnp.dot(marks, piece, precision=lax.Precision.HIGHEST, preferred_element_...  37.2 us
    psum x3, blocking collectives, total(): return lax.psum(value, 'leaf')  20.5 us
    another operation x3, loops' own time, backward_range(): blocks = lax.map(block, jnp.arange(count // block_cols, dtype=jnp.int32))  17.2 us
  transfers between devices with their start and end apart: 5, of which 5 were waited for; matrix products, arithmetic and copies ran while one was open for 0% of the time, Pallas kernels for 0%

commit v1 on v0

v1 whole, which is shorter than its diff:
```python
import jax
import jax.numpy as jnp
from jax import lax
from jax.experimental import pallas as pl
from jax.experimental.pallas import tpu as pltpu
from jax.sharding import PartitionSpec as P


LEAVES = 64
LANES = 128
PIECES = 3
TREE_BLOCK = 16
ridge_weight = 1.0
F32, BF16 = jnp.float32, jnp.bfloat16
VMEM_LIMIT = 32 * 1024 * 1024
VMEM = pl.BlockSpec(memory_space=pltpu.VMEM)


def onehot(leaves):
    trees, rows = leaves.shape
    which = lax.broadcasted_iota(jnp.int32, (LEAVES, rows), 0).astype(F32).astype(BF16)
    leaves = leaves.astype(BF16)
    one, zero = jnp.ones((LEAVES, rows), BF16), jnp.zeros((LEAVES, rows), BF16)
    marks = [
        jnp.where(jnp.broadcast_to(leaves[t : t + 1, :], (LEAVES, rows)) == which, one, zero)
        for t in range(trees)
    ]
    return jnp.concatenate(marks, 0)


def pieces_of(value):
    found = []
    for _ in range(PIECES):
        high = value.astype(BF16)
        found.append(high)
        value = value - high.astype(F32)
    return jnp.concatenate(found, 0)


def pieces_sum(value):
    rows = value.shape[0] // PIECES
    total = value[(PIECES - 1) * rows :]
    for index in reversed(range(PIECES - 1)):
        total = total + value[index * rows : (index + 1) * rows]
    return total


def lane_sums(value):
    groups = [value[:, at : at + LANES] for at in range(0, value.shape[1], LANES)]
    while len(groups) > 1:
        groups = [sum(groups[at : at + 2]) for at in range(0, len(groups), 2)]
    return groups[0]


def call(kernel, outs, scratch, flops, *args):
    return pl.pallas_call(
        kernel,
        out_shape=outs,
        in_specs=[VMEM] * len(args),
        out_specs=jax.tree.map(lambda _: VMEM, outs),
        scratch_shapes=scratch,
        compiler_params=pltpu.CompilerParams(vmem_limit_bytes=VMEM_LIMIT),
        cost_estimate=pl.CostEstimate(flops=flops, bytes_accessed=1 << 20, transcendentals=0),
    )(*args)


def array(*shape):
    return jax.ShapeDtypeStruct(shape, F32)


def spread(leaf_refs, offsets, trees, split_ref, out_ref, scale, before=None):
    rows = leaf_refs[0].shape[1]

    @pl.loop(0, trees // TREE_BLOCK)
    def _(step):
        total = None
        for index, (leaf_ref, offset) in enumerate(zip(leaf_refs, offsets)):
            marks = onehot(leaf_ref[pl.ds(pl.multiple_of(offset + step * TREE_BLOCK, 8), TREE_BLOCK), :])
            part = lax.dot_general(
                split_ref[:, index * rows : (index + 1) * rows],
                marks,
                (((1,), (1,)), ((), ())),
                preferred_element_type=F32,
            )
            total = part if total is None else total + part
        width = TREE_BLOCK * LEAVES
        at = pl.ds(pl.multiple_of(step * width, width), width)
        result = scale * pieces_sum(total)
        out_ref[:, at] = result if before is None else before[:, at] + result


def collect(leaf_refs, offsets, trees, split_ref, out_ref, total_ref):
    rows = leaf_refs[0].shape[1]
    total_ref[...] = jnp.zeros_like(total_ref)

    @pl.loop(0, trees // TREE_BLOCK)
    def _(step):
        width = TREE_BLOCK * LEAVES
        split = split_ref[:, pl.ds(pl.multiple_of(step * width, width), width)]
        for index, (leaf_ref, offset) in enumerate(zip(leaf_refs, offsets)):
            marks = onehot(leaf_ref[pl.ds(pl.multiple_of(offset + step * TREE_BLOCK, 8), TREE_BLOCK), :])
            at = slice(index * rows, (index + 1) * rows)
            part = jnp.dot(split, marks, preferred_element_type=F32)
            total_ref[:, at] = total_ref[:, at] + part

    out_ref[:, : total_ref.shape[1]] = pieces_sum(total_ref[...])


def solution(mesh):
    n_row, n_leaf = mesh.shape["row"], mesh.shape["leaf"]
    far_stride, near_stride = n_row // 2, 1
    row_strides = [1 << bit for bit in range(1, n_row.bit_length() - 2)]
    leaf_strides = [1 << bit for bit in range(n_leaf.bit_length() - 1)]
    n_keys = 4
    n_share = n_row // n_keys

    def swap(value, axis, stride):
        size = n_row if axis == "row" else n_leaf
        return lax.ppermute(value, axis, [(i, i ^ stride) for i in range(size)])

    def gather(value):
        far = swap(value, "row", far_stride)
        near = swap(value, "row", near_stride)
        return [value, near, far, swap(far, "row", near_stride)]

    def half_sum(value, axis, strides):
        for stride in strides[:-1]:
            value = value + swap(value, axis, stride)
        return value, swap(value, axis, strides[-1])

    def per_device(leaf_index, targets):
        width = targets.shape[1] // n_keys
        rows, trees = leaf_index.shape
        columns, span = trees * LEAVES, n_keys * rows
        scale = (LEAVES / (rows * n_row)) ** 0.5
        flops = 2 * columns * rows * 256
        row = lax.axis_index("row")
        key = (row // far_stride) * 2 + row % 2
        place = jnp.stack([key, key ^ 1, key ^ 2, key ^ 3]).astype(jnp.int32)
        split_rows = pltpu.VMEM((PIECES * width, span), BF16)
        split_columns = pltpu.VMEM((PIECES * width, columns), BF16)

        def pack(place_ref, leaf_ref, target_ref, own_ref, near_ref, far_ref):
            leaves = leaf_ref[...].astype(F32)
            chunk = lambda m: target_ref[pl.ds(pl.multiple_of(place_ref[m] * width, width), width), :]
            own_ref[:trees, :] = leaves
            own_ref[trees:, :] = chunk(0)
            near_ref[:trees, :] = leaves
            near_ref[trees:, :] = chunk(1)
            far_ref[:width, :] = chunk(2)
            far_ref[width : width + trees, :] = leaves
            far_ref[width + trees :, :] = chunk(3)

        packed = array(trees + width, rows)
        own, near, far = pl.pallas_call(
            pack,
            out_shape=(packed, packed, array(trees + 2 * width, rows)),
            in_specs=[pl.BlockSpec(memory_space=pltpu.SMEM), VMEM, VMEM],
            out_specs=(VMEM, VMEM, VMEM),
            compiler_params=pltpu.CompilerParams(vmem_limit_bytes=VMEM_LIMIT),
            name="pack",
        )(place, leaf_index.T, targets.T)
        far = swap(far, "row", far_stride)
        near = swap(near, "row", near_stride)
        both = swap(far[width:], "row", near_stride)
        leaves, offsets = (own, near, far, both), (0, 0, width, 0)

        def first(own_ref, near_ref, out_ref, split_ref):
            for index, ref in enumerate((own_ref, near_ref)):
                split_ref[:, index * rows : (index + 1) * rows] = pieces_of(ref[trees:, :])
            spread((own_ref, near_ref), offsets[:2], trees, split_ref, out_ref, scale)

        def second(far_ref, both_ref, before_ref, out_ref, split_ref):
            split_ref[:, :rows] = pieces_of(far_ref[:width, :])
            split_ref[:, rows : 2 * rows] = pieces_of(both_ref[trees:, :])
            spread((far_ref, both_ref), offsets[2:], trees, split_ref, out_ref, scale, before_ref)

        b_shape = array(width, columns)
        part = call(first, b_shape, [split_rows], 2 * flops, own, near)
        part = call(second, b_shape, [split_rows], 2 * flops, far, both, part)
        mine, theirs = half_sum(part, "row", row_strides)

        def forward0(l0, l1, l2, l3, mine_ref, theirs_ref, out_ref, base_ref, split_ref, total_ref):
            base = mine_ref[...] + theirs_ref[...]
            base_ref[...] = base
            split_ref[...] = pieces_of(base)
            collect((l0, l1, l2, l3), offsets, trees, split_ref, out_ref, total_ref)
            out_ref[:, span:] = lane_sums(base * base)

        total_rows = pltpu.VMEM((PIECES * width, span), F32)
        part, b0 = call(
            forward0,
            (array(width, span + LANES), b_shape),
            [split_columns, total_rows],
            4 * flops,
            *leaves,
            mine,
            theirs,
        )
        mine, theirs = half_sum(part, "leaf", leaf_strides)

        def backward1(l0, l1, l2, l3, mine_ref, theirs_ref, out_ref, rows_ref, split_ref):
            value = mine_ref[:, :span] + theirs_ref[:, :span]
            rows_ref[...] = value
            split_ref[...] = pieces_of(value)
            out_ref[:, columns : columns + LANES] = (scale * scale) * lane_sums(value * value)
            out_ref[:, columns + LANES :] = (mine_ref[:, span:] + theirs_ref[:, span:]) * (1.0 / n_share)
            spread((l0, l1, l2, l3), offsets, trees, split_ref, out_ref, scale * scale)

        part, w0 = call(
            backward1,
            (array(width, columns + 2 * LANES), array(width, span)),
            [split_rows],
            4 * flops,
            *leaves,
            mine,
            theirs,
        )
        mine, theirs = half_sum(part, "row", row_strides)

        def step_of(norm, curve):
            return jnp.where(norm > 0.0, norm / (curve + ridge_weight * norm), 1.0)

        def scalar(value):
            return jnp.sum(value, axis=(0, 1), keepdims=True)

        def forward1(
            l0, l1, l2, l3, mine_ref, theirs_ref, base_ref, out_ref, res_ref, split_ref, total_ref
        ):
            tail = mine_ref[:, columns:] + theirs_ref[:, columns:]
            theta = step_of(scalar(tail[:, LANES:]), scalar(tail[:, :LANES]))
            base = base_ref[...]
            image = mine_ref[:, :columns] + theirs_ref[:, :columns] + ridge_weight * base
            res = base - theta * image
            res_ref[:, :columns] = res
            res_ref[:, columns:] = tail
            split_ref[...] = pieces_of(res)
            collect((l0, l1, l2, l3), offsets, trees, split_ref, out_ref, total_ref)
            out_ref[:, span : span + LANES] = lane_sums(res * res)
            out_ref[:, span + LANES :] = lane_sums(res * base)

        part, res = call(
            forward1,
            (array(width, span + 2 * LANES), array(width, columns + 2 * LANES)),
            [split_columns, total_rows],
            4 * flops,
            *leaves,
            mine,
            theirs,
            b0,
        )
        mine, theirs = half_sum(part, "leaf", leaf_strides)

        def backward2(l0, l1, l2, l3, mine_ref, theirs_ref, rows_ref, out_ref, split_ref):
            value = mine_ref[:, :span] + theirs_ref[:, :span]
            split_ref[...] = pieces_of(value)
            out_ref[:, columns : columns + LANES] = (scale * scale) * lane_sums(value * value)
            out_ref[:, columns + LANES : columns + 2 * LANES] = (scale * scale) * lane_sums(
                value * rows_ref[...]
            )
            out_ref[:, columns + 2 * LANES :] = (mine_ref[:, span:] + theirs_ref[:, span:]) * (
                1.0 / n_share
            )
            spread((l0, l1, l2, l3), offsets, trees, split_ref, out_ref, scale * scale)

        part = call(
            backward2,
            array(width, columns + 4 * LANES),
            [split_rows],
            4 * flops,
            *leaves,
            mine,
            theirs,
            w0,
        )
        mine, theirs = half_sum(part, "row", row_strides)
        b2 = mine + theirs

        def combine(place_ref, *refs):
            bases, ress, seconds = (refs[k * n_keys : (k + 1) * n_keys] for k in range(3))
            solution_ref, residual_ref = refs[3 * n_keys :]
            tail = lambda ref, at: scalar(ref[:, columns + at * LANES : columns + (at + 1) * LANES])
            keys = range(n_keys)
            b = [tail(ress[m], 0) for m in keys]
            a = [tail(ress[m], 1) for m in keys]
            e, f, c, d = ([tail(seconds[m], at) for m in keys] for at in range(4))
            norm0 = sum(a)
            alpha0 = norm0 / (sum(b) + ridge_weight * norm0)
            theta = [step_of(a[m], b[m]) for m in keys]
            rho = [alpha0 / theta[m] for m in keys]
            square = lambda x, y, xx, xy, yy: x * x * xx + 2.0 * x * y * xy + y * y * yy
            norm1 = sum(square(rho[m], 1.0 - rho[m], c[m], d[m], a[m]) for m in keys)
            beta = norm1 / norm0
            other = [1.0 - rho[m] + beta for m in keys]
            curve = sum(
                square(rho[m], other[m], e[m], f[m], b[m])
                + ridge_weight * square(rho[m], other[m], c[m], d[m], a[m])
                for m in keys
            )
            alpha1 = norm1 / curve
            for m in keys:
                at = pl.ds(pl.multiple_of(place_ref[m] * width, width), width)
                base, res, image = bases[m][...], ress[m][:, :columns], seconds[m][:, :columns]
                solution_ref[at, :] = (alpha0 + alpha1 * other[m]) * base + (alpha1 * rho[m]) * res
                residual_ref[at, :] = (
                    ((1.0 - rho[m]) - alpha1 * other[m] / theta[m]) * base
                    + (rho[m] + alpha1 * (other[m] / theta[m] - ridge_weight * rho[m])) * res
                    - (alpha1 * rho[m]) * image
                )

        out = array(n_keys * width, columns)
        result = pl.pallas_call(
            combine,
            out_shape=(out, out),
            in_specs=[pl.BlockSpec(memory_space=pltpu.SMEM)] + [VMEM] * (3 * n_keys),
            out_specs=(VMEM, VMEM),
            compiler_params=pltpu.CompilerParams(vmem_limit_bytes=VMEM_LIMIT),
            name="combine",
        )(place, *gather(b0), *gather(res), *gather(b2))
        return tuple(value.T for value in result)

    return jax.shard_map(
        per_device,
        mesh=mesh,
        in_specs=(P("row", "leaf"), P("row", None)),
        out_specs=(P("leaf", None), P("leaf", None)),
        check_vma=False,
    )
```

time: 667 us -> 177 us (0.27)
  local copies, waits for them, and re-layouts: 215 us -> 1.92 us
  waiting for transfers between devices: 301 us -> 97.5 us
  matrix products: 76.4 us -> 0 us
  Pallas kernels: 0 us -> 47.5 us
  starting transfers between devices: 0.38 us -> 29.1 us
  blocking collectives: 20.5 us -> 0 us
  loops' own time: 17.9 us -> 0 us
  between operations: 17.5 us -> 0.74 us
  other arithmetic: 15.1 us -> 0.17 us
    psum x5 -> x0, waiting for transfers between devices: 301 us -> none  [the longest x3 238 us: normal(): return scale * lax.psum(local_term, 'row')]
    ppermute x0 -> x19, waiting for transfers between devices: none -> 97.5 us  [swap(): return lax.ppermute(value, axis, [(i, i ^ stride) for i in range(size)])]
    dynamic_update_slice x48 -> x0, local copies, waits for them, and re-layouts: 93.2 us -> none  [backward_range(): blocks = lax.map(block, jnp.arange(count // block_cols, dtype=jnp.int32))]
    gather x40 -> x0, local copies, waits for them, and re-layouts: 92 us -> none  [indicator(): picked = jnp.take(leaf_index, trees, axis=1)]
    dot_general x40 -> x0, matrix products: 76.4 us -> none  [the longest x24 39.2 us: block(): lax.dot_general(marks, values, (((0,), (0,)), ((), ())), precision=lax.Pr...]
    pallas_call x0 -> x8, Pallas kernels: none -> 47.5 us  [the longest x6 44.7 us: call(): pl.pallas_call(kernel, out_shape=outs, in_specs=[VMEM] * len(args), out_s...]
    ppermute x0 -> x19, starting transfers between devices: none -> 29.1 us  [swap(): return lax.ppermute(value, axis, [(i, i ^ stride) for i in range(size)])]
    psum x3 -> x0, blocking collectives: 20.5 us -> none  [total(): return lax.psum(value, 'leaf')]
  transfers between devices with their start and end apart: 5 -> 19, of which waited for: 5 -> 12; matrix products, arithmetic and copies ran while one was open for 0% -> 0% of each run, Pallas kernels for 0% -> 3%
where the time goes in v1:
time: 177 us
  waiting for transfers between devices  97.5 us (55%)
  Pallas kernels  47.5 us (27%)
  starting transfers between devices  29.1 us (16%)
  local copies, waits for them, and re-layouts  1.92 us (1%)
    ppermute x19, waiting for transfers between devices, swap(): return lax.ppermute(value, axis, [(i, i ^ stride) for i in range(size)])  97.5 us
    pallas_call x6, Pallas kernels, call(): pl.pallas_call(kernel, out_shape=outs, in_specs=[VMEM] * len(args), out_s...  44.7 us
    ppermute x19, starting transfers between devices, swap(): return lax.ppermute(value, axis, [(i, i ^ stride) for i in range(size)])  29.1 us
  transfers between devices with their start and end apart: 19, of which 12 were waited for; matrix products, arithmetic and copies ran while one was open for 0% of the time, Pallas kernels for 3%

profile of v1, /device:TPU:0, one launch (start us, length us, event | category | flops | bytes accessed | tf_op | source)
XLA Modules:
  0.0 176.9 jit_solution(15617765291265564)
XLA Ops:
  3.2 4.1 %collective-permute-start.1 = (f32[96,1024]{1,0:T(8,128)S(1)}, f32[96,1024]{1,0:T(8,128)S(1)}, u32[]{:S(2)}, u32[]{:S(2)}) collective-permute-start(f32[96,1024]{1,0:T(8,128)S(1)} %get-tuple-element.15), channel_id=1, source_target_pairs={{0,16},{4,20},{8,24},{12,28},{16,0},{20,4},{24,8},{28,12},{1,17},{... | collective-permute-start | bytes 1179656 | tf_op jit(solution)/shard_map/ppermute | solution.py:119
  7.4 1.5 collective-permute-start
  8.9 16.0 %collective-permute-done.1.far_ref.l2 = f32[96,1024]{1,0:T(8,128)S(1)} collective-permute-done((f32[96,1024]{1,0:T(8,128)S(1)}, f32[96,1024]{1,0:T(8,128)S(1)}, u32[]{:S(2)}, u32[]{:S(2)}) %collective-permute-start.1) | collective-permute-done | bytes 393248 | tf_op jit(solution)/shard_map/ppermute | solution.py:119
  24.9 1.6 collective-permute-start.2
  26.6 5.4 %shard_map.41.before_ref = f32[16,4096]{1,0:T(8,128)S(1)} custom-call(f32[80,1024]{1,0:T(8,128)S(1)} %get-tuple-element.13.own_ref.l0, f32[80,1024]{1,0:T(8,128)S(1)} %collective-permute-done.near_ref.l1), custom_call_target="tpu_custom_call" | custom-call | flops 4294967296 | bytes 1048576 | tf_op jit(solution)/shard_map/pallas_call | solution.py:56
  32.0 1.9 %collective-permute-done.2.both_ref.l3 = f32[80,1024]{1,0:T(8,128)S(1)} collective-permute-done((f32[80,1024]{1,0:T(8,128)S(1)}, f32[80,1024]{1,0:T(8,128)S(1)}, u32[]{:S(2)}, u32[]{:S(2)}) %collective-permute-start.2) | collective-permute-done | bytes 327712 | tf_op jit(solution)/shard_map/ppermute | solution.py:119
  33.9 5.4 %shard_map.42.mine_ref = f32[16,4096]{1,0:T(8,128)S(1)} custom-call(f32[96,1024]{1,0:T(8,128)S(1)} %collective-permute-done.1.far_ref.l2, f32[80,1024]{1,0:T(8,128)S(1)} %collective-permute-done.2.both_ref.l3, f32[16,4096]{1,0:T(8,128)S(1)} %shard_map.41.before_ref), custom_call_target="tpu_custom_call" | custom-call | flops 4294967296 | bytes 1048576 | tf_op jit(solution)/shard_map/pallas_call | solution.py:56
  39.3 1.5 collective-permute-start.3
  40.8 5.6 %collective-permute-done.3.theirs_ref = f32[16,4096]{1,0:T(8,128)S(1)} collective-permute-done((f32[16,4096]{1,0:T(8,128)S(1)}, f32[16,4096]{1,0:T(8,128)S(1)}, u32[]{:S(2)}, u32[]{:S(2)}) %collective-permute-start.3) | collective-permute-done | bytes 262176 | tf_op jit(solution)/shard_map/ppermute | solution.py:119
  46.4 6.5 %shard_map.43 = (f32[16,4224]{1,0:T(8,128)S(1)}, f32[16,4096]{1,0:T(8,128)S(1)}) custom-call(f32[80,1024]{1,0:T(8,128)S(1)} %get-tuple-element.13.own_ref.l0, f32[80,1024]{1,0:T(8,128)S(1)} %collective-permute-done.near_ref.l1, f32[96,1024]{1,0:T(8,128)S(1)} %collective-permute-done.1.far_ref.l2, f32[80,1024]{1,0:T(8,128)S(1)} %collective-permute-done.2.both_ref.l3, ...), custom_call_target="tpu_custom_call" | custom-call | flops 8589934592 | bytes 1048576 | tf_op jit(solution)/shard_map/pallas_call | solution.py:56
  53.0 1.5 collective-permute-done.7
  54.6 1.6 collective-permute-start.8
  56.1 7.0 %collective-permute-done.8.theirs_ref = f32[16,4224]{1,0:T(8,128)S(1)} collective-permute-done((f32[16,4224]{1,0:T(8,128)S(1)}, f32[16,4224]{1,0:T(8,128)S(1)}, u32[]{:S(2)}, u32[]{:S(2)}) %collective-permute-start.8) | collective-permute-done | bytes 270368 | tf_op jit(solution)/shard_map/ppermute | solution.py:119
  63.2 10.4 %shard_map.44 = (f32[16,4352]{1,0:T(8,128)S(1)}, f32[16,4096]{1,0:T(8,128)S(1)}) custom-call(f32[80,1024]{1,0:T(8,128)S(1)} %get-tuple-element.13.own_ref.l0, f32[80,1024]{1,0:T(8,128)S(1)} %collective-permute-done.near_ref.l1, f32[96,1024]{1,0:T(8,128)S(1)} %collective-permute-done.1.far_ref.l2, f32[80,1024]{1,0:T(8,128)S(1)} %collective-permute-done.2.both_ref.l3, ...), custom_call_target="tpu_custom_call" | custom-call | flops 8589934592 | bytes 1048576 | tf_op jit(solution)/shard_map/pallas_call | solution.py:56
  73.5 1.8 %collective-permute-start.9 = (f32[16,4352]{1,0:T(8,128)S(1)}, f32[16,4352]{1,0:T(8,128)S(1)}, u32[]{:S(2)}, u32[]{:S(2)}) collective-permute-start(f32[16,4352]{1,0:T(8,128)S(1)} %get-tuple-element.18.mine_ref), channel_id=1, source_target_pairs={{0,8},{4,12},{8,0},{12,4},{16,24},{20,28},{24,16},{28,20},{1,9},{5... | collective-permute-start | bytes 835592 | tf_op jit(solution)/shard_map/ppermute | solution.py:119
  75.3 6.1 %collective-permute-done.9.theirs_ref = f32[16,4352]{1,0:T(8,128)S(1)} collective-permute-done((f32[16,4352]{1,0:T(8,128)S(1)}, f32[16,4352]{1,0:T(8,128)S(1)}, u32[]{:S(2)}, u32[]{:S(2)}) %collective-permute-start.9) | collective-permute-done | bytes 278560 | tf_op jit(solution)/shard_map/ppermute | solution.py:119
  81.4 6.7 %shard_map.45 = (f32[16,4352]{1,0:T(8,128)S(1)}, f32[16,4352]{1,0:T(8,128)S(1)}) custom-call(f32[80,1024]{1,0:T(8,128)S(1)} %get-tuple-element.13.own_ref.l0, f32[80,1024]{1,0:T(8,128)S(1)} %collective-permute-done.near_ref.l1, f32[96,1024]{1,0:T(8,128)S(1)} %collective-permute-done.1.far_ref.l2, f32[80,1024]{1,0:T(8,128)S(1)} %collective-permute-done.2.both_ref.l3, ...), custom_call_target="tpu_custom_call" | custom-call | flops 8589934592 | bytes 1048576 | tf_op jit(solution)/shard_map/pallas_call | solution.py:56
  88.2 1.5 collective-permute-done.13
  89.8 1.6 collective-permute-start.14
  91.3 7.2 %collective-permute-done.14.theirs_ref = f32[16,4352]{1,0:T(8,128)S(1)} collective-permute-done((f32[16,4352]{1,0:T(8,128)S(1)}, f32[16,4352]{1,0:T(8,128)S(1)}, u32[]{:S(2)}, u32[]{:S(2)}) %collective-permute-start.14) | collective-permute-done | bytes 278560 | tf_op jit(solution)/shard_map/ppermute | solution.py:119
  98.5 10.4 %shard_map.46 = f32[16,4608]{1,0:T(8,128)S(1)} custom-call(f32[80,1024]{1,0:T(8,128)S(1)} %get-tuple-element.13.own_ref.l0, f32[80,1024]{1,0:T(8,128)S(1)} %collective-permute-done.near_ref.l1, f32[96,1024]{1,0:T(8,128)S(1)} %collective-permute-done.1.far_ref.l2, f32[80,1024]{1,0:T(8,128)S(1)} %collective-permute-done.2.both_ref.l3, ...), custom_call_target="tpu_custom_call" | custom-call | flops 8589934592 | bytes 1048576 | tf_op jit(solution)/shard_map/pallas_call | solution.py:56
  108.9 1.8 %collective-permute-start.15 = (f32[16,4608]{1,0:T(8,128)S(1)}, f32[16,4608]{1,0:T(8,128)S(1)}, u32[]{:S(2)}, u32[]{:S(2)}) collective-permute-start(f32[16,4608]{1,0:T(8,128)S(1)} %shard_map.46), channel_id=1, source_target_pairs={{0,8},{4,12},{8,0},{12,4},{16,24},{20,28},{24,16},{28,20},{1,9},{5... | collective-permute-start | bytes 884744 | tf_op jit(solution)/shard_map/ppermute | solution.py:119
  110.7 6.5 %collective-permute-done.15 = f32[16,4608]{1,0:T(8,128)S(1)} collective-permute-done((f32[16,4608]{1,0:T(8,128)S(1)}, f32[16,4608]{1,0:T(8,128)S(1)}, u32[]{:S(2)}, u32[]{:S(2)}) %collective-permute-start.15) | collective-permute-done | bytes 294944 | tf_op jit(solution)/shard_map/ppermute | solution.py:119
  117.2 3.4 %collective-permute-start.17 = (f32[16,4608]{1,0:T(8,128)S(1)}, f32[16,4608]{1,0:T(8,128)S(1)}, u32[]{:S(2)}, u32[]{:S(2)}) collective-permute-start(f32[16,4608]{1,0:T(8,128)S(1)} %add.21.refs_8_), channel_id=1, source_target_pairs={{0,16},{4,20},{8,24},{12,28},{16,0},{20,4},{24,8},{28,12},{1,17},{... | collective-permute-start | bytes 884744 | tf_op jit(solution)/shard_map/ppermute | solution.py:119
  120.7 2.8 %collective-permute-start.5 = (f32[16,4096]{1,0:T(8,128)S(1)}, f32[16,4096]{1,0:T(8,128)S(1)}, u32[]{:S(2)}, u32[]{:S(2)}) collective-permute-start(f32[16,4096]{1,0:T(8,128)S(1)} %get-tuple-element.16.base_ref.refs_0_), channel_id=1, source_target_pairs={{0,16},{4,20},{8,24},{12,28},{16,0},{20,4},{24,8},{28,12},{1,17},{... | collective-permute-start | bytes 786440 | tf_op jit(solution)/shard_map/ppermute | solution.py:119
  123.5 1.5 collective-permute-start.4
  125.6 19.8 %collective-permute-done.17.refs_10_ = f32[16,4608]{1,0:T(8,128)S(1)} collective-permute-done((f32[16,4608]{1,0:T(8,128)S(1)}, f32[16,4608]{1,0:T(8,128)S(1)}, u32[]{:S(2)}, u32[]{:S(2)}) %collective-permute-start.17) | collective-permute-done | bytes 294944 | tf_op jit(solution)/shard_map/ppermute | solution.py:119
  145.4 1.5 collective-permute-start.18
  146.9 8.8 %collective-permute-done.5.refs_2_ = f32[16,4096]{1,0:T(8,128)S(1)} collective-permute-done((f32[16,4096]{1,0:T(8,128)S(1)}, f32[16,4096]{1,0:T(8,128)S(1)}, u32[]{:S(2)}, u32[]{:S(2)}) %collective-permute-start.5) | collective-permute-done | bytes 262176 | tf_op jit(solution)/shard_map/ppermute | solution.py:119
  157.7 1.5 collective-permute-start.6
  159.3 15.4 %collective-permute-done.6.refs_3_ = f32[16,4096]{1,0:T(8,128)S(1)} collective-permute-done((f32[16,4096]{1,0:T(8,128)S(1)}, f32[16,4096]{1,0:T(8,128)S(1)}, u32[]{:S(2)}, u32[]{:S(2)}) %collective-permute-start.6) | collective-permute-done | bytes 262176 | tf_op jit(solution)/shard_map/ppermute | solution.py:119
  174.7 2.2 %combine.1 = (f32[64,4096]{1,0:T(8,128)}, f32[64,4096]{1,0:T(8,128)}) custom-call(s32[4]{0:T(128)S(1)} %pad_add_fusion.place_ref, f32[16,4096]{1,0:T(8,128)S(1)} %get-tuple-element.16.base_ref.refs_0_, f32[16,4096]{1,0:T(8,128)S(1)} %collective-permute-done.4.refs_1_, f32[16,4096]{1,0:T(8,128)S(1)} %collective-permute-done.5.refs_2_, ...), custom_call_target="tpu_custom_call" | custom-call | tf_op jit(solution)/shard_map/combine/pallas_call | solution.py:312
  (23 shorter events, 5.5 us)
Async XLA Ops:
  0.7 1.0 copy-start
  1.7 0.9 copy-start.1
  3.2 21.7 %collective-permute-start.1 = (f32[96,1024]{1,0:T(8,128)S(1)}, f32[96,1024]{1,0:T(8,128)S(1)}, u32[]{:S(2)}, u32[]{:S(2)}) collective-permute-start(f32[96,1024]{1,0:T(8,128)S(1)} %get-tuple-element.15), channel_id=1, source_target_pairs={{0,16},{4,20},{8,24},{12,28},{16,0},{20,4},{24,8},{28,12},{1,17},{... | collective-permute-start | bytes 1179656 | tf_op jit(solution)/shard_map/ppermute | solution.py:119
  7.4 19.2 %collective-permute-start = (f32[80,1024]{1,0:T(8,128)S(1)}, f32[80,1024]{1,0:T(8,128)S(1)}, u32[]{:S(2)}, u32[]{:S(2)}) collective-permute-start(f32[80,1024]{1,0:T(8,128)S(1)} %get-tuple-element.14), channel_id=1, source_target_pairs={{0,4},{4,0},{8,12},{12,8},{16,20},{20,16},{24,28},{28,24},{1,5},{5... | collective-permute-start | bytes 983048 | tf_op jit(solution)/shard_map/ppermute | solution.py:119
  24.9 8.9 %collective-permute-start.2 = (f32[80,1024]{1,0:T(8,128)S(1)}, f32[80,1024]{1,0:T(8,128)S(1)}, u32[]{:S(2)}, u32[]{:S(2)}) collective-permute-start(f32[80,1024]{1,0:T(8,128)S(1)} %slice.4), channel_id=1, source_target_pairs={{0,4},{4,0},{8,12},{12,8},{16,20},{20,16},{24,28},{28,24},{1,5},{5... | collective-permute-start | bytes 983048 | tf_op jit(solution)/shard_map/ppermute | solution.py:119
  39.3 7.1 %collective-permute-start.3 = (f32[16,4096]{1,0:T(8,128)S(1)}, f32[16,4096]{1,0:T(8,128)S(1)}, u32[]{:S(2)}, u32[]{:S(2)}) collective-permute-start(f32[16,4096]{1,0:T(8,128)S(1)} %shard_map.42.mine_ref), channel_id=1, source_target_pairs={{0,8},{4,12},{8,0},{12,4},{16,24},{20,28},{24,16},{28,20},{1,9},{5... | collective-permute-start | bytes 786440 | tf_op jit(solution)/shard_map/ppermute | solution.py:119
  52.9 1.6 collective-permute-start.7
  54.6 8.6 %collective-permute-start.8 = (f32[16,4224]{1,0:T(8,128)S(1)}, f32[16,4224]{1,0:T(8,128)S(1)}, u32[]{:S(2)}, u32[]{:S(2)}) collective-permute-start(f32[16,4224]{1,0:T(8,128)S(1)} %add.19.mine_ref), channel_id=1, source_target_pairs={{0,2},{1,3},{2,0},{3,1},{4,6},{5,7},{6,4},{7,5},{8,10},{9,11},{10,... | collective-permute-start | bytes 811016 | tf_op jit(solution)/shard_map/ppermute | solution.py:119
  73.5 7.9 %collective-permute-start.9 = (f32[16,4352]{1,0:T(8,128)S(1)}, f32[16,4352]{1,0:T(8,128)S(1)}, u32[]{:S(2)}, u32[]{:S(2)}) collective-permute-start(f32[16,4352]{1,0:T(8,128)S(1)} %get-tuple-element.18.mine_ref), channel_id=1, source_target_pairs={{0,8},{4,12},{8,0},{12,4},{16,24},{20,28},{24,16},{28,20},{1,9},{5... | collective-permute-start | bytes 835592 | tf_op jit(solution)/shard_map/ppermute | solution.py:119
  88.1 1.6 collective-permute-start.13
  89.8 8.8 %collective-permute-start.14 = (f32[16,4352]{1,0:T(8,128)S(1)}, f32[16,4352]{1,0:T(8,128)S(1)}, u32[]{:S(2)}, u32[]{:S(2)}) collective-permute-start(f32[16,4352]{1,0:T(8,128)S(1)} %add.20.mine_ref), channel_id=1, source_target_pairs={{0,2},{1,3},{2,0},{3,1},{4,6},{5,7},{6,4},{7,5},{8,10},{9,11},{10,... | collective-permute-start | bytes 835592 | tf_op jit(solution)/shard_map/ppermute | solution.py:119
  108.9 8.2 %collective-permute-start.15 = (f32[16,4608]{1,0:T(8,128)S(1)}, f32[16,4608]{1,0:T(8,128)S(1)}, u32[]{:S(2)}, u32[]{:S(2)}) collective-permute-start(f32[16,4608]{1,0:T(8,128)S(1)} %shard_map.46), channel_id=1, source_target_pairs={{0,8},{4,12},{8,0},{12,4},{16,24},{20,28},{24,16},{28,20},{1,9},{5... | collective-permute-start | bytes 884744 | tf_op jit(solution)/shard_map/ppermute | solution.py:119
  117.2 28.2 %collective-permute-start.17 = (f32[16,4608]{1,0:T(8,128)S(1)}, f32[16,4608]{1,0:T(8,128)S(1)}, u32[]{:S(2)}, u32[]{:S(2)}) collective-permute-start(f32[16,4608]{1,0:T(8,128)S(1)} %add.21.refs_8_), channel_id=1, source_target_pairs={{0,16},{4,20},{8,24},{12,28},{16,0},{20,4},{24,8},{28,12},{1,17},{... | collective-permute-start | bytes 884744 | tf_op jit(solution)/shard_map/ppermute | solution.py:119
  120.6 36.6 %collective-permute-start.11 = (f32[16,4352]{1,0:T(8,128)S(1)}, f32[16,4352]{1,0:T(8,128)S(1)}, u32[]{:S(2)}, u32[]{:S(2)}) collective-permute-start(f32[16,4352]{1,0:T(8,128)S(1)} %get-tuple-element.19.refs_4_), channel_id=1, source_target_pairs={{0,16},{4,20},{8,24},{12,28},{16,0},{20,4},{24,8},{28,12},{1,17},{... | collective-permute-start | bytes 835592 | tf_op jit(solution)/shard_map/ppermute | solution.py:119
  120.7 35.0 %collective-permute-start.5 = (f32[16,4096]{1,0:T(8,128)S(1)}, f32[16,4096]{1,0:T(8,128)S(1)}, u32[]{:S(2)}, u32[]{:S(2)}) collective-permute-start(f32[16,4096]{1,0:T(8,128)S(1)} %get-tuple-element.16.base_ref.refs_0_), channel_id=1, source_target_pairs={{0,16},{4,20},{8,24},{12,28},{16,0},{20,4},{24,8},{28,12},{1,17},{... | collective-permute-start | bytes 786440 | tf_op jit(solution)/shard_map/ppermute | solution.py:119
  123.5 34.2 %collective-permute-start.4 = (f32[16,4096]{1,0:T(8,128)S(1)}, f32[16,4096]{1,0:T(8,128)S(1)}, u32[]{:S(2)}, u32[]{:S(2)}) collective-permute-start(f32[16,4096]{1,0:T(8,128)S(1)} %get-tuple-element.16.base_ref.refs_0_), channel_id=1, source_target_pairs={{0,4},{4,0},{8,12},{12,8},{16,20},{20,16},{24,28},{28,24},{1,5},{5... | collective-permute-start | bytes 786440 | tf_op jit(solution)/shard_map/ppermute | solution.py:119
  125.1 49.6 %collective-permute-start.16 = (f32[16,4608]{1,0:T(8,128)S(1)}, f32[16,4608]{1,0:T(8,128)S(1)}, u32[]{:S(2)}, u32[]{:S(2)}) collective-permute-start(f32[16,4608]{1,0:T(8,128)S(1)} %add.21.refs_8_), channel_id=1, source_target_pairs={{0,4},{4,0},{8,12},{12,8},{16,20},{20,16},{24,28},{28,24},{1,5},{5... | collective-permute-start | bytes 884744 | tf_op jit(solution)/shard_map/ppermute | solution.py:119
  145.4 29.3 %collective-permute-start.18 = (f32[16,4608]{1,0:T(8,128)S(1)}, f32[16,4608]{1,0:T(8,128)S(1)}, u32[]{:S(2)}, u32[]{:S(2)}) collective-permute-start(f32[16,4608]{1,0:T(8,128)S(1)} %collective-permute-done.17.refs_10_), channel_id=1, source_target_pairs={{0,4},{4,0},{8,12},{12,8},{16,20},{20,16},{24,28},{28,24},{1,5},{5... | collective-permute-start | bytes 884744 | tf_op jit(solution)/shard_map/ppermute | solution.py:119
  155.7 19.0 %collective-permute-start.10 = (f32[16,4352]{1,0:T(8,128)S(1)}, f32[16,4352]{1,0:T(8,128)S(1)}, u32[]{:S(2)}, u32[]{:S(2)}) collective-permute-start(f32[16,4352]{1,0:T(8,128)S(1)} %get-tuple-element.19.refs_4_), channel_id=1, source_target_pairs={{0,4},{4,0},{8,12},{12,8},{16,20},{20,16},{24,28},{28,24},{1,5},{5... | collective-permute-start | bytes 835592 | tf_op jit(solution)/shard_map/ppermute | solution.py:119
  157.2 17.5 %collective-permute-start.12 = (f32[16,4352]{1,0:T(8,128)S(1)}, f32[16,4352]{1,0:T(8,128)S(1)}, u32[]{:S(2)}, u32[]{:S(2)}) collective-permute-start(f32[16,4352]{1,0:T(8,128)S(1)} %collective-permute-done.11.refs_6_), channel_id=1, source_target_pairs={{0,4},{4,0},{8,12},{12,8},{16,20},{20,16},{24,28},{28,24},{1,5},{5... | collective-permute-start | bytes 835592 | tf_op jit(solution)/shard_map/ppermute | solution.py:119
  157.7 17.0 %collective-permute-start.6 = (f32[16,4096]{1,0:T(8,128)S(1)}, f32[16,4096]{1,0:T(8,128)S(1)}, u32[]{:S(2)}, u32[]{:S(2)}) collective-permute-start(f32[16,4096]{1,0:T(8,128)S(1)} %collective-permute-done.5.refs_2_), channel_id=1, source_target_pairs={{0,4},{4,0},{8,12},{12,8},{16,20},{20,16},{24,28},{28,24},{1,5},{5... | collective-permute-start | bytes 786440 | tf_op jit(solution)/shard_map/ppermute | solution.py:119

commit v2 on v1

--- a/solution.py
+++ b/solution.py
@@ -8,10 +8,9 @@
 
 LEAVES = 64
 LANES = 128
-PIECES = 3
-TREE_BLOCK = 16
+TREE_BLOCK = 32
 ridge_weight = 1.0
-F32, BF16 = jnp.float32, jnp.bfloat16
+F32, BF16, F8 = jnp.float32, jnp.bfloat16, jnp.float8_e4m3fn
 VMEM_LIMIT = 32 * 1024 * 1024
 VMEM = pl.BlockSpec(memory_space=pltpu.VMEM)
 
@@ -25,24 +24,35 @@
         jnp.where(jnp.broadcast_to(leaves[t : t + 1, :], (LEAVES, rows)) == which, one, zero)
         for t in range(trees)
     ]
-    return jnp.concatenate(marks, 0)
-
-
-def pieces_of(value):
+    return jnp.concatenate(marks, 0).astype(F8)
+
+
+WIDE, NARROW = (16.0, 6), (4.0, 12)
+ROUND = 12582912.0
+
+
+def top_of(value):
+    return jnp.maximum(jnp.max(jnp.abs(value), axis=1, keepdims=True), 1e-30)
+
+
+def digits_of(value, top, code):
+    base, count = code
+    value = value * (0.5 * base / top)
     found = []
-    for _ in range(PIECES):
-        high = value.astype(BF16)
-        found.append(high)
-        value = value - high.astype(F32)
+    for _ in range(count):
+        digit = (value + ROUND) - ROUND
+        found.append(digit.astype(F8))
+        value = (value - digit) * base
     return jnp.concatenate(found, 0)
 
 
-def pieces_sum(value):
-    rows = value.shape[0] // PIECES
-    total = value[(PIECES - 1) * rows :]
-    for index in reversed(range(PIECES - 1)):
-        total = total + value[index * rows : (index + 1) * rows]
-    return total
+def digits_sum(value, top, code):
+    base, count = code
+    rows = value.shape[0] // count
+    total = value[(count - 1) * rows :]
+    for index in reversed(range(count - 1)):
+        total = value[index * rows : (index + 1) * rows] + total * (1.0 / base)
+    return total * (top * (2.0 / base))
 
 
 def lane_sums(value):
@@ -68,7 +78,7 @@
     return jax.ShapeDtypeStruct(shape, F32)
 
 
-def spread(leaf_refs, offsets, trees, split_ref, out_ref, scale, before=None):
+def spread(leaf_refs, offsets, trees, split_ref, top, out_ref, scale, before=None):
     rows = leaf_refs[0].shape[1]
 
     @pl.loop(0, trees // TREE_BLOCK)
@@ -85,11 +95,11 @@
             total = part if total is None else total + part
         width = TREE_BLOCK * LEAVES
         at = pl.ds(pl.multiple_of(step * width, width), width)
-        result = scale * pieces_sum(total)
+        result = digits_sum(total, scale * top, NARROW)
         out_ref[:, at] = result if before is None else before[:, at] + result
 
 
-def collect(leaf_refs, offsets, trees, split_ref, out_ref, total_ref):
+def collect(leaf_refs, offsets, trees, split_ref, top, out_ref, total_ref):
     rows = leaf_refs[0].shape[1]
     total_ref[...] = jnp.zeros_like(total_ref)
 
@@ -103,7 +113,7 @@
             part = jnp.dot(split, marks, preferred_element_type=F32)
             total_ref[:, at] = total_ref[:, at] + part
 
-    out_ref[:, : total_ref.shape[1]] = pieces_sum(total_ref[...])
+    out_ref[:, : total_ref.shape[1]] = digits_sum(total_ref[...], top, WIDE)
 
 
 def solution(mesh):
@@ -137,8 +147,8 @@
         row = lax.axis_index("row")
         key = (row // far_stride) * 2 + row % 2
         place = jnp.stack([key, key ^ 1, key ^ 2, key ^ 3]).astype(jnp.int32)
-        split_rows = pltpu.VMEM((PIECES * width, span), BF16)
-        split_columns = pltpu.VMEM((PIECES * width, columns), BF16)
+        split_rows = pltpu.VMEM((NARROW[1] * width, span), F8)
+        split_columns = pltpu.VMEM((WIDE[1] * width, columns), F8)
 
         def pack(place_ref, leaf_ref, target_ref, own_ref, near_ref, far_ref):
             leaves = leaf_ref[...].astype(F32)
@@ -166,14 +176,18 @@
         leaves, offsets = (own, near, far, both), (0, 0, width, 0)
 
         def first(own_ref, near_ref, out_ref, split_ref):
-            for index, ref in enumerate((own_ref, near_ref)):
-                split_ref[:, index * rows : (index + 1) * rows] = pieces_of(ref[trees:, :])
-            spread((own_ref, near_ref), offsets[:2], trees, split_ref, out_ref, scale)
+            chunks = own_ref[trees:, :], near_ref[trees:, :]
+            top = jnp.maximum(top_of(chunks[0]), top_of(chunks[1]))
+            for index, chunk in enumerate(chunks):
+                split_ref[:, index * rows : (index + 1) * rows] = digits_of(chunk, top, NARROW)
+            spread((own_ref, near_ref), offsets[:2], trees, split_ref, top, out_ref, scale)
 
         def second(far_ref, both_ref, before_ref, out_ref, split_ref):
-            split_ref[:, :rows] = pieces_of(far_ref[:width, :])
-            split_ref[:, rows : 2 * rows] = pieces_of(both_ref[trees:, :])
-            spread((far_ref, both_ref), offsets[2:], trees, split_ref, out_ref, scale, before_ref)
+            chunks = far_ref[:width, :], both_ref[trees:, :]
+            top = jnp.maximum(top_of(chunks[0]), top_of(chunks[1]))
+            for index, chunk in enumerate(chunks):
+                split_ref[:, index * rows : (index + 1) * rows] = digits_of(chunk, top, NARROW)
+            spread((far_ref, both_ref), offsets[2:], trees, split_ref, top, out_ref, scale, before_ref)
 
         b_shape = array(width, columns)
         part = call(first, b_shape, [split_rows], 2 * flops, own, near)
@@ -183,11 +197,12 @@
         def forward0(l0, l1, l2, l3, mine_ref, theirs_ref, out_ref, base_ref, split_ref, total_ref):
             base = mine_ref[...] + theirs_ref[...]
             base_ref[...] = base
-            split_ref[...] = pieces_of(base)
-            collect((l0, l1, l2, l3), offsets, trees, split_ref, out_ref, total_ref)
+            top = top_of(base)
+            split_ref[...] = digits_of(base, top, WIDE)
+            collect((l0, l1, l2, l3), offsets, trees, split_ref, top, out_ref, total_ref)
             out_ref[:, span:] = lane_sums(base * base)
 
-        total_rows = pltpu.VMEM((PIECES * width, span), F32)
+        total_rows = pltpu.VMEM((WIDE[1] * width, span), F32)
         part, b0 = call(
             forward0,
             (array(width, span + LANES), b_shape),
@@ -202,10 +217,11 @@
         def backward1(l0, l1, l2, l3, mine_ref, theirs_ref, out_ref, rows_ref, split_ref):
             value = mine_ref[:, :span] + theirs_ref[:, :span]
             rows_ref[...] = value
-            split_ref[...] = pieces_of(value)
+            top = top_of(value)
+            split_ref[...] = digits_of(value, top, NARROW)
             out_ref[:, columns : columns + LANES] = (scale * scale) * lane_sums(value * value)
             out_ref[:, columns + LANES :] = (mine_ref[:, span:] + theirs_ref[:, span:]) * (1.0 / n_share)
-            spread((l0, l1, l2, l3), offsets, trees, split_ref, out_ref, scale * scale)
+            spread((l0, l1, l2, l3), offsets, trees, split_ref, top, out_ref, scale * scale)
 
         part, w0 = call(
             backward1,
@@ -234,8 +250,9 @@
             res = base - theta * image
             res_ref[:, :columns] = res
             res_ref[:, columns:] = tail
-            split_ref[...] = pieces_of(res)
-            collect((l0, l1, l2, l3), offsets, trees, split_ref, out_ref, total_ref)
+            top = top_of(res)
+            split_ref[...] = digits_of(res, top, WIDE)
+            collect((l0, l1, l2, l3), offsets, trees, split_ref, top, out_ref, total_ref)
             out_ref[:, span : span + LANES] = lane_sums(res * res)
             out_ref[:, span + LANES :] = lane_sums(res * base)
 
@@ -253,7 +270,8 @@
 
         def backward2(l0, l1, l2, l3, mine_ref, theirs_ref, rows_ref, out_ref, split_ref):
             value = mine_ref[:, :span] + theirs_ref[:, :span]
-            split_ref[...] = pieces_of(value)
+            top = top_of(value)
+            split_ref[...] = digits_of(value, top, NARROW)
             out_ref[:, columns : columns + LANES] = (scale * scale) * lane_sums(value * value)
             out_ref[:, columns + LANES : columns + 2 * LANES] = (scale * scale) * lane_sums(
                 value * rows_ref[...]
@@ -261,7 +279,7 @@
             out_ref[:, columns + 2 * LANES :] = (mine_ref[:, span:] + theirs_ref[:, span:]) * (
                 1.0 / n_share
             )
-            spread((l0, l1, l2, l3), offsets, trees, split_ref, out_ref, scale * scale)
+            spread((l0, l1, l2, l3), offsets, trees, split_ref, top, out_ref, scale * scale)
 
         part = call(
             backward2,

time: 177 us -> 161 us (0.910)
  Pallas kernels: 47.5 us -> 28.7 us
  waiting for transfers between devices: 97.5 us -> 100 us
    pallas_call x6, Pallas kernels: 44.7 us -> 25.8 us  [call(): pl.pallas_call(kernel, out_shape=outs, in_specs=[VMEM] * len(args), out_s...]
    ppermute x19, waiting for transfers between devices: 97.5 us -> 100 us  [swap(): return lax.ppermute(value, axis, [(i, i ^ stride) for i in range(size)])]
  transfers between devices with their start and end apart: 19 -> 19, of which waited for: 12 -> 12; matrix products, arithmetic and copies ran while one was open for 0% -> 0% of each run, Pallas kernels for 3% -> 2%
where the time goes in v2:
time: 161 us
  waiting for transfers between devices  100 us (62%)
  starting transfers between devices  29.2 us (18%)
  Pallas kernels  28.7 us (18%)
  local copies, waits for them, and re-layouts  1.92 us (1%)
    ppermute x19, waiting for transfers between devices, swap(): return lax.ppermute(value, axis, [(i, i ^ stride) for i in range(size)])  100 us
    ppermute x19, starting transfers between devices, swap(): return lax.ppermute(value, axis, [(i, i ^ stride) for i in range(size)])  29.2 us
    pallas_call x6, Pallas kernels, call(): pl.pallas_call(kernel, out_shape=outs, in_specs=[VMEM] * len(args), out_s...  25.8 us
  transfers between devices with their start and end apart: 19, of which 12 were waited for; matrix products, arithmetic and copies ran while one was open for 0% of the time, Pallas kernels for 2%

profile of v2, /device:TPU:0, one launch (start us, length us, event | category | flops | bytes accessed | tf_op | source)
XLA Modules:
  0.0 160.7 jit_solution(1729191976520814235)
XLA Ops:
  3.2 4.1 %collective-permute-start.1 = (f32[96,1024]{1,0:T(8,128)S(1)}, f32[96,1024]{1,0:T(8,128)S(1)}, u32[]{:S(2)}, u32[]{:S(2)}) collective-permute-start(f32[96,1024]{1,0:T(8,128)S(1)} %get-tuple-element.15), channel_id=1, source_target_pairs={{0,16},{4,20},{8,24},{12,28},{16,0},{20,4},{24,8},{28,12},{1,17},{... | collective-permute-start | bytes 1179656 | tf_op jit(solution)/shard_map/ppermute | solution.py:129
  7.4 1.5 collective-permute-start
  8.9 16.0 %collective-permute-done.1.far_ref.l2 = f32[96,1024]{1,0:T(8,128)S(1)} collective-permute-done((f32[96,1024]{1,0:T(8,128)S(1)}, f32[96,1024]{1,0:T(8,128)S(1)}, u32[]{:S(2)}, u32[]{:S(2)}) %collective-permute-start.1) | collective-permute-done | bytes 393248 | tf_op jit(solution)/shard_map/ppermute | solution.py:129
  24.9 1.6 %collective-permute-start.2 = (f32[80,1024]{1,0:T(8,128)S(1)}, f32[80,1024]{1,0:T(8,128)S(1)}, u32[]{:S(2)}, u32[]{:S(2)}) collective-permute-start(f32[80,1024]{1,0:T(8,128)S(1)} %slice.4), channel_id=1, source_target_pairs={{0,4},{4,0},{8,12},{12,8},{16,20},{20,16},{24,28},{28,24},{1,5},{5... | collective-permute-start | bytes 983048 | tf_op jit(solution)/shard_map/ppermute | solution.py:129
  26.6 2.9 %shard_map.41.before_ref = f32[16,4096]{1,0:T(8,128)S(1)} custom-call(f32[80,1024]{1,0:T(8,128)S(1)} %get-tuple-element.13.own_ref.l0, f32[80,1024]{1,0:T(8,128)S(1)} %collective-permute-done.near_ref.l1), custom_call_target="tpu_custom_call" | custom-call | flops 4294967296 | bytes 1048576 | tf_op jit(solution)/shard_map/pallas_call | solution.py:66
  29.5 4.4 %collective-permute-done.2.both_ref.l3 = f32[80,1024]{1,0:T(8,128)S(1)} collective-permute-done((f32[80,1024]{1,0:T(8,128)S(1)}, f32[80,1024]{1,0:T(8,128)S(1)}, u32[]{:S(2)}, u32[]{:S(2)}) %collective-permute-start.2) | collective-permute-done | bytes 327712 | tf_op jit(solution)/shard_map/ppermute | solution.py:129
  33.9 2.9 %shard_map.42.mine_ref = f32[16,4096]{1,0:T(8,128)S(1)} custom-call(f32[96,1024]{1,0:T(8,128)S(1)} %collective-permute-done.1.far_ref.l2, f32[80,1024]{1,0:T(8,128)S(1)} %collective-permute-done.2.both_ref.l3, f32[16,4096]{1,0:T(8,128)S(1)} %shard_map.41.before_ref), custom_call_target="tpu_custom_call" | custom-call | flops 4294967296 | bytes 1048576 | tf_op jit(solution)/shard_map/pallas_call | solution.py:66
  36.8 1.5 collective-permute-start.3
  38.4 5.6 %collective-permute-done.3.theirs_ref = f32[16,4096]{1,0:T(8,128)S(1)} collective-permute-done((f32[16,4096]{1,0:T(8,128)S(1)}, f32[16,4096]{1,0:T(8,128)S(1)}, u32[]{:S(2)}, u32[]{:S(2)}) %collective-permute-start.3) | collective-permute-done | bytes 262176 | tf_op jit(solution)/shard_map/ppermute | solution.py:129
  44.0 4.1 %shard_map.43 = (f32[16,4224]{1,0:T(8,128)S(1)}, f32[16,4096]{1,0:T(8,128)S(1)}) custom-call(f32[80,1024]{1,0:T(8,128)S(1)} %get-tuple-element.13.own_ref.l0, f32[80,1024]{1,0:T(8,128)S(1)} %collective-permute-done.near_ref.l1, f32[96,1024]{1,0:T(8,128)S(1)} %collective-permute-done.1.far_ref.l2, f32[80,1024]{1,0:T(8,128)S(1)} %collective-permute-done.2.both_ref.l3, ...), custom_call_target="tpu_custom_call" | custom-call | flops 8589934592 | bytes 1048576 | tf_op jit(solution)/shard_map/pallas_call | solution.py:66
  48.2 1.5 collective-permute-done.7
  49.8 1.6 collective-permute-start.8
  51.3 7.0 %collective-permute-done.8.theirs_ref = f32[16,4224]{1,0:T(8,128)S(1)} collective-permute-done((f32[16,4224]{1,0:T(8,128)S(1)}, f32[16,4224]{1,0:T(8,128)S(1)}, u32[]{:S(2)}, u32[]{:S(2)}) %collective-permute-start.8) | collective-permute-done | bytes 270368 | tf_op jit(solution)/shard_map/ppermute | solution.py:129
  58.4 5.7 %shard_map.44 = (f32[16,4352]{1,0:T(8,128)S(1)}, f32[16,4096]{1,0:T(8,128)S(1)}) custom-call(f32[80,1024]{1,0:T(8,128)S(1)} %get-tuple-element.13.own_ref.l0, f32[80,1024]{1,0:T(8,128)S(1)} %collective-permute-done.near_ref.l1, f32[96,1024]{1,0:T(8,128)S(1)} %collective-permute-done.1.far_ref.l2, f32[80,1024]{1,0:T(8,128)S(1)} %collective-permute-done.2.both_ref.l3, ...), custom_call_target="tpu_custom_call" | custom-call | flops 8589934592 | bytes 1048576 | tf_op jit(solution)/shard_map/pallas_call | solution.py:66
  64.1 1.8 %collective-permute-start.9 = (f32[16,4352]{1,0:T(8,128)S(1)}, f32[16,4352]{1,0:T(8,128)S(1)}, u32[]{:S(2)}, u32[]{:S(2)}) collective-permute-start(f32[16,4352]{1,0:T(8,128)S(1)} %get-tuple-element.18.mine_ref), channel_id=1, source_target_pairs={{0,8},{4,12},{8,0},{12,4},{16,24},{20,28},{24,16},{28,20},{1,9},{5... | collective-permute-start | bytes 835592 | tf_op jit(solution)/shard_map/ppermute | solution.py:129
  65.9 6.1 %collective-permute-done.9.theirs_ref = f32[16,4352]{1,0:T(8,128)S(1)} collective-permute-done((f32[16,4352]{1,0:T(8,128)S(1)}, f32[16,4352]{1,0:T(8,128)S(1)}, u32[]{:S(2)}, u32[]{:S(2)}) %collective-permute-start.9) | collective-permute-done | bytes 278560 | tf_op jit(solution)/shard_map/ppermute | solution.py:129
  72.0 4.5 %shard_map.45 = (f32[16,4352]{1,0:T(8,128)S(1)}, f32[16,4352]{1,0:T(8,128)S(1)}) custom-call(f32[80,1024]{1,0:T(8,128)S(1)} %get-tuple-element.13.own_ref.l0, f32[80,1024]{1,0:T(8,128)S(1)} %collective-permute-done.near_ref.l1, f32[96,1024]{1,0:T(8,128)S(1)} %collective-permute-done.1.far_ref.l2, f32[80,1024]{1,0:T(8,128)S(1)} %collective-permute-done.2.both_ref.l3, ...), custom_call_target="tpu_custom_call" | custom-call | flops 8589934592 | bytes 1048576 | tf_op jit(solution)/shard_map/pallas_call | solution.py:66
  76.5 1.5 collective-permute-done.13
  78.1 1.6 collective-permute-start.14
  79.7 7.2 %collective-permute-done.14.theirs_ref = f32[16,4352]{1,0:T(8,128)S(1)} collective-permute-done((f32[16,4352]{1,0:T(8,128)S(1)}, f32[16,4352]{1,0:T(8,128)S(1)}, u32[]{:S(2)}, u32[]{:S(2)}) %collective-permute-start.14) | collective-permute-done | bytes 278560 | tf_op jit(solution)/shard_map/ppermute | solution.py:129
  86.9 5.7 %shard_map.46 = f32[16,4608]{1,0:T(8,128)S(1)} custom-call(f32[80,1024]{1,0:T(8,128)S(1)} %get-tuple-element.13.own_ref.l0, f32[80,1024]{1,0:T(8,128)S(1)} %collective-permute-done.near_ref.l1, f32[96,1024]{1,0:T(8,128)S(1)} %collective-permute-done.1.far_ref.l2, f32[80,1024]{1,0:T(8,128)S(1)} %collective-permute-done.2.both_ref.l3, ...), custom_call_target="tpu_custom_call" | custom-call | flops 8589934592 | bytes 1048576 | tf_op jit(solution)/shard_map/pallas_call | solution.py:66
  92.6 1.8 %collective-permute-start.15 = (f32[16,4608]{1,0:T(8,128)S(1)}, f32[16,4608]{1,0:T(8,128)S(1)}, u32[]{:S(2)}, u32[]{:S(2)}) collective-permute-start(f32[16,4608]{1,0:T(8,128)S(1)} %shard_map.46), channel_id=1, source_target_pairs={{0,8},{4,12},{8,0},{12,4},{16,24},{20,28},{24,16},{28,20},{1,9},{5... | collective-permute-start | bytes 884744 | tf_op jit(solution)/shard_map/ppermute | solution.py:129
  94.4 6.5 %collective-permute-done.15 = f32[16,4608]{1,0:T(8,128)S(1)} collective-permute-done((f32[16,4608]{1,0:T(8,128)S(1)}, f32[16,4608]{1,0:T(8,128)S(1)}, u32[]{:S(2)}, u32[]{:S(2)}) %collective-permute-start.15) | collective-permute-done | bytes 294944 | tf_op jit(solution)/shard_map/ppermute | solution.py:129
  100.9 3.4 %collective-permute-start.17 = (f32[16,4608]{1,0:T(8,128)S(1)}, f32[16,4608]{1,0:T(8,128)S(1)}, u32[]{:S(2)}, u32[]{:S(2)}) collective-permute-start(f32[16,4608]{1,0:T(8,128)S(1)} %add.21.refs_8_), channel_id=1, source_target_pairs={{0,16},{4,20},{8,24},{12,28},{16,0},{20,4},{24,8},{28,12},{1,17},{... | collective-permute-start | bytes 884744 | tf_op jit(solution)/shard_map/ppermute | solution.py:129
  104.4 2.8 %collective-permute-start.5 = (f32[16,4096]{1,0:T(8,128)S(1)}, f32[16,4096]{1,0:T(8,128)S(1)}, u32[]{:S(2)}, u32[]{:S(2)}) collective-permute-start(f32[16,4096]{1,0:T(8,128)S(1)} %get-tuple-element.16.base_ref.refs_0_), channel_id=1, source_target_pairs={{0,16},{4,20},{8,24},{12,28},{16,0},{20,4},{24,8},{28,12},{1,17},{... | collective-permute-start | bytes 786440 | tf_op jit(solution)/shard_map/ppermute | solution.py:129
  107.3 1.5 collective-permute-start.4
  109.3 19.8 %collective-permute-done.17.refs_10_ = f32[16,4608]{1,0:T(8,128)S(1)} collective-permute-done((f32[16,4608]{1,0:T(8,128)S(1)}, f32[16,4608]{1,0:T(8,128)S(1)}, u32[]{:S(2)}, u32[]{:S(2)}) %collective-permute-start.17) | collective-permute-done | bytes 294944 | tf_op jit(solution)/shard_map/ppermute | solution.py:129
  129.1 1.5 collective-permute-start.18
  130.6 8.8 %collective-permute-done.5.refs_2_ = f32[16,4096]{1,0:T(8,128)S(1)} collective-permute-done((f32[16,4096]{1,0:T(8,128)S(1)}, f32[16,4096]{1,0:T(8,128)S(1)}, u32[]{:S(2)}, u32[]{:S(2)}) %collective-permute-start.5) | collective-permute-done | bytes 262176 | tf_op jit(solution)/shard_map/ppermute | solution.py:129
  141.5 1.5 collective-permute-start.6
  143.0 15.4 %collective-permute-done.6.refs_3_ = f32[16,4096]{1,0:T(8,128)S(1)} collective-permute-done((f32[16,4096]{1,0:T(8,128)S(1)}, f32[16,4096]{1,0:T(8,128)S(1)}, u32[]{:S(2)}, u32[]{:S(2)}) %collective-permute-start.6) | collective-permute-done | bytes 262176 | tf_op jit(solution)/shard_map/ppermute | solution.py:129
  158.4 2.2 %combine.1 = (f32[64,4096]{1,0:T(8,128)}, f32[64,4096]{1,0:T(8,128)}) custom-call(s32[4]{0:T(128)S(1)} %pad_add_fusion.place_ref, f32[16,4096]{1,0:T(8,128)S(1)} %get-tuple-element.16.base_ref.refs_0_, f32[16,4096]{1,0:T(8,128)S(1)} %collective-permute-done.4.refs_1_, f32[16,4096]{1,0:T(8,128)S(1)} %collective-permute-done.5.refs_2_, ...), custom_call_target="tpu_custom_call" | custom-call | tf_op jit(solution)/shard_map/combine/pallas_call | solution.py:330
  (23 shorter events, 5.5 us)
Async XLA Ops:
  0.7 1.0 copy-start
  1.7 0.9 copy-start.1
  3.2 21.7 %collective-permute-start.1 = (f32[96,1024]{1,0:T(8,128)S(1)}, f32[96,1024]{1,0:T(8,128)S(1)}, u32[]{:S(2)}, u32[]{:S(2)}) collective-permute-start(f32[96,1024]{1,0:T(8,128)S(1)} %get-tuple-element.15), channel_id=1, source_target_pairs={{0,16},{4,20},{8,24},{12,28},{16,0},{20,4},{24,8},{28,12},{1,17},{... | collective-permute-start | bytes 1179656 | tf_op jit(solution)/shard_map/ppermute | solution.py:129
  7.4 19.2 %collective-permute-start = (f32[80,1024]{1,0:T(8,128)S(1)}, f32[80,1024]{1,0:T(8,128)S(1)}, u32[]{:S(2)}, u32[]{:S(2)}) collective-permute-start(f32[80,1024]{1,0:T(8,128)S(1)} %get-tuple-element.14), channel_id=1, source_target_pairs={{0,4},{4,0},{8,12},{12,8},{16,20},{20,16},{24,28},{28,24},{1,5},{5... | collective-permute-start | bytes 983048 | tf_op jit(solution)/shard_map/ppermute | solution.py:129
  24.9 8.9 %collective-permute-start.2 = (f32[80,1024]{1,0:T(8,128)S(1)}, f32[80,1024]{1,0:T(8,128)S(1)}, u32[]{:S(2)}, u32[]{:S(2)}) collective-permute-start(f32[80,1024]{1,0:T(8,128)S(1)} %slice.4), channel_id=1, source_target_pairs={{0,4},{4,0},{8,12},{12,8},{16,20},{20,16},{24,28},{28,24},{1,5},{5... | collective-permute-start | bytes 983048 | tf_op jit(solution)/shard_map/ppermute | solution.py:129
  36.8 7.2 %collective-permute-start.3 = (f32[16,4096]{1,0:T(8,128)S(1)}, f32[16,4096]{1,0:T(8,128)S(1)}, u32[]{:S(2)}, u32[]{:S(2)}) collective-permute-start(f32[16,4096]{1,0:T(8,128)S(1)} %shard_map.42.mine_ref), channel_id=1, source_target_pairs={{0,8},{4,12},{8,0},{12,4},{16,24},{20,28},{24,16},{28,20},{1,9},{5... | collective-permute-start | bytes 786440 | tf_op jit(solution)/shard_map/ppermute | solution.py:129
  48.1 1.6 %collective-permute-start.7 = (f32[16,4224]{1,0:T(8,128)S(1)}, f32[16,4224]{1,0:T(8,128)S(1)}, u32[]{:S(2)}, u32[]{:S(2)}) collective-permute-start(f32[16,4224]{1,0:T(8,128)S(1)} %get-tuple-element.17), channel_id=1, source_target_pairs={{0,1},{1,0},{2,3},{3,2},{4,5},{5,4},{6,7},{7,6},{8,9},{9,8},{10,11... | collective-permute-start | bytes 811016 | tf_op jit(solution)/shard_map/ppermute | solution.py:129
  49.8 8.6 %collective-permute-start.8 = (f32[16,4224]{1,0:T(8,128)S(1)}, f32[16,4224]{1,0:T(8,128)S(1)}, u32[]{:S(2)}, u32[]{:S(2)}) collective-permute-start(f32[16,4224]{1,0:T(8,128)S(1)} %add.19.mine_ref), channel_id=1, source_target_pairs={{0,2},{1,3},{2,0},{3,1},{4,6},{5,7},{6,4},{7,5},{8,10},{9,11},{10,... | collective-permute-start | bytes 811016 | tf_op jit(solution)/shard_map/ppermute | solution.py:129
  64.1 7.9 %collective-permute-start.9 = (f32[16,4352]{1,0:T(8,128)S(1)}, f32[16,4352]{1,0:T(8,128)S(1)}, u32[]{:S(2)}, u32[]{:S(2)}) collective-permute-start(f32[16,4352]{1,0:T(8,128)S(1)} %get-tuple-element.18.mine_ref), channel_id=1, source_target_pairs={{0,8},{4,12},{8,0},{12,4},{16,24},{20,28},{24,16},{28,20},{1,9},{5... | collective-permute-start | bytes 835592 | tf_op jit(solution)/shard_map/ppermute | solution.py:129
  76.5 1.6 %collective-permute-start.13 = (f32[16,4352]{1,0:T(8,128)S(1)}, f32[16,4352]{1,0:T(8,128)S(1)}, u32[]{:S(2)}, u32[]{:S(2)}) collective-permute-start(f32[16,4352]{1,0:T(8,128)S(1)} %get-tuple-element.20), channel_id=1, source_target_pairs={{0,1},{1,0},{2,3},{3,2},{4,5},{5,4},{6,7},{7,6},{8,9},{9,8},{10,11... | collective-permute-start | bytes 835592 | tf_op jit(solution)/shard_map/ppermute | solution.py:129
  78.1 8.8 %collective-permute-start.14 = (f32[16,4352]{1,0:T(8,128)S(1)}, f32[16,4352]{1,0:T(8,128)S(1)}, u32[]{:S(2)}, u32[]{:S(2)}) collective-permute-start(f32[16,4352]{1,0:T(8,128)S(1)} %add.20.mine_ref), channel_id=1, source_target_pairs={{0,2},{1,3},{2,0},{3,1},{4,6},{5,7},{6,4},{7,5},{8,10},{9,11},{10,... | collective-permute-start | bytes 835592 | tf_op jit(solution)/shard_map/ppermute | solution.py:129
  92.6 8.3 %collective-permute-start.15 = (f32[16,4608]{1,0:T(8,128)S(1)}, f32[16,4608]{1,0:T(8,128)S(1)}, u32[]{:S(2)}, u32[]{:S(2)}) collective-permute-start(f32[16,4608]{1,0:T(8,128)S(1)} %shard_map.46), channel_id=1, source_target_pairs={{0,8},{4,12},{8,0},{12,4},{16,24},{20,28},{24,16},{28,20},{1,9},{5... | collective-permute-start | bytes 884744 | tf_op jit(solution)/shard_map/ppermute | solution.py:129
  100.9 28.2 %collective-permute-start.17 = (f32[16,4608]{1,0:T(8,128)S(1)}, f32[16,4608]{1,0:T(8,128)S(1)}, u32[]{:S(2)}, u32[]{:S(2)}) collective-permute-start(f32[16,4608]{1,0:T(8,128)S(1)} %add.21.refs_8_), channel_id=1, source_target_pairs={{0,16},{4,20},{8,24},{12,28},{16,0},{20,4},{24,8},{28,12},{1,17},{... | collective-permute-start | bytes 884744 | tf_op jit(solution)/shard_map/ppermute | solution.py:129
  104.3 36.6 %collective-permute-start.11 = (f32[16,4352]{1,0:T(8,128)S(1)}, f32[16,4352]{1,0:T(8,128)S(1)}, u32[]{:S(2)}, u32[]{:S(2)}) collective-permute-start(f32[16,4352]{1,0:T(8,128)S(1)} %get-tuple-element.19.refs_4_), channel_id=1, source_target_pairs={{0,16},{4,20},{8,24},{12,28},{16,0},{20,4},{24,8},{28,12},{1,17},{... | collective-permute-start | bytes 835592 | tf_op jit(solution)/shard_map/ppermute | solution.py:129
  104.4 35.0 %collective-permute-start.5 = (f32[16,4096]{1,0:T(8,128)S(1)}, f32[16,4096]{1,0:T(8,128)S(1)}, u32[]{:S(2)}, u32[]{:S(2)}) collective-permute-start(f32[16,4096]{1,0:T(8,128)S(1)} %get-tuple-element.16.base_ref.refs_0_), channel_id=1, source_target_pairs={{0,16},{4,20},{8,24},{12,28},{16,0},{20,4},{24,8},{28,12},{1,17},{... | collective-permute-start | bytes 786440 | tf_op jit(solution)/shard_map/ppermute | solution.py:129
  107.3 34.2 %collective-permute-start.4 = (f32[16,4096]{1,0:T(8,128)S(1)}, f32[16,4096]{1,0:T(8,128)S(1)}, u32[]{:S(2)}, u32[]{:S(2)}) collective-permute-start(f32[16,4096]{1,0:T(8,128)S(1)} %get-tuple-element.16.base_ref.refs_0_), channel_id=1, source_target_pairs={{0,4},{4,0},{8,12},{12,8},{16,20},{20,16},{24,28},{28,24},{1,5},{5... | collective-permute-start | bytes 786440 | tf_op jit(solution)/shard_map/ppermute | solution.py:129
  108.8 49.6 %collective-permute-start.16 = (f32[16,4608]{1,0:T(8,128)S(1)}, f32[16,4608]{1,0:T(8,128)S(1)}, u32[]{:S(2)}, u32[]{:S(2)}) collective-permute-start(f32[16,4608]{1,0:T(8,128)S(1)} %add.21.refs_8_), channel_id=1, source_target_pairs={{0,4},{4,0},{8,12},{12,8},{16,20},{20,16},{24,28},{28,24},{1,5},{5... | collective-permute-start | bytes 884744 | tf_op jit(solution)/shard_map/ppermute | solution.py:129
  129.1 29.3 %collective-permute-start.18 = (f32[16,4608]{1,0:T(8,128)S(1)}, f32[16,4608]{1,0:T(8,128)S(1)}, u32[]{:S(2)}, u32[]{:S(2)}) collective-permute-start(f32[16,4608]{1,0:T(8,128)S(1)} %collective-permute-done.17.refs_10_), channel_id=1, source_target_pairs={{0,4},{4,0},{8,12},{12,8},{16,20},{20,16},{24,28},{28,24},{1,5},{5... | collective-permute-start | bytes 884744 | tf_op jit(solution)/shard_map/ppermute | solution.py:129
  139.4 19.0 %collective-permute-start.10 = (f32[16,4352]{1,0:T(8,128)S(1)}, f32[16,4352]{1,0:T(8,128)S(1)}, u32[]{:S(2)}, u32[]{:S(2)}) collective-permute-start(f32[16,4352]{1,0:T(8,128)S(1)} %get-tuple-element.19.refs_4_), channel_id=1, source_target_pairs={{0,4},{4,0},{8,12},{12,8},{16,20},{20,16},{24,28},{28,24},{1,5},{5... | collective-permute-start | bytes 835592 | tf_op jit(solution)/shard_map/ppermute | solution.py:129
  141.0 17.5 %collective-permute-start.12 = (f32[16,4352]{1,0:T(8,128)S(1)}, f32[16,4352]{1,0:T(8,128)S(1)}, u32[]{:S(2)}, u32[]{:S(2)}) collective-permute-start(f32[16,4352]{1,0:T(8,128)S(1)} %collective-permute-done.11.refs_6_), channel_id=1, source_target_pairs={{0,4},{4,0},{8,12},{12,8},{16,20},{20,16},{24,28},{28,24},{1,5},{5... | collective-permute-start | bytes 835592 | tf_op jit(solution)/shard_map/ppermute | solution.py:129
  141.5 17.0 %collective-permute-start.6 = (f32[16,4096]{1,0:T(8,128)S(1)}, f32[16,4096]{1,0:T(8,128)S(1)}, u32[]{:S(2)}, u32[]{:S(2)}) collective-permute-start(f32[16,4096]{1,0:T(8,128)S(1)} %collective-permute-done.5.refs_2_), channel_id=1, source_target_pairs={{0,4},{4,0},{8,12},{12,8},{16,20},{20,16},{24,28},{28,24},{1,5},{5... | collective-permute-start | bytes 786440 | tf_op jit(solution)/shard_map/ppermute | solution.py:129

commit v3 on v2

v3 whole, which is shorter than its diff:
```python
import jax
import jax.numpy as jnp
from jax import lax
from jax.experimental import pallas as pl
from jax.experimental.pallas import tpu as pltpu
from jax.sharding import PartitionSpec as P


LEAVES = 64
LANES = 128
ridge_weight = 1.0
F32, BF16, F8 = jnp.float32, jnp.bfloat16, jnp.float8_e4m3fn
VMEM_LIMIT = 32 * 1024 * 1024
VMEM = pl.BlockSpec(memory_space=pltpu.VMEM)


def onehot(leaves):
    trees, rows = leaves.shape
    which = lax.broadcasted_iota(jnp.int32, (LEAVES, rows), 0).astype(F32).astype(BF16)
    leaves = leaves.astype(F32).astype(BF16)
    one, zero = jnp.ones((LEAVES, rows), BF16), jnp.zeros((LEAVES, rows), BF16)
    marks = [
        jnp.where(jnp.broadcast_to(leaves[t : t + 1, :], (LEAVES, rows)) == which, one, zero)
        for t in range(trees)
    ]
    return jnp.concatenate(marks, 0).astype(F8)


WIDE, NARROW = (16.0, 6), (4.0, 12)
ROUND = 12582912.0


def top_of(value):
    return jnp.maximum(jnp.max(jnp.abs(value), axis=1, keepdims=True), 1e-30)


def digits_of(value, top, code):
    base, count = code
    value = value * (0.5 * base / top)
    found = []
    for _ in range(count):
        digit = (value + ROUND) - ROUND
        found.append(digit.astype(F8))
        value = (value - digit) * base
    return jnp.concatenate(found, 0)


def digits_sum(value, top, code):
    base, count = code
    rows = value.shape[0] // count
    total = value[(count - 1) * rows :]
    for index in reversed(range(count - 1)):
        total = value[index * rows : (index + 1) * rows] + total * (1.0 / base)
    return total * (top * (2.0 / base))


def lane_sums(value):
    groups = [value[:, at : at + LANES] for at in range(0, value.shape[1], LANES)]
    while len(groups) > 1:
        groups = [sum(groups[at : at + 2]) for at in range(0, len(groups), 2)]
    return groups[0]


def call(kernel, outs, scratch, flops, *args):
    return pl.pallas_call(
        kernel,
        out_shape=outs,
        in_specs=[VMEM] * len(args),
        out_specs=jax.tree.map(lambda _: VMEM, outs),
        scratch_shapes=scratch,
        compiler_params=pltpu.CompilerParams(vmem_limit_bytes=VMEM_LIMIT),
        cost_estimate=pl.CostEstimate(flops=flops, bytes_accessed=1 << 20, transcendentals=0),
    )(*args)


def array(*shape):
    return jax.ShapeDtypeStruct(shape, F32)


def spread(blocks, split_ref, top, scale):
    total, at = None, 0
    for ref, start, trees in blocks:
        rows = ref.shape[1]
        part = lax.dot_general(
            split_ref[:, at : at + rows],
            onehot(ref[start : start + trees, :]),
            (((1,), (1,)), ((), ())),
            preferred_element_type=F32,
        )
        total = part if total is None else total + part
        at += rows
    return digits_sum(total, scale * top, NARROW)


def collect(blocks, vector, out_ref, before_ref):
    top = top_of(vector)
    split = digits_of(vector, top, WIDE)
    at = 0
    for ref, start, trees in blocks:
        rows = ref.shape[1]
        part = jnp.dot(split, onehot(ref[start : start + trees, :]), preferred_element_type=F32)
        part = digits_sum(part, top, WIDE)
        if before_ref is not None:
            part = part + before_ref[:, at : at + rows]
        out_ref[:, at : at + rows] = part
        at += rows


def solution(mesh):
    n_row, n_leaf = mesh.shape["row"], mesh.shape["leaf"]
    far_stride, near_stride = n_row // 2, 1
    row_strides = [1 << bit for bit in range(1, n_row.bit_length() - 2)]
    leaf_strides = [1 << bit for bit in range(n_leaf.bit_length() - 1)]
    n_keys = 4
    n_share = n_row // n_keys

    def swap(value, axis, stride):
        size = n_row if axis == "row" else n_leaf
        return lax.ppermute(value, axis, [(i, i ^ stride) for i in range(size)])

    def far_swap(value):
        return swap(value, "row", far_stride)

    def near_swap(value):
        return swap(value, "row", near_stride)

    def gather(value):
        far = far_swap(value)
        near = near_swap(value)
        return [value, near, far, near_swap(far)]

    def half_sum(value, axis, strides):
        for stride in strides[:-1]:
            value = value + swap(value, axis, stride)
        return value, swap(value, axis, strides[-1])

    def per_device(leaf_index, targets):
        width = targets.shape[1] // n_keys
        rows, trees = leaf_index.shape
        half = trees // 2
        columns, span = half * LEAVES, n_keys * rows
        scale = (LEAVES / (rows * n_row)) ** 0.5
        flops = 2 * columns * rows * 256
        row = lax.axis_index("row")
        key = (row // far_stride) * 2 + row % 2
        place = jnp.stack([key, key ^ 1, key ^ 2, key ^ 3]).astype(jnp.int32)

        def pack(place_ref, target_ref, own_ref, near_ref, far_ref):
            chunk = lambda m: target_ref[pl.ds(pl.multiple_of(place_ref[m] * width, width), width), :]
            own_ref[...] = chunk(0)
            near_ref[...] = chunk(1)
            far_ref[:width, :] = chunk(2)
            far_ref[width:, :] = chunk(3)

        own = leaf_index.T
        t_own, t_near, t_far = pl.pallas_call(
            pack,
            out_shape=(array(width, rows), array(width, rows), array(2 * width, rows)),
            in_specs=[pl.BlockSpec(memory_space=pltpu.SMEM), VMEM],
            out_specs=(VMEM, VMEM, VMEM),
            compiler_params=pltpu.CompilerParams(vmem_limit_bytes=VMEM_LIMIT),
            name="pack",
        )(place, targets.T)
        far = [far_swap(own[:half]), far_swap(own[half:])]
        t_far = far_swap(t_far)
        near = near_swap(own)
        t_near = near_swap(t_near)
        both = [near_swap(far[0]), near_swap(far[1])]
        t_both = near_swap(t_far[width:])

        def leaves_of(h):
            return own, near, far[h], both[h]

        def blocks_of(refs, h):
            return tuple((ref, start, half) for ref, start in zip(refs, (h * half, h * half, 0, 0)))

        split_two = pltpu.VMEM((NARROW[1] * width, 2 * rows), F8)
        split_one = pltpu.VMEM((NARROW[1] * width, rows), F8)

        def back0_own(own_ref, near_ref, first_ref, second_ref, out0_ref, out1_ref, split_ref):
            chunks = first_ref[...], second_ref[...]
            top = jnp.maximum(top_of(chunks[0]), top_of(chunks[1]))
            for index, chunk in enumerate(chunks):
                split_ref[:, index * rows : (index + 1) * rows] = digits_of(chunk, top, NARROW)
            for h, ref in enumerate((out0_ref, out1_ref)):
                ref[...] = spread(blocks_of((own_ref, near_ref), h), split_ref, top, scale)

        def back0_far(far0_ref, far1_ref, value_ref, in0_ref, in1_ref, out0_ref, out1_ref, split_ref):
            value = value_ref[:width, :]
            top = top_of(value)
            split_ref[...] = digits_of(value, top, NARROW)
            out0_ref[...] = in0_ref[...] + spread(((far0_ref, 0, half),), split_ref, top, scale)
            out1_ref[...] = in1_ref[...] + spread(((far1_ref, 0, half),), split_ref, top, scale)

        def back0_both(leaf_ref, value_ref, in_ref, out_ref, split_ref):
            value = value_ref[...]
            top = top_of(value)
            split_ref[...] = digits_of(value, top, NARROW)
            out_ref[...] = in_ref[...] + spread(((leaf_ref, 0, half),), split_ref, top, scale)

        b_half = array(width, columns)
        parts = call(back0_own, (b_half, b_half), [split_two], 4 * flops, own, near, t_own, t_near)
        parts = call(back0_far, (b_half, b_half), [split_one], 2 * flops, *far, t_far, *parts)
        pairs = []
        for h in range(2):
            part = call(back0_both, b_half, [split_one], flops, both[h], t_both, parts[h])
            pairs.append(half_sum(part, "row", row_strides))

        w_shape = array(width, span + LANES)

        def forward0_first(l0, l1, l2, l3, mine_ref, theirs_ref, out_ref, base_ref):
            base = mine_ref[...] + theirs_ref[...]
            base_ref[...] = base
            collect(blocks_of((l0, l1, l2, l3), 0), base, out_ref, None)
            out_ref[:, span:] = lane_sums(base * base)

        def forward0_second(l0, l1, l2, l3, mine_ref, theirs_ref, in_ref, first_ref, out_ref, base_ref):
            base = mine_ref[...] + theirs_ref[...]
            base_ref[:, :columns] = first_ref[...]
            base_ref[:, columns:] = base
            collect(blocks_of((l0, l1, l2, l3), 1), base, out_ref, in_ref)
            out_ref[:, span:] = in_ref[:, span:] + lane_sums(base * base)

        part, first = call(forward0_first, (w_shape, b_half), [], 4 * flops, *leaves_of(0), *pairs[0])
        part, b0 = call(
            forward0_second, (w_shape, array(width, 2 * columns)), [], 4 * flops, *leaves_of(1), *pairs[1], part, first
        )
        w_pair = half_sum(part, "leaf", leaf_strides)

        split_shape = jax.ShapeDtypeStruct((NARROW[1] * width, span), F8)
        top_shape = array(width, 1)

        def backward_first(l0, l1, l2, l3, mine_ref, theirs_ref, *refs):
            rows_ref, (out_ref, split_ref, top_ref, last_ref) = refs[:-4], refs[-4:]
            value = mine_ref[:, :span] + theirs_ref[:, :span]
            if not rows_ref:
                last_ref[...] = value
            top = top_of(value)
            top_ref[...] = top
            split_ref[...] = digits_of(value, top, NARROW)
            tail = [value * value] + [value * ref[...] for ref in rows_ref]
            at = columns
            for product in tail:
                out_ref[:, at : at + LANES] = (scale * scale) * lane_sums(product)
                at += LANES
            out_ref[:, at:] = (mine_ref[:, span:] + theirs_ref[:, span:]) * (1.0 / n_share)
            out_ref[:, :columns] = spread(
                blocks_of((l0, l1, l2, l3), 0), split_ref, top, scale * scale
            )
            if rows_ref:
                last_ref[...] = jnp.zeros_like(last_ref)

        def backward_second(l0, l1, l2, l3, split_ref, top_ref, out_ref):
            out_ref[...] = spread(blocks_of((l0, l1, l2, l3), 1), split_ref, top_ref[...], scale * scale)

        def backward(w_pair, extra, *rows_before):
            part, split, top, last = call(
                backward_first,
                (
                    array(width, columns + extra * LANES),
                    split_shape,
                    top_shape,
                    array(8, LANES) if rows_before else array(width, span),
                ),
                [],
                4 * flops,
                *leaves_of(0),
                *w_pair,
                *rows_before,
            )
            pairs = [half_sum(part, "row", row_strides)]
            part = call(backward_second, b_half, [], 4 * flops, *leaves_of(1), split, top)
            return pairs + [half_sum(part, "row", row_strides)], last

        pairs, w0 = backward(w_pair, 2)

        def step_of(norm, curve):
            return jnp.where(norm > 0.0, norm / (curve + ridge_weight * norm), 1.0)

        def scalar(value):
            return jnp.sum(value, axis=(0, 1), keepdims=True)

        def theta_of(tail):
            return step_of(scalar(tail[:, LANES:]), scalar(tail[:, :LANES]))

        def residual(base, mine_ref, theirs_ref, theta):
            image = mine_ref[:, :columns] + theirs_ref[:, :columns]
            return base - theta * (image + ridge_weight * base)

        def forward1_first(l0, l1, l2, l3, mine_ref, theirs_ref, base_ref, out_ref, res_ref):
            tail = mine_ref[:, columns:] + theirs_ref[:, columns:]
            base = base_ref[:, :columns]
            res = residual(base, mine_ref, theirs_ref, theta_of(tail))
            res_ref[:, :columns] = res
            res_ref[:, columns:] = tail
            collect(blocks_of((l0, l1, l2, l3), 0), res, out_ref, None)
            out_ref[:, span : span + LANES] = lane_sums(res * res)
            out_ref[:, span + LANES :] = lane_sums(res * base)

        def forward1_second(
            l0, l1, l2, l3, mine_ref, theirs_ref, base_ref, in_ref, first_ref, out_ref, res_ref
        ):
            tail = first_ref[:, columns:]
            base = base_ref[:, columns:]
            res = residual(base, mine_ref, theirs_ref, theta_of(tail))
            res_ref[:, :columns] = first_ref[:, :columns]
            res_ref[:, columns : 2 * columns] = res
            res_ref[:, 2 * columns :] = tail
            collect(blocks_of((l0, l1, l2, l3), 1), res, out_ref, in_ref)
            out_ref[:, span : span + LANES] = in_ref[:, span : span + LANES] + lane_sums(res * res)
            out_ref[:, span + LANES :] = in_ref[:, span + LANES :] + lane_sums(res * base)

        w_shape = array(width, span + 2 * LANES)
        part, first = call(
            forward1_first, (w_shape, array(width, columns + 2 * LANES)), [], 4 * flops, *leaves_of(0), *pairs[0], b0
        )
        part, res = call(
            forward1_second,
            (w_shape, array(width, 2 * columns + 2 * LANES)),
            [],
            4 * flops,
            *leaves_of(1),
            *pairs[1],
            b0,
            part,
            first,
        )
        w_pair = half_sum(part, "leaf", leaf_strides)

        pairs, _ = backward(w_pair, 4, w0)
        b2 = [mine + theirs for mine, theirs in pairs]

        def combine(place_ref, *refs):
            bases, ress, firsts, seconds = (refs[k * n_keys : (k + 1) * n_keys] for k in range(4))
            solution_ref, residual_ref = refs[4 * n_keys :]

            def tail(ref, start, at):
                return scalar(ref[:, start + at * LANES : start + (at + 1) * LANES])

            keys = range(n_keys)
            b = [tail(ress[m], 2 * columns, 0) for m in keys]
            a = [tail(ress[m], 2 * columns, 1) for m in keys]
            e, f, c, d = ([tail(firsts[m], columns, at) for m in keys] for at in range(4))
            norm0 = sum(a)
            alpha0 = norm0 / (sum(b) + ridge_weight * norm0)
            theta = [step_of(a[m], b[m]) for m in keys]
            rho = [alpha0 / theta[m] for m in keys]
            square = lambda x, y, xx, xy, yy: x * x * xx + 2.0 * x * y * xy + y * y * yy
            norm1 = sum(square(rho[m], 1.0 - rho[m], c[m], d[m], a[m]) for m in keys)
            beta = norm1 / norm0
            other = [1.0 - rho[m] + beta for m in keys]
            curve = sum(
                square(rho[m], other[m], e[m], f[m], b[m])
                + ridge_weight * square(rho[m], other[m], c[m], d[m], a[m])
                for m in keys
            )
            alpha1 = norm1 / curve
            for m in keys:
                at = pl.ds(pl.multiple_of(place_ref[m] * width, width), width)
                for h, images in enumerate((firsts, seconds)):
                    of_half = slice(h * columns, (h + 1) * columns)
                    base, res, image = bases[m][:, of_half], ress[m][:, of_half], images[m][:, :columns]
                    solution_ref[at, of_half] = (alpha0 + alpha1 * other[m]) * base + (
                        alpha1 * rho[m]
                    ) * res
                    residual_ref[at, of_half] = (
                        ((1.0 - rho[m]) - alpha1 * other[m] / theta[m]) * base
                        + (rho[m] + alpha1 * (other[m] / theta[m] - ridge_weight * rho[m])) * res
                        - (alpha1 * rho[m]) * image
                    )

        out = array(n_keys * width, 2 * columns)
        result = pl.pallas_call(
            combine,
            out_shape=(out, out),
            in_specs=[pl.BlockSpec(memory_space=pltpu.SMEM)] + [VMEM] * (4 * n_keys),
            out_specs=(VMEM, VMEM),
            compiler_params=pltpu.CompilerParams(vmem_limit_bytes=VMEM_LIMIT),
            name="combine",
        )(place, *gather(b0), *gather(res), *gather(b2[0]), *gather(b2[1]))
        return tuple(value.T for value in result)

    return jax.shard_map(
        per_device,
        mesh=mesh,
        in_specs=(P("row", "leaf"), P("row", None)),
        out_specs=(P("leaf", None), P("leaf", None)),
        check_vma=False,
    )
```

time: 161 us -> 128 us (0.80)
  waiting for transfers between devices: 100 us -> 58 us
  starting transfers between devices: 29.2 us -> 39.1 us
    ppermute x19 -> x30, waiting for transfers between devices: 100 us -> 58 us  [swap(): return lax.ppermute(value, axis, [(i, i ^ stride) for i in range(size)])]
    ppermute x19 -> x30, starting transfers between devices: 29.2 us -> 39.1 us  [swap(): return lax.ppermute(value, axis, [(i, i ^ stride) for i in range(size)])]
    pallas_call x6 -> x12, Pallas kernels: 25.8 us -> 25.7 us  [call(): pl.pallas_call(kernel, out_shape=outs, in_specs=[VMEM] * len(args), out_s...]
  transfers between devices with their start and end apart: 19 -> 30, of which waited for: 12 -> 15; matrix products, arithmetic and copies ran while one was open for 0% -> 0% of each run, Pallas kernels for 2% -> 14%
where the time goes in v3:
time: 128 us
  waiting for transfers between devices  58 us (45%)
  starting transfers between devices  39.1 us (31%)
  Pallas kernels  28.4 us (22%)
    ppermute x30, waiting for transfers between devices, swap(): return lax.ppermute(value, axis, [(i, i ^ stride) for i in range(size)])  58 us
    ppermute x30, starting transfers between devices, swap(): return lax.ppermute(value, axis, [(i, i ^ stride) for i in range(size)])  39.1 us
    pallas_call x12, Pallas kernels, call(): pl.pallas_call(kernel, out_shape=outs, in_specs=[VMEM] * len(args), out_s...  25.7 us
  transfers between devices with their start and end apart: 30, of which 15 were waited for; matrix products, arithmetic and copies ran while one was open for 0% of the time, Pallas kernels for 14%

profile of v3, /device:TPU:0, one launch (start us, length us, event | category | flops | bytes accessed | tf_op | source)
XLA Modules:
  0.0 127.5 jit_solution(10288838472712411642)
XLA Ops:
  2.3 4.1 %collective-permute-start.3 = (f32[32,1024]{1,0:T(8,128)S(1)}, f32[32,1024]{1,0:T(8,128)S(1)}, u32[]{:S(2)}, u32[]{:S(2)}) collective-permute-start(f32[32,1024]{1,0:T(8,128)S(1)} %get-tuple-element.26), channel_id=1, source_target_pairs={{0,16},{4,20},{8,24},{12,28},{16,0},{20,4},{24,8},{28,12},{1,17},{... | collective-permute-start | bytes 393224 | tf_op jit(solution)/shard_map/ppermute | solution.py:119
  6.4 1.5 %collective-permute-start = (s32[64,1024]{1,0:T(8,128)S(1)}, s32[64,1024]{1,0:T(8,128)S(1)}, u32[]{:S(2)}, u32[]{:S(2)}) collective-permute-start(s32[64,1024]{1,0:T(8,128)S(1)} %bitcast.9), channel_id=1, source_target_pairs={{0,4},{4,0},{8,12},{12,8},{16,20},{20,16},{24,28},{28,24},{1,5},{5... | collective-permute-start | bytes 786440 | tf_op jit(solution)/shard_map/ppermute | solution.py:119
  8.3 2.6 %collective-permute-start.1 = (s32[32,1024]{1,0:T(8,128)S(1)}, s32[32,1024]{1,0:T(8,128)S(1)}, u32[]{:S(2)}, u32[]{:S(2)}) collective-permute-start(s32[32,1024]{1,0:T(8,128)S(1)} %get-tuple-element.51), channel_id=1, source_target_pairs={{0,16},{4,20},{8,24},{12,28},{16,0},{20,4},{24,8},{28,12},{1,17},{... | collective-permute-start | bytes 393224 | tf_op jit(solution)/shard_map/ppermute | solution.py:119
  11.4 7.7 %collective-permute-done.3.value_ref = f32[32,1024]{1,0:T(8,128)S(1)} collective-permute-done((f32[32,1024]{1,0:T(8,128)S(1)}, f32[32,1024]{1,0:T(8,128)S(1)}, u32[]{:S(2)}, u32[]{:S(2)}) %collective-permute-start.3) | collective-permute-done | bytes 131104 | tf_op jit(solution)/shard_map/ppermute | solution.py:119
  19.2 1.8 %collective-permute-start.4 = (f32[16,1024]{1,0:T(8,128)S(1)}, f32[16,1024]{1,0:T(8,128)S(1)}, u32[]{:S(2)}, u32[]{:S(2)}) collective-permute-start(f32[16,1024]{1,0:T(8,128)S(1)} %slice.13), channel_id=1, source_target_pairs={{0,4},{4,0},{8,12},{12,8},{16,20},{20,16},{24,28},{28,24},{1,5},{5... | collective-permute-start | bytes 196616 | tf_op jit(solution)/shard_map/ppermute | solution.py:119
  22.0 1.8 %collective-permute-start.8 = (s32[32,1024]{1,0:T(8,128)S(1)}, s32[32,1024]{1,0:T(8,128)S(1)}, u32[]{:S(2)}, u32[]{:S(2)}) collective-permute-start(s32[32,1024]{1,0:T(8,128)S(1)} %collective-permute-done.5.far0_ref.l2), channel_id=1, source_target_pairs={{0,4},{4,0},{8,12},{12,8},{16,20},{20,16},{24,28},{28,24},{1,5},{5... | collective-permute-start | bytes 393224 | tf_op jit(solution)/shard_map/ppermute | solution.py:119
  23.9 1.6 %collective-permute-start.2 = (s32[32,1024]{1,0:T(8,128)S(1)}, s32[32,1024]{1,0:T(8,128)S(1)}, u32[]{:S(2)}, u32[]{:S(2)}) collective-permute-start(s32[32,1024]{1,0:T(8,128)S(1)} %collective-permute-done.1.far1_ref.l2), channel_id=1, source_target_pairs={{0,4},{4,0},{8,12},{12,8},{16,20},{20,16},{24,28},{28,24},{1,5},{5... | collective-permute-start | bytes 393224 | tf_op jit(solution)/shard_map/ppermute | solution.py:119
  25.5 2.5 %shard_map.41 = (f32[16,2048]{1,0:T(8,128)S(1)}, f32[16,2048]{1,0:T(8,128)S(1)}) custom-call(s32[64,1024]{1,0:T(8,128)S(1)} %bitcast.11, s32[64,1024]{1,0:T(8,128)S(1)} %collective-permute-done.near_ref.l1, f32[16,1024]{1,0:T(8,128)S(1)} %get-tuple-element.27.first_ref, f32[16,1024]{1,0:T(8,128)S(1)} %collective-permute-done.6.second_ref), custom_call_target="tpu_custom_call" | custom-call | flops 4294967296 | bytes 1048576 | tf_op jit(solution)/shard_map/pallas_call | solution.py:65
  28.0 1.5 %shard_map.42 = (f32[16,2048]{1,0:T(8,128)S(1)}, f32[16,2048]{1,0:T(8,128)S(1)}) custom-call(s32[32,1024]{1,0:T(8,128)S(1)} %collective-permute-done.5.far0_ref.l2, s32[32,1024]{1,0:T(8,128)S(1)} %collective-permute-done.1.far1_ref.l2, f32[32,1024]{1,0:T(8,128)S(1)} %collective-permute-done.3.value_ref, f32[16,2048]{1,0:T(8,128)S(1)} %get-tuple-element.29.in0_ref, ...), custom_call_target="tpu_custom_call" | custom-call | flops 2147483648 | bytes 1048576 | tf_op jit(solution)/shard_map/pallas_call | solution.py:65
  33.5 3.3 %collective-permute-done.9.theirs_ref = f32[16,2048]{1,0:T(8,128)S(1)} collective-permute-done((f32[16,2048]{1,0:T(8,128)S(1)}, f32[16,2048]{1,0:T(8,128)S(1)}, u32[]{:S(2)}, u32[]{:S(2)}) %collective-permute-start.9) | collective-permute-done | bytes 131104 | tf_op jit(solution)/shard_map/ppermute | solution.py:119
  36.8 1.9 %shard_map.45 = (f32[16,4224]{1,0:T(8,128)S(1)}, f32[16,2048]{1,0:T(8,128)S(1)}) custom-call(s32[64,1024]{1,0:T(8,128)S(1)} %bitcast.12, s32[64,1024]{1,0:T(8,128)S(1)} %collective-permute-done.near_ref.l1, s32[32,1024]{1,0:T(8,128)S(1)} %collective-permute-done.5.far0_ref.l2, s32[32,1024]{1,0:T(8,128)S(1)} %collective-permute-done.8.leaf_ref.l3, ...), custom_call_target="tpu_custom_call" | custom-call | flops 4294967296 | bytes 1048576 | tf_op jit(solution)/shard_map/pallas_call | solution.py:65
  38.8 2.0 %shard_map.46 = (f32[16,4224]{1,0:T(8,128)S(1)}, f32[16,4096]{1,0:T(8,128)S(1)}) custom-call(s32[64,1024]{1,0:T(8,128)S(1)} %bitcast.13, s32[64,1024]{1,0:T(8,128)S(1)} %collective-permute-done.near_ref.l1, s32[32,1024]{1,0:T(8,128)S(1)} %collective-permute-done.1.far1_ref.l2, s32[32,1024]{1,0:T(8,128)S(1)} %collective-permute-done.2.leaf_ref.l3, ...), custom_call_target="tpu_custom_call" | custom-call | flops 4294967296 | bytes 1048576 | tf_op jit(solution)/shard_map/pallas_call | solution.py:65
  40.8 1.5 %collective-permute-done.13 = f32[16,4224]{1,0:T(8,128)S(1)} collective-permute-done((f32[16,4224]{1,0:T(8,128)S(1)}, f32[16,4224]{1,0:T(8,128)S(1)}, u32[]{:S(2)}, u32[]{:S(2)}) %collective-permute-start.13) | collective-permute-done | bytes 270368 | tf_op jit(solution)/shard_map/ppermute | solution.py:119
  42.4 1.6 %collective-permute-start.14 = (f32[16,4224]{1,0:T(8,128)S(1)}, f32[16,4224]{1,0:T(8,128)S(1)}, u32[]{:S(2)}, u32[]{:S(2)}) collective-permute-start(f32[16,4224]{1,0:T(8,128)S(1)} %add.22.mine_ref), channel_id=1, source_target_pairs={{0,2},{1,3},{2,0},{3,1},{4,6},{5,7},{6,4},{7,5},{8,10},{9,11},{10,... | collective-permute-start | bytes 811016 | tf_op jit(solution)/shard_map/ppermute | solution.py:119
  43.9 7.0 %collective-permute-done.14.theirs_ref = f32[16,4224]{1,0:T(8,128)S(1)} collective-permute-done((f32[16,4224]{1,0:T(8,128)S(1)}, f32[16,4224]{1,0:T(8,128)S(1)}, u32[]{:S(2)}, u32[]{:S(2)}) %collective-permute-start.14) | collective-permute-done | bytes 270368 | tf_op jit(solution)/shard_map/ppermute | solution.py:119
  51.0 3.3 %shard_map.47 = (f32[16,2304]{1,0:T(8,128)S(1)}, f8e4m3fn[192,4096]{1,0:T(32,128)(4,1)S(1)}, f32[16,1]{1,0:T(8,128)S(1)}, f32[16,4096]{1,0:T(8,128)S(1)}) custom-call(s32[64,1024]{1,0:T(8,128)S(1)} %bitcast.14, s32[64,1024]{1,0:T(8,128)S(1)} %collective-permute-done.near_ref.l1, s32[32,1024]{1,0:T(8,128)S(1)} %collective-permute-done.5.far0_ref.l2, ...), custom_call_target="tpu_custom_call" | custom-call | flops 4294967296 | bytes 1048576 | tf_op jit(solution)/shard_map/pallas_call | solution.py:65
  55.1 2.3 %shard_map.48.mine_ref = f32[16,2048]{1,0:T(8,128)S(1)} custom-call(s32[64,1024]{1,0:T(8,128)S(1)} %bitcast.15, s32[64,1024]{1,0:T(8,128)S(1)} %collective-permute-done.near_ref.l1, s32[32,1024]{1,0:T(8,128)S(1)} %collective-permute-done.1.far1_ref.l2, s32[32,1024]{1,0:T(8,128)S(1)} %collective-permute-done.2.leaf_ref.l3, ...), custom_call_target="tpu_custom_call" | custom-call | flops 4294967296 | bytes 1048576 | tf_op jit(solution)/shard_map/pallas_call | solution.py:65
  59.9 2.1 %shard_map.49 = (f32[16,4352]{1,0:T(8,128)S(1)}, f32[16,2304]{1,0:T(8,128)S(1)}) custom-call(s32[64,1024]{1,0:T(8,128)S(1)} %bitcast.16, s32[64,1024]{1,0:T(8,128)S(1)} %collective-permute-done.near_ref.l1, s32[32,1024]{1,0:T(8,128)S(1)} %collective-permute-done.5.far0_ref.l2, s32[32,1024]{1,0:T(8,128)S(1)} %collective-permute-done.8.leaf_ref.l3, ...), custom_call_target="tpu_custom_call" | custom-call | flops 4294967296 | bytes 1048576 | tf_op jit(solution)/shard_map/pallas_call | solution.py:65
  62.5 2.1 %shard_map.50 = (f32[16,4352]{1,0:T(8,128)S(1)}, f32[16,4352]{1,0:T(8,128)S(1)}) custom-call(s32[64,1024]{1,0:T(8,128)S(1)} %bitcast.17, s32[64,1024]{1,0:T(8,128)S(1)} %collective-permute-done.near_ref.l1, s32[32,1024]{1,0:T(8,128)S(1)} %collective-permute-done.1.far1_ref.l2, s32[32,1024]{1,0:T(8,128)S(1)} %collective-permute-done.2.leaf_ref.l3, ...), custom_call_target="tpu_custom_call" | custom-call | flops 4294967296 | bytes 1048576 | tf_op jit(solution)/shard_map/pallas_call | solution.py:65
  64.7 1.5 %collective-permute-done.20 = f32[16,4352]{1,0:T(8,128)S(1)} collective-permute-done((f32[16,4352]{1,0:T(8,128)S(1)}, f32[16,4352]{1,0:T(8,128)S(1)}, u32[]{:S(2)}, u32[]{:S(2)}) %collective-permute-start.20) | collective-permute-done | bytes 278560 | tf_op jit(solution)/shard_map/ppermute | solution.py:119
  66.3 1.6 %collective-permute-start.21 = (f32[16,4352]{1,0:T(8,128)S(1)}, f32[16,4352]{1,0:T(8,128)S(1)}, u32[]{:S(2)}, u32[]{:S(2)}) collective-permute-start(f32[16,4352]{1,0:T(8,128)S(1)} %add.23.mine_ref), channel_id=1, source_target_pairs={{0,2},{1,3},{2,0},{3,1},{4,6},{5,7},{6,4},{7,5},{8,10},{9,11},{10,... | collective-permute-start | bytes 835592 | tf_op jit(solution)/shard_map/ppermute | solution.py:119
  67.8 3.4 %collective-permute-start.11 = (f32[16,4096]{1,0:T(8,128)S(1)}, f32[16,4096]{1,0:T(8,128)S(1)}, u32[]{:S(2)}, u32[]{:S(2)}) collective-permute-start(f32[16,4096]{1,0:T(8,128)S(1)} %get-tuple-element.35.base_ref.refs_0_), channel_id=1, source_target_pairs={{0,16},{4,20},{8,24},{12,28},{16,0},{20,4},{24,8},{28,12},{1,17},{... | collective-permute-start | bytes 786440 | tf_op jit(solution)/shard_map/ppermute | solution.py:119
  71.7 11.4 %collective-permute-done.11.refs_2_ = f32[16,4096]{1,0:T(8,128)S(1)} collective-permute-done((f32[16,4096]{1,0:T(8,128)S(1)}, f32[16,4096]{1,0:T(8,128)S(1)}, u32[]{:S(2)}, u32[]{:S(2)}) %collective-permute-start.11) | collective-permute-done | bytes 262176 | tf_op jit(solution)/shard_map/ppermute | solution.py:119
  83.6 3.6 %shard_map.51 = (f32[16,2560]{1,0:T(8,128)S(1)}, f8e4m3fn[192,4096]{1,0:T(32,128)(4,1)S(1)}, f32[16,1]{1,0:T(8,128)S(1)}, f32[8,128]{1,0:T(8,128)}) custom-call(s32[64,1024]{1,0:T(8,128)S(1)} %bitcast.18, s32[64,1024]{1,0:T(8,128)S(1)} %collective-permute-done.near_ref.l1, s32[32,1024]{1,0:T(8,128)S(1)} %collective-permute-done.5.far0_ref.l2, ...), custom_call_target="tpu_custom_call" | custom-call | flops 4294967296 | bytes 1048576 | tf_op jit(solution)/shard_map/pallas_call | solution.py:65
  87.3 3.3 %collective-permute-start.22 = (f32[16,2560]{1,0:T(8,128)S(1)}, f32[16,2560]{1,0:T(8,128)S(1)}, u32[]{:S(2)}, u32[]{:S(2)}) collective-permute-start(f32[16,2560]{1,0:T(8,128)S(1)} %get-tuple-element.45), channel_id=1, source_target_pairs={{0,8},{4,12},{8,0},{12,4},{16,24},{20,28},{24,16},{28,20},{1,9},{5... | collective-permute-start | bytes 491528 | tf_op jit(solution)/shard_map/ppermute | solution.py:119
  90.6 2.6 %shard_map.52 = f32[16,2048]{1,0:T(8,128)S(1)} custom-call(s32[64,1024]{1,0:T(8,128)S(1)} %bitcast.19, s32[64,1024]{1,0:T(8,128)S(1)} %collective-permute-done.near_ref.l1, s32[32,1024]{1,0:T(8,128)S(1)} %collective-permute-done.1.far1_ref.l2, s32[32,1024]{1,0:T(8,128)S(1)} %collective-permute-done.2.leaf_ref.l3, ...), custom_call_target="tpu_custom_call" | custom-call | flops 4294967296 | bytes 1048576 | tf_op jit(solution)/shard_map/pallas_call | solution.py:65
  93.2 7.6 %collective-permute-done.22 = f32[16,2560]{1,0:T(8,128)S(1)} collective-permute-done((f32[16,2560]{1,0:T(8,128)S(1)}, f32[16,2560]{1,0:T(8,128)S(1)}, u32[]{:S(2)}, u32[]{:S(2)}) %collective-permute-start.22) | collective-permute-done | bytes 163872 | tf_op jit(solution)/shard_map/ppermute | solution.py:119
  103.9 2.0 %collective-permute-start.28 = (f32[16,2048]{1,0:T(8,128)S(1)}, f32[16,2048]{1,0:T(8,128)S(1)}, u32[]{:S(2)}, u32[]{:S(2)}) collective-permute-start(f32[16,2048]{1,0:T(8,128)S(1)} %add.25.refs_12_), channel_id=1, source_target_pairs={{0,16},{4,20},{8,24},{12,28},{16,0},{20,4},{24,8},{28,12},{1,17},{... | collective-permute-start | bytes 393224 | tf_op jit(solution)/shard_map/ppermute | solution.py:119
  105.9 1.5 %collective-permute-start.23 = (f32[16,2560]{1,0:T(8,128)S(1)}, f32[16,2560]{1,0:T(8,128)S(1)}, u32[]{:S(2)}, u32[]{:S(2)}) collective-permute-start(f32[16,2560]{1,0:T(8,128)S(1)} %add.24.refs_8_), channel_id=1, source_target_pairs={{0,4},{4,0},{8,12},{12,8},{16,20},{20,16},{24,28},{28,24},{1,5},{5... | collective-permute-start | bytes 491528 | tf_op jit(solution)/shard_map/ppermute | solution.py:119
  107.5 5.4 %collective-permute-done.24.refs_10_ = f32[16,2560]{1,0:T(8,128)S(1)} collective-permute-done((f32[16,2560]{1,0:T(8,128)S(1)}, f32[16,2560]{1,0:T(8,128)S(1)}, u32[]{:S(2)}, u32[]{:S(2)}) %collective-permute-start.24) | collective-permute-done | bytes 163872 | tf_op jit(solution)/shard_map/ppermute | solution.py:119
  116.3 7.7 %collective-permute-done.27.refs_13_ = f32[16,2048]{1,0:T(8,128)S(1)} collective-permute-done((f32[16,2048]{1,0:T(8,128)S(1)}, f32[16,2048]{1,0:T(8,128)S(1)}, u32[]{:S(2)}, u32[]{:S(2)}) %collective-permute-start.27) | collective-permute-done | bytes 131104 | tf_op jit(solution)/shard_map/ppermute | solution.py:119
  125.4 2.2 %combine.1 = (f32[64,4096]{1,0:T(8,128)}, f32[64,4096]{1,0:T(8,128)}) custom-call(s32[4]{0:T(128)S(1)} %pad_add_fusion.place_ref, f32[16,4096]{1,0:T(8,128)S(1)} %get-tuple-element.35.base_ref.refs_0_, f32[16,4096]{1,0:T(8,128)S(1)} %collective-permute-done.10.refs_1_, f32[16,4096]{1,0:T(8,128)S(1)} %collective-permute-done.11.refs_2_, ...), custom_call_target="tpu_custom_call" | custom-call | tf_op jit(solution)/shard_map/combine/pallas_call | solution.py:373
  (53 shorter events, 20.6 us)
Async XLA Ops:
  0.7 1.0 copy-start
  1.7 4.7 %copy-start.1 = (s32[1024,64]{0,1:T(8,128)S(1)}, s32[1024,64]{0,1:T(8,128)}, u32[]{:S(2)}) copy-start(s32[1024,64]{0,1:T(8,128)} %param.2) | copy-start | bytes 786436
  2.3 16.9 %collective-permute-start.3 = (f32[32,1024]{1,0:T(8,128)S(1)}, f32[32,1024]{1,0:T(8,128)S(1)}, u32[]{:S(2)}, u32[]{:S(2)}) collective-permute-start(f32[32,1024]{1,0:T(8,128)S(1)} %get-tuple-element.26), channel_id=1, source_target_pairs={{0,16},{4,20},{8,24},{12,28},{16,0},{20,4},{24,8},{28,12},{1,17},{... | collective-permute-start | bytes 393224 | tf_op jit(solution)/shard_map/ppermute | solution.py:119
  6.4 19.1 %collective-permute-start = (s32[64,1024]{1,0:T(8,128)S(1)}, s32[64,1024]{1,0:T(8,128)S(1)}, u32[]{:S(2)}, u32[]{:S(2)}) collective-permute-start(s32[64,1024]{1,0:T(8,128)S(1)} %bitcast.9), channel_id=1, source_target_pairs={{0,4},{4,0},{8,12},{12,8},{16,20},{20,16},{24,28},{28,24},{1,5},{5... | collective-permute-start | bytes 786440 | tf_op jit(solution)/shard_map/ppermute | solution.py:119
  7.9 14.0 %collective-permute-start.5 = (s32[32,1024]{1,0:T(8,128)S(1)}, s32[32,1024]{1,0:T(8,128)S(1)}, u32[]{:S(2)}, u32[]{:S(2)}) collective-permute-start(s32[32,1024]{1,0:T(8,128)S(1)} %get-tuple-element.50), channel_id=1, source_target_pairs={{0,16},{4,20},{8,24},{12,28},{16,0},{20,4},{24,8},{28,12},{1,17},{... | collective-permute-start | bytes 393224 | tf_op jit(solution)/shard_map/ppermute | solution.py:119
  8.3 15.6 %collective-permute-start.1 = (s32[32,1024]{1,0:T(8,128)S(1)}, s32[32,1024]{1,0:T(8,128)S(1)}, u32[]{:S(2)}, u32[]{:S(2)}) collective-permute-start(s32[32,1024]{1,0:T(8,128)S(1)} %get-tuple-element.51), channel_id=1, source_target_pairs={{0,16},{4,20},{8,24},{12,28},{16,0},{20,4},{24,8},{28,12},{1,17},{... | collective-permute-start | bytes 393224 | tf_op jit(solution)/shard_map/ppermute | solution.py:119
  10.9 14.6 %collective-permute-start.6 = (f32[16,1024]{1,0:T(8,128)S(1)}, f32[16,1024]{1,0:T(8,128)S(1)}, u32[]{:S(2)}, u32[]{:S(2)}) collective-permute-start(f32[16,1024]{1,0:T(8,128)S(1)} %get-tuple-element.28), channel_id=1, source_target_pairs={{0,4},{4,0},{8,12},{12,8},{16,20},{20,16},{24,28},{28,24},{1,5},{5... | collective-permute-start | bytes 196616 | tf_op jit(solution)/shard_map/ppermute | solution.py:119
  19.2 10.4 %collective-permute-start.4 = (f32[16,1024]{1,0:T(8,128)S(1)}, f32[16,1024]{1,0:T(8,128)S(1)}, u32[]{:S(2)}, u32[]{:S(2)}) collective-permute-start(f32[16,1024]{1,0:T(8,128)S(1)} %slice.13), channel_id=1, source_target_pairs={{0,4},{4,0},{8,12},{12,8},{16,20},{20,16},{24,28},{28,24},{1,5},{5... | collective-permute-start | bytes 196616 | tf_op jit(solution)/shard_map/ppermute | solution.py:119
  22.0 7.6 %collective-permute-start.8 = (s32[32,1024]{1,0:T(8,128)S(1)}, s32[32,1024]{1,0:T(8,128)S(1)}, u32[]{:S(2)}, u32[]{:S(2)}) collective-permute-start(s32[32,1024]{1,0:T(8,128)S(1)} %collective-permute-done.5.far0_ref.l2), channel_id=1, source_target_pairs={{0,4},{4,0},{8,12},{12,8},{16,20},{20,16},{24,28},{28,24},{1,5},{5... | collective-permute-start | bytes 393224 | tf_op jit(solution)/shard_map/ppermute | solution.py:119
  23.9 7.3 %collective-permute-start.2 = (s32[32,1024]{1,0:T(8,128)S(1)}, s32[32,1024]{1,0:T(8,128)S(1)}, u32[]{:S(2)}, u32[]{:S(2)}) collective-permute-start(s32[32,1024]{1,0:T(8,128)S(1)} %collective-permute-done.1.far1_ref.l2), channel_id=1, source_target_pairs={{0,4},{4,0},{8,12},{12,8},{16,20},{20,16},{24,28},{28,24},{1,5},{5... | collective-permute-start | bytes 393224 | tf_op jit(solution)/shard_map/ppermute | solution.py:119
  30.5 6.3 %collective-permute-start.9 = (f32[16,2048]{1,0:T(8,128)S(1)}, f32[16,2048]{1,0:T(8,128)S(1)}, u32[]{:S(2)}, u32[]{:S(2)}) collective-permute-start(f32[16,2048]{1,0:T(8,128)S(1)} %shard_map.44.mine_ref), channel_id=1, source_target_pairs={{0,8},{4,12},{8,0},{12,4},{16,24},{20,28},{24,16},{28,20},{1,9},{5... | collective-permute-start | bytes 393224 | tf_op jit(solution)/shard_map/ppermute | solution.py:119
  32.1 6.7 %collective-permute-start.7 = (f32[16,2048]{1,0:T(8,128)S(1)}, f32[16,2048]{1,0:T(8,128)S(1)}, u32[]{:S(2)}, u32[]{:S(2)}) collective-permute-start(f32[16,2048]{1,0:T(8,128)S(1)} %shard_map.43.mine_ref), channel_id=1, source_target_pairs={{0,8},{4,12},{8,0},{12,4},{16,24},{20,28},{24,16},{28,20},{1,9},{5... | collective-permute-start | bytes 393224 | tf_op jit(solution)/shard_map/ppermute | solution.py:119
  40.7 1.6 %collective-permute-start.13 = (f32[16,4224]{1,0:T(8,128)S(1)}, f32[16,4224]{1,0:T(8,128)S(1)}, u32[]{:S(2)}, u32[]{:S(2)}) collective-permute-start(f32[16,4224]{1,0:T(8,128)S(1)} %get-tuple-element.36), channel_id=1, source_target_pairs={{0,1},{1,0},{2,3},{3,2},{4,5},{5,4},{6,7},{7,6},{8,9},{9,8},{10,11... | collective-permute-start | bytes 811016 | tf_op jit(solution)/shard_map/ppermute | solution.py:119
  42.4 8.6 %collective-permute-start.14 = (f32[16,4224]{1,0:T(8,128)S(1)}, f32[16,4224]{1,0:T(8,128)S(1)}, u32[]{:S(2)}, u32[]{:S(2)}) collective-permute-start(f32[16,4224]{1,0:T(8,128)S(1)} %add.22.mine_ref), channel_id=1, source_target_pairs={{0,2},{1,3},{2,0},{3,1},{4,6},{5,7},{6,4},{7,5},{8,10},{9,11},{10,... | collective-permute-start | bytes 811016 | tf_op jit(solution)/shard_map/ppermute | solution.py:119
  54.3 5.6 %collective-permute-start.16 = (f32[16,2304]{1,0:T(8,128)S(1)}, f32[16,2304]{1,0:T(8,128)S(1)}, u32[]{:S(2)}, u32[]{:S(2)}) collective-permute-start(f32[16,2304]{1,0:T(8,128)S(1)} %get-tuple-element.39.mine_ref), channel_id=1, source_target_pairs={{0,8},{4,12},{8,0},{12,4},{16,24},{20,28},{24,16},{28,20},{1,9},{5... | collective-permute-start | bytes 442376 | tf_op jit(solution)/shard_map/ppermute | solution.py:119
  57.5 5.0 %collective-permute-start.15 = (f32[16,2048]{1,0:T(8,128)S(1)}, f32[16,2048]{1,0:T(8,128)S(1)}, u32[]{:S(2)}, u32[]{:S(2)}) collective-permute-start(f32[16,2048]{1,0:T(8,128)S(1)} %shard_map.48.mine_ref), channel_id=1, source_target_pairs={{0,8},{4,12},{8,0},{12,4},{16,24},{20,28},{24,16},{28,20},{1,9},{5... | collective-permute-start | bytes 393224 | tf_op jit(solution)/shard_map/ppermute | solution.py:119
  64.6 1.6 %collective-permute-start.20 = (f32[16,4352]{1,0:T(8,128)S(1)}, f32[16,4352]{1,0:T(8,128)S(1)}, u32[]{:S(2)}, u32[]{:S(2)}) collective-permute-start(f32[16,4352]{1,0:T(8,128)S(1)} %get-tuple-element.43), channel_id=1, source_target_pairs={{0,1},{1,0},{2,3},{3,2},{4,5},{5,4},{6,7},{7,6},{8,9},{9,8},{10,11... | collective-permute-start | bytes 835592 | tf_op jit(solution)/shard_map/ppermute | solution.py:119
  66.3 17.4 %collective-permute-start.21 = (f32[16,4352]{1,0:T(8,128)S(1)}, f32[16,4352]{1,0:T(8,128)S(1)}, u32[]{:S(2)}, u32[]{:S(2)}) collective-permute-start(f32[16,4352]{1,0:T(8,128)S(1)} %add.23.mine_ref), channel_id=1, source_target_pairs={{0,2},{1,3},{2,0},{3,1},{4,6},{5,7},{6,4},{7,5},{8,10},{9,11},{10,... | collective-permute-start | bytes 835592 | tf_op jit(solution)/shard_map/ppermute | solution.py:119
  67.8 15.3 %collective-permute-start.11 = (f32[16,4096]{1,0:T(8,128)S(1)}, f32[16,4096]{1,0:T(8,128)S(1)}, u32[]{:S(2)}, u32[]{:S(2)}) collective-permute-start(f32[16,4096]{1,0:T(8,128)S(1)} %get-tuple-element.35.base_ref.refs_0_), channel_id=1, source_target_pairs={{0,16},{4,20},{8,24},{12,28},{16,0},{20,4},{24,8},{28,12},{1,17},{... | collective-permute-start | bytes 786440 | tf_op jit(solution)/shard_map/ppermute | solution.py:119
  71.2 32.7 %collective-permute-start.10 = (f32[16,4096]{1,0:T(8,128)S(1)}, f32[16,4096]{1,0:T(8,128)S(1)}, u32[]{:S(2)}, u32[]{:S(2)}) collective-permute-start(f32[16,4096]{1,0:T(8,128)S(1)} %get-tuple-element.35.base_ref.refs_0_), channel_id=1, source_target_pairs={{0,4},{4,0},{8,12},{12,8},{16,20},{20,16},{24,28},{28,24},{1,5},{5... | collective-permute-start | bytes 786440 | tf_op jit(solution)/shard_map/ppermute | solution.py:119
  83.1 22.8 %collective-permute-start.12 = (f32[16,4096]{1,0:T(8,128)S(1)}, f32[16,4096]{1,0:T(8,128)S(1)}, u32[]{:S(2)}, u32[]{:S(2)}) collective-permute-start(f32[16,4096]{1,0:T(8,128)S(1)} %collective-permute-done.11.refs_2_), channel_id=1, source_target_pairs={{0,4},{4,0},{8,12},{12,8},{16,20},{20,16},{24,28},{28,24},{1,5},{5... | collective-permute-start | bytes 786440 | tf_op jit(solution)/shard_map/ppermute | solution.py:119
  83.6 18.7 %collective-permute-start.18 = (f32[16,4352]{1,0:T(8,128)S(1)}, f32[16,4352]{1,0:T(8,128)S(1)}, u32[]{:S(2)}, u32[]{:S(2)}) collective-permute-start(f32[16,4352]{1,0:T(8,128)S(1)} %get-tuple-element.42.refs_4_), channel_id=1, source_target_pairs={{0,16},{4,20},{8,24},{12,28},{16,0},{20,4},{24,8},{28,12},{1,17},{... | collective-permute-start | bytes 835592 | tf_op jit(solution)/shard_map/ppermute | solution.py:119
  87.3 13.5 %collective-permute-start.22 = (f32[16,2560]{1,0:T(8,128)S(1)}, f32[16,2560]{1,0:T(8,128)S(1)}, u32[]{:S(2)}, u32[]{:S(2)}) collective-permute-start(f32[16,2560]{1,0:T(8,128)S(1)} %get-tuple-element.45), channel_id=1, source_target_pairs={{0,8},{4,12},{8,0},{12,4},{16,24},{20,28},{24,16},{28,20},{1,9},{5... | collective-permute-start | bytes 491528 | tf_op jit(solution)/shard_map/ppermute | solution.py:119
  93.1 9.3 %collective-permute-start.26 = (f32[16,2048]{1,0:T(8,128)S(1)}, f32[16,2048]{1,0:T(8,128)S(1)}, u32[]{:S(2)}, u32[]{:S(2)}) collective-permute-start(f32[16,2048]{1,0:T(8,128)S(1)} %shard_map.52), channel_id=1, source_target_pairs={{0,8},{4,12},{8,0},{12,4},{16,24},{20,28},{24,16},{28,20},{1,9},{5... | collective-permute-start | bytes 393224 | tf_op jit(solution)/shard_map/ppermute | solution.py:119
  100.8 12.8 %collective-permute-start.17 = (f32[16,4352]{1,0:T(8,128)S(1)}, f32[16,4352]{1,0:T(8,128)S(1)}, u32[]{:S(2)}, u32[]{:S(2)}) collective-permute-start(f32[16,4352]{1,0:T(8,128)S(1)} %get-tuple-element.42.refs_4_), channel_id=1, source_target_pairs={{0,4},{4,0},{8,12},{12,8},{16,20},{20,16},{24,28},{28,24},{1,5},{5... | collective-permute-start | bytes 835592 | tf_op jit(solution)/shard_map/ppermute | solution.py:119
  102.3 10.5 %collective-permute-start.24 = (f32[16,2560]{1,0:T(8,128)S(1)}, f32[16,2560]{1,0:T(8,128)S(1)}, u32[]{:S(2)}, u32[]{:S(2)}) collective-permute-start(f32[16,2560]{1,0:T(8,128)S(1)} %add.24.refs_8_), channel_id=1, source_target_pairs={{0,16},{4,20},{8,24},{12,28},{16,0},{20,4},{24,8},{28,12},{1,17},{... | collective-permute-start | bytes 491528 | tf_op jit(solution)/shard_map/ppermute | solution.py:119
  102.4 13.9 %collective-permute-start.19 = (f32[16,4352]{1,0:T(8,128)S(1)}, f32[16,4352]{1,0:T(8,128)S(1)}, u32[]{:S(2)}, u32[]{:S(2)}) collective-permute-start(f32[16,4352]{1,0:T(8,128)S(1)} %collective-permute-done.18.refs_6_), channel_id=1, source_target_pairs={{0,4},{4,0},{8,12},{12,8},{16,20},{20,16},{24,28},{28,24},{1,5},{5... | collective-permute-start | bytes 835592 | tf_op jit(solution)/shard_map/ppermute | solution.py:119
  103.9 10.9 %collective-permute-start.28 = (f32[16,2048]{1,0:T(8,128)S(1)}, f32[16,2048]{1,0:T(8,128)S(1)}, u32[]{:S(2)}, u32[]{:S(2)}) collective-permute-start(f32[16,2048]{1,0:T(8,128)S(1)} %add.25.refs_12_), channel_id=1, source_target_pairs={{0,16},{4,20},{8,24},{12,28},{16,0},{20,4},{24,8},{28,12},{1,17},{... | collective-permute-start | bytes 393224 | tf_op jit(solution)/shard_map/ppermute | solution.py:119
  105.9 18.0 %collective-permute-start.23 = (f32[16,2560]{1,0:T(8,128)S(1)}, f32[16,2560]{1,0:T(8,128)S(1)}, u32[]{:S(2)}, u32[]{:S(2)}) collective-permute-start(f32[16,2560]{1,0:T(8,128)S(1)} %add.24.refs_8_), channel_id=1, source_target_pairs={{0,4},{4,0},{8,12},{12,8},{16,20},{20,16},{24,28},{28,24},{1,5},{5... | collective-permute-start | bytes 491528 | tf_op jit(solution)/shard_map/ppermute | solution.py:119
  112.8 12.5 %collective-permute-start.25 = (f32[16,2560]{1,0:T(8,128)S(1)}, f32[16,2560]{1,0:T(8,128)S(1)}, u32[]{:S(2)}, u32[]{:S(2)}) collective-permute-start(f32[16,2560]{1,0:T(8,128)S(1)} %collective-permute-done.24.refs_10_), channel_id=1, source_target_pairs={{0,4},{4,0},{8,12},{12,8},{16,20},{20,16},{24,28},{28,24},{1,5},{5... | collective-permute-start | bytes 491528 | tf_op jit(solution)/shard_map/ppermute | solution.py:119
  113.5 10.4 %collective-permute-start.27 = (f32[16,2048]{1,0:T(8,128)S(1)}, f32[16,2048]{1,0:T(8,128)S(1)}, u32[]{:S(2)}, u32[]{:S(2)}) collective-permute-start(f32[16,2048]{1,0:T(8,128)S(1)} %add.25.refs_12_), channel_id=1, source_target_pairs={{0,4},{4,0},{8,12},{12,8},{16,20},{20,16},{24,28},{28,24},{1,5},{5... | collective-permute-start | bytes 393224 | tf_op jit(solution)/shard_map/ppermute | solution.py:119
  114.8 10.5 %collective-permute-start.29 = (f32[16,2048]{1,0:T(8,128)S(1)}, f32[16,2048]{1,0:T(8,128)S(1)}, u32[]{:S(2)}, u32[]{:S(2)}) collective-permute-start(f32[16,2048]{1,0:T(8,128)S(1)} %collective-permute-done.28.refs_14_), channel_id=1, source_target_pairs={{0,4},{4,0},{8,12},{12,8},{16,20},{20,16},{24,28},{28,24},{1,5},{5... | collective-permute-start | bytes 393224 | tf_op jit(solution)/shard_map/ppermute | solution.py:119

commit v4 on v3

--- a/solution.py
+++ b/solution.py
@@ -95,15 +95,14 @@
 def collect(blocks, vector, out_ref, before_ref):
     top = top_of(vector)
     split = digits_of(vector, top, WIDE)
-    at = 0
-    for ref, start, trees in blocks:
+    for index, (ref, start, trees) in enumerate(blocks):
         rows = ref.shape[1]
+        at = index * rows + (0 if index < 2 else out_ref.shape[1] - len(blocks) * rows)
         part = jnp.dot(split, onehot(ref[start : start + trees, :]), preferred_element_type=F32)
         part = digits_sum(part, top, WIDE)
         if before_ref is not None:
             part = part + before_ref[:, at : at + rows]
         out_ref[:, at : at + rows] = part
-        at += rows
 
 
 def solution(mesh):
@@ -124,49 +123,71 @@
     def near_swap(value):
         return swap(value, "row", near_stride)
 
-    def gather(value):
-        far = far_swap(value)
-        near = near_swap(value)
-        return [value, near, far, near_swap(far)]
-
     def half_sum(value, axis, strides):
         for stride in strides[:-1]:
             value = value + swap(value, axis, stride)
         return value, swap(value, axis, strides[-1])
+
+    def leaf_sum(value, cut):
+        for stride in leaf_strides[:-1]:
+            value = value + swap(value, "leaf", stride)
+        parts = value[:, :cut], value[:, cut:]
+        return [(v, swap(v, "leaf", leaf_strides[-1])) for v in parts]
 
     def per_device(leaf_index, targets):
         width = targets.shape[1] // n_keys
         rows, trees = leaf_index.shape
         half = trees // 2
         columns, span = half * LEAVES, n_keys * rows
+        cut = span // 2
         scale = (LEAVES / (rows * n_row)) ** 0.5
         flops = 2 * columns * rows * 256
         row = lax.axis_index("row")
         key = (row // far_stride) * 2 + row % 2
-        place = jnp.stack([key, key ^ 1, key ^ 2, key ^ 3]).astype(jnp.int32)
+        share_stride = row_strides[-1]
+        share = (row // share_stride) % 2
+        core = lax.axis_index("leaf") % 2
+        place = jnp.stack([key, key ^ 1, key ^ 2, key ^ 3, share, key ^ (2 + core)]).astype(jnp.int32)
+
+        def share_of(first, second, tail=None):
+            value = jnp.where(share == 0, first, second)
+            return value if tail is None else jnp.concatenate([value, tail], 1)
+
+        def share_swap(value):
+            return swap(value, "row", share_stride)
+
+        def gather(value):
+            m = 2 * columns
+            tail = value[:, m:] if value.shape[1] > m else None
+            far = far_swap(share_of(value[:, :columns], value[:, columns:m], tail))
+            near = near_swap(value)
+            both = near_swap(far)
+            other = share_swap(jnp.concatenate([far[:, :columns], both[:, :columns]], 0))
+            return [value, near, far, both, other]
 
         def pack(place_ref, target_ref, own_ref, near_ref, far_ref):
             chunk = lambda m: target_ref[pl.ds(pl.multiple_of(place_ref[m] * width, width), width), :]
             own_ref[...] = chunk(0)
             near_ref[...] = chunk(1)
-            far_ref[:width, :] = chunk(2)
-            far_ref[width:, :] = chunk(3)
+            far_ref[...] = chunk(5)
 
         own = leaf_index.T
         t_own, t_near, t_far = pl.pallas_call(
             pack,
-            out_shape=(array(width, rows), array(width, rows), array(2 * width, rows)),
+            out_shape=(array(width, rows), array(width, rows), array(width, rows)),
             in_specs=[pl.BlockSpec(memory_space=pltpu.SMEM), VMEM],
             out_specs=(VMEM, VMEM, VMEM),
             compiler_params=pltpu.CompilerParams(vmem_limit_bytes=VMEM_LIMIT),
             name="pack",
         )(place, targets.T)
         far = [far_swap(own[:half]), far_swap(own[half:])]
-        t_far = far_swap(t_far)
+        t_mine = far_swap(t_far)
+        t_near = near_swap(t_near)
+        t_theirs = swap(t_mine, "leaf", 1)
+        t_far, t_relay = (jnp.where(core == c, t_mine, t_theirs) for c in range(2))
         near = near_swap(own)
-        t_near = near_swap(t_near)
         both = [near_swap(far[0]), near_swap(far[1])]
-        t_both = near_swap(t_far[width:])
+        t_both = near_swap(t_relay)
 
         def leaves_of(h):
             return own, near, far[h], both[h]
@@ -186,7 +207,7 @@
                 ref[...] = spread(blocks_of((own_ref, near_ref), h), split_ref, top, scale)
 
         def back0_far(far0_ref, far1_ref, value_ref, in0_ref, in1_ref, out0_ref, out1_ref, split_ref):
-            value = value_ref[:width, :]
+            value = value_ref[...]
             top = top_of(value)
             split_ref[...] = digits_of(value, top, NARROW)
             out0_ref[...] = in0_ref[...] + spread(((far0_ref, 0, half),), split_ref, top, scale)
@@ -212,67 +233,86 @@
             base = mine_ref[...] + theirs_ref[...]
             base_ref[...] = base
             collect(blocks_of((l0, l1, l2, l3), 0), base, out_ref, None)
-            out_ref[:, span:] = lane_sums(base * base)
+            out_ref[:, cut : cut + LANES] = lane_sums(base * base)
 
         def forward0_second(l0, l1, l2, l3, mine_ref, theirs_ref, in_ref, first_ref, out_ref, base_ref):
             base = mine_ref[...] + theirs_ref[...]
             base_ref[:, :columns] = first_ref[...]
             base_ref[:, columns:] = base
             collect(blocks_of((l0, l1, l2, l3), 1), base, out_ref, in_ref)
-            out_ref[:, span:] = in_ref[:, span:] + lane_sums(base * base)
+            tail = slice(cut, cut + LANES)
+            out_ref[:, tail] = in_ref[:, tail] + lane_sums(base * base)
 
         part, first = call(forward0_first, (w_shape, b_half), [], 4 * flops, *leaves_of(0), *pairs[0])
         part, b0 = call(
             forward0_second, (w_shape, array(width, 2 * columns)), [], 4 * flops, *leaves_of(1), *pairs[1], part, first
         )
-        w_pair = half_sum(part, "leaf", leaf_strides)
-
-        split_shape = jax.ShapeDtypeStruct((NARROW[1] * width, span), F8)
-        top_shape = array(width, 1)
-
-        def backward_first(l0, l1, l2, l3, mine_ref, theirs_ref, *refs):
-            rows_ref, (out_ref, split_ref, top_ref, last_ref) = refs[:-4], refs[-4:]
-            value = mine_ref[:, :span] + theirs_ref[:, :span]
-            if not rows_ref:
-                last_ref[...] = value
+        w_pairs = leaf_sum(part, cut + LANES)
+
+        def backward_rows0(own_ref, near_ref, mine_ref, theirs_ref, *refs):
+            rows_ref, (out0_ref, out1_ref, last_ref, split_ref) = refs[:-4], refs[-4:]
+            value = mine_ref[:, :cut] + theirs_ref[:, :cut]
+            last_ref[...] = value
+            top = top_of(value)
+            split_ref[...] = digits_of(value, top, NARROW)
+            at = columns
+            for other in [value] + [ref[...] for ref in rows_ref]:
+                out0_ref[:, at : at + LANES] = (scale * scale) * lane_sums(value * other)
+                at += LANES
+            out0_ref[:, at:] = (mine_ref[:, cut:] + theirs_ref[:, cut:]) * (1.0 / n_share)
+            blocks = (own_ref, near_ref)
+            out0_ref[:, :columns] = spread(blocks_of(blocks, 0), split_ref, top, scale * scale)
+            out1_ref[...] = spread(blocks_of(blocks, 1), split_ref, top, scale * scale)
+
+        def backward_rows1(far_ref, both_ref, mine_ref, theirs_ref, in_ref, *refs):
+            rows_ref, (out_ref, last_ref, split_ref, top_ref) = refs[:-4], refs[-4:]
+            value = mine_ref[...] + theirs_ref[...]
+            last_ref[...] = value
             top = top_of(value)
             top_ref[...] = top
             split_ref[...] = digits_of(value, top, NARROW)
-            tail = [value * value] + [value * ref[...] for ref in rows_ref]
             at = columns
-            for product in tail:
-                out_ref[:, at : at + LANES] = (scale * scale) * lane_sums(product)
+            for other in [value] + [ref[...] for ref in rows_ref]:
+                found = (scale * scale) * lane_sums(value * other)
+                out_ref[:, at : at + LANES] = in_ref[:, at : at + LANES] + found
                 at += LANES
-            out_ref[:, at:] = (mine_ref[:, span:] + theirs_ref[:, span:]) * (1.0 / n_share)
-            out_ref[:, :columns] = spread(
-                blocks_of((l0, l1, l2, l3), 0), split_ref, top, scale * scale
+            out_ref[:, at:] = in_ref[:, at:]
+            blocks = ((far_ref, 0, half), (both_ref, 0, half))
+            found = spread(blocks, split_ref, top, scale * scale)
+            out_ref[:, :columns] = in_ref[:, :columns] + found
+
+        def backward_last(far_ref, both_ref, split_ref, top_ref, in_ref, out_ref):
+            blocks = ((far_ref, 0, half), (both_ref, 0, half))
+            out_ref[...] = in_ref[...] + spread(blocks, split_ref, top_ref[...], scale * scale)
+
+        def backward(w_pairs, extra, rows_before=((), ())):
+            payload, w_half = array(width, columns + extra * LANES), array(width, cut)
+            part0, part1, last0 = call(
+                backward_rows0,
+                (payload, b_half, w_half),
+                [split_two],
+                4 * flops,
+                own,
+                near,
+                *w_pairs[0],
+                *rows_before[0],
             )
-            if rows_ref:
-                last_ref[...] = jnp.zeros_like(last_ref)
-
-        def backward_second(l0, l1, l2, l3, split_ref, top_ref, out_ref):
-            out_ref[...] = spread(blocks_of((l0, l1, l2, l3), 1), split_ref, top_ref[...], scale * scale)
-
-        def backward(w_pair, extra, *rows_before):
-            part, split, top, last = call(
-                backward_first,
-                (
-                    array(width, columns + extra * LANES),
-                    split_shape,
-                    top_shape,
-                    array(8, LANES) if rows_before else array(width, span),
-                ),
+            part0, last1, split, top = call(
+                backward_rows1,
+                (payload, w_half, jax.ShapeDtypeStruct((NARROW[1] * width, cut), F8), array(width, 1)),
                 [],
-                4 * flops,
-                *leaves_of(0),
-                *w_pair,
-                *rows_before,
+                2 * flops,
+                far[0],
+                both[0],
+                *w_pairs[1],
+                part0,
+                *rows_before[1],
             )
-            pairs = [half_sum(part, "row", row_strides)]
-            part = call(backward_second, b_half, [], 4 * flops, *leaves_of(1), split, top)
-            return pairs + [half_sum(part, "row", row_strides)], last
-
-        pairs, w0 = backward(w_pair, 2)
+            pairs = [half_sum(part0, "row", row_strides)]
+            part1 = call(backward_last, b_half, [], 2 * flops, far[1], both[1], split, top, part1)
+            return pairs + [half_sum(part1, "row", row_strides)], ((last0,), (last1,))
+
+        pairs, w0 = backward(w_pairs, 2)
 
         def step_of(norm, curve):
             return jnp.where(norm > 0.0, norm / (curve + ridge_weight * norm), 1.0)
@@ -294,8 +334,8 @@
             res_ref[:, :columns] = res
             res_ref[:, columns:] = tail
             collect(blocks_of((l0, l1, l2, l3), 0), res, out_ref, None)
-            out_ref[:, span : span + LANES] = lane_sums(res * res)
-            out_ref[:, span + LANES :] = lane_sums(res * base)
+            out_ref[:, cut : cut + LANES] = lane_sums(res * res)
+            out_ref[:, cut + LANES : cut + 2 * LANES] = lane_sums(res * base)
 
         def forward1_second(
             l0, l1, l2, l3, mine_ref, theirs_ref, base_ref, in_ref, first_ref, out_ref, res_ref
@@ -307,8 +347,9 @@
             res_ref[:, columns : 2 * columns] = res
             res_ref[:, 2 * columns :] = tail
             collect(blocks_of((l0, l1, l2, l3), 1), res, out_ref, in_ref)
-            out_ref[:, span : span + LANES] = in_ref[:, span : span + LANES] + lane_sums(res * res)
-            out_ref[:, span + LANES :] = in_ref[:, span + LANES :] + lane_sums(res * base)
+            for index, other in enumerate((res, base)):
+                tail = slice(cut + index * LANES, cut + (index + 1) * LANES)
+                out_ref[:, tail] = in_ref[:, tail] + lane_sums(res * other)
 
         w_shape = array(width, span + 2 * LANES)
         part, first = call(
@@ -325,22 +366,25 @@
             part,
             first,
         )
-        w_pair = half_sum(part, "leaf", leaf_strides)
-
-        pairs, _ = backward(w_pair, 4, w0)
+        w_pairs = leaf_sum(part, cut + 2 * LANES)
+
+        pairs, _ = backward(w_pairs, 4, w0)
         b2 = [mine + theirs for mine, theirs in pairs]
 
         def combine(place_ref, *refs):
-            bases, ress, firsts, seconds = (refs[k * n_keys : (k + 1) * n_keys] for k in range(4))
-            solution_ref, residual_ref = refs[4 * n_keys :]
+            base, res = refs[:5], refs[5:10]
+            (image0, near0, image1, near1, far2, both2, z_far2, z_both2) = refs[10:18]
+            solution_ref, residual_ref = refs[18:]
 
             def tail(ref, start, at):
                 return scalar(ref[:, start + at * LANES : start + (at + 1) * LANES])
 
             keys = range(n_keys)
-            b = [tail(ress[m], 2 * columns, 0) for m in keys]
-            a = [tail(ress[m], 2 * columns, 1) for m in keys]
-            e, f, c, d = ([tail(firsts[m], columns, at) for m in keys] for at in range(4))
+            starts = (2 * columns, 2 * columns, columns, columns)
+            b = [tail(res[m], starts[m], 0) for m in keys]
+            a = [tail(res[m], starts[m], 1) for m in keys]
+            tails = (image0, near0, far2, both2)
+            e, f, c, d = ([tail(tails[m], columns, at) for m in keys] for at in range(4))
             norm0 = sum(a)
             alpha0 = norm0 / (sum(b) + ridge_weight * norm0)
             theta = [step_of(a[m], b[m]) for m in keys]
@@ -355,29 +399,43 @@
                 for m in keys
             )
             alpha1 = norm1 / curve
-            for m in keys:
+
+            def finish(m, at_columns, v0, v1, v2):
                 at = pl.ds(pl.multiple_of(place_ref[m] * width, width), width)
-                for h, images in enumerate((firsts, seconds)):
-                    of_half = slice(h * columns, (h + 1) * columns)
-                    base, res, image = bases[m][:, of_half], ress[m][:, of_half], images[m][:, :columns]
-                    solution_ref[at, of_half] = (alpha0 + alpha1 * other[m]) * base + (
-                        alpha1 * rho[m]
-                    ) * res
-                    residual_ref[at, of_half] = (
-                        ((1.0 - rho[m]) - alpha1 * other[m] / theta[m]) * base
-                        + (rho[m] + alpha1 * (other[m] / theta[m] - ridge_weight * rho[m])) * res
-                        - (alpha1 * rho[m]) * image
-                    )
-
+                solution_ref[at, at_columns] = (alpha0 + alpha1 * other[m]) * v0 + (alpha1 * rho[m]) * v1
+                residual_ref[at, at_columns] = (
+                    ((1.0 - rho[m]) - alpha1 * other[m] / theta[m]) * v0
+                    + (rho[m] + alpha1 * (other[m] / theta[m] - ridge_weight * rho[m])) * v1
+                    - (alpha1 * rho[m]) * v2
+                )
+
+            for m, images in enumerate(((image0, image1), (near0, near1))):
+                for h in range(2):
+                    at = slice(h * columns, (h + 1) * columns)
+                    finish(m, at, base[m][:, at], res[m][:, at], images[h][:, :columns])
+            mine = pl.ds(pl.multiple_of(place_ref[4] * columns, columns), columns)
+            theirs = pl.ds(pl.multiple_of((1 - place_ref[4]) * columns, columns), columns)
+            for m, image, z_image in ((2, far2, z_far2), (3, both2, z_both2)):
+                finish(m, mine, base[m][:, :columns], res[m][:, :columns], image[:, :columns])
+                z = slice((m - 2) * width, (m - 1) * width)
+                finish(m, theirs, base[4][z, :], res[4][z, :], z_image[...])
+
+        far = share_of(b2[0][:, :columns], b2[1], b2[0][:, columns:])
+        far = far_swap(far)
+        nears = near_swap(b2[0]), near_swap(b2[1])
+        z_far = share_swap(far[:, :columns])
+        both = near_swap(far)
+        z_both = share_swap(both[:, :columns])
         out = array(n_keys * width, 2 * columns)
+        parts = (*gather(b0), *gather(res), b2[0], nears[0], b2[1], nears[1], far, both, z_far, z_both)
         result = pl.pallas_call(
             combine,
             out_shape=(out, out),
-            in_specs=[pl.BlockSpec(memory_space=pltpu.SMEM)] + [VMEM] * (4 * n_keys),
+            in_specs=[pl.BlockSpec(memory_space=pltpu.SMEM)] + [VMEM] * len(parts),
             out_specs=(VMEM, VMEM),
             compiler_params=pltpu.CompilerParams(vmem_limit_bytes=VMEM_LIMIT),
             name="combine",
-        )(place, *gather(b0), *gather(res), *gather(b2[0]), *gather(b2[1]))
+        )(place, *parts)
         return tuple(value.T for value in result)
 
     return jax.shard_map(

time: 128 us -> 114 us (0.89)
  waiting for transfers between devices: 58 us -> 45.3 us
    ppermute x30 -> x35, waiting for transfers between devices: 58 us -> 45.3 us  [swap(): return lax.ppermute(value, axis, [(i, i ^ stride) for i in range(size)])]
    pallas_call x12 -> x14, Pallas kernels: 25.7 us -> 24.7 us  [call(): pl.pallas_call(kernel, out_shape=outs, in_specs=[VMEM] * len(args), out_s...]
    ppermute x30 -> x35, starting transfers between devices: 39.1 us -> 38.9 us  [swap(): return lax.ppermute(value, axis, [(i, i ^ stride) for i in range(size)])]
  transfers between devices with their start and end apart: 30 -> 35, of which waited for: 15 -> 17; matrix products, arithmetic and copies ran while one was open for 0% -> 0% of each run, Pallas kernels for 14% -> 20%
where the time goes in v4:
time: 114 us
  waiting for transfers between devices  45.3 us (40%)
  starting transfers between devices  38.9 us (34%)
  Pallas kernels  27.5 us (24%)
  local copies, waits for them, and re-layouts  1.15 us (1%)
    ppermute x35, waiting for transfers between devices, swap(): return lax.ppermute(value, axis, [(i, i ^ stride) for i in range(size)])  45.3 us
    ppermute x35, starting transfers between devices, swap(): return lax.ppermute(value, axis, [(i, i ^ stride) for i in range(size)])  38.9 us
    pallas_call x14, Pallas kernels, call(): pl.pallas_call(kernel, out_shape=outs, in_specs=[VMEM] * len(args), out_s...  24.7 us
  transfers between devices with their start and end apart: 35, of which 17 were waited for; matrix products, arithmetic and copies ran while one was open for 0% of the time, Pallas kernels for 20%

profile of v4, /device:TPU:0, one launch (start us, length us, event | category | flops | bytes accessed | tf_op | source)
XLA Modules:
  0.0 114.1 jit_solution(7459910297935486850)
XLA Ops:
  2.3 4.1 %collective-permute-start.3 = (f32[16,1024]{1,0:T(8,128)S(1)}, f32[16,1024]{1,0:T(8,128)S(1)}, u32[]{:S(2)}, u32[]{:S(2)}) collective-permute-start(f32[16,1024]{1,0:T(8,128)S(1)} %get-tuple-element.31), channel_id=1, source_target_pairs={{0,16},{4,20},{8,24},{12,28},{16,0},{20,4},{24,8},{28,12},{1,17},{... | collective-permute-start | bytes 196616 | tf_op jit(solution)/shard_map/ppermute | solution.py:118
  8.4 1.6 %collective-permute-done.3 = f32[16,1024]{1,0:T(8,128)S(1)} collective-permute-done((f32[16,1024]{1,0:T(8,128)S(1)}, f32[16,1024]{1,0:T(8,128)S(1)}, u32[]{:S(2)}, u32[]{:S(2)}) %collective-permute-start.3) | collective-permute-done | bytes 65568 | tf_op jit(solution)/shard_map/ppermute | solution.py:118
  10.1 1.6 %collective-permute-start.6 = (s32[32,1024]{1,0:T(8,128)S(1)}, s32[32,1024]{1,0:T(8,128)S(1)}, u32[]{:S(2)}, u32[]{:S(2)}) collective-permute-start(s32[32,1024]{1,0:T(8,128)S(1)} %get-tuple-element.62), channel_id=1, source_target_pairs={{0,16},{4,20},{8,24},{12,28},{16,0},{20,4},{24,8},{28,12},{1,17},{... | collective-permute-start | bytes 393224 | tf_op jit(solution)/shard_map/ppermute | solution.py:118
  13.1 1.8 %collective-permute-start.5 = (f32[16,1024]{1,0:T(8,128)S(1)}, f32[16,1024]{1,0:T(8,128)S(1)}, u32[]{:S(2)}, u32[]{:S(2)}) collective-permute-start(f32[16,1024]{1,0:T(8,128)S(1)} %get-tuple-element.65), channel_id=1, source_target_pairs={{0,4},{4,0},{8,12},{12,8},{16,20},{20,16},{24,28},{28,24},{1,5},{5... | collective-permute-start | bytes 196616 | tf_op jit(solution)/shard_map/ppermute | solution.py:118
  14.9 8.1 %collective-permute-done.6.far0_ref.l2.far_ref = s32[32,1024]{1,0:T(8,128)S(1)} collective-permute-done((s32[32,1024]{1,0:T(8,128)S(1)}, s32[32,1024]{1,0:T(8,128)S(1)}, u32[]{:S(2)}, u32[]{:S(2)}) %collective-permute-start.6) | collective-permute-done | bytes 131104 | tf_op jit(solution)/shard_map/ppermute | solution.py:118
  23.0 1.7 %collective-permute-start.9 = (s32[32,1024]{1,0:T(8,128)S(1)}, s32[32,1024]{1,0:T(8,128)S(1)}, u32[]{:S(2)}, u32[]{:S(2)}) collective-permute-start(s32[32,1024]{1,0:T(8,128)S(1)} %collective-permute-done.6.far0_ref.l2.far_ref), channel_id=1, source_target_pairs={{0,4},{4,0},{8,12},{12,8},{16,20},{20,16},{24,28},{28,24},{1,5},{5... | collective-permute-start | bytes 393224 | tf_op jit(solution)/shard_map/ppermute | solution.py:118
  25.4 1.7 %collective-permute-start.2 = (s32[32,1024]{1,0:T(8,128)S(1)}, s32[32,1024]{1,0:T(8,128)S(1)}, u32[]{:S(2)}, u32[]{:S(2)}) collective-permute-start(s32[32,1024]{1,0:T(8,128)S(1)} %collective-permute-done.1.far1_ref.l2.far_ref), channel_id=1, source_target_pairs={{0,4},{4,0},{8,12},{12,8},{16,20},{20,16},{24,28},{28,24},{1,5},{5... | collective-permute-start | bytes 393224 | tf_op jit(solution)/shard_map/ppermute | solution.py:118
  27.1 2.5 %shard_map.41 = (f32[16,2048]{1,0:T(8,128)S(1)}, f32[16,2048]{1,0:T(8,128)S(1)}) custom-call(s32[64,1024]{1,0:T(8,128)S(1)} %bitcast.13, s32[64,1024]{1,0:T(8,128)S(1)} %collective-permute-done.near_ref.l1, f32[16,1024]{1,0:T(8,128)S(1)} %get-tuple-element.32.first_ref, f32[16,1024]{1,0:T(8,128)S(1)} %collective-permute-done.7.second_ref), custom_call_target="tpu_custom_call" | custom-call | flops 4294967296 | bytes 1048576 | tf_op jit(solution)/shard_map/pallas_call | solution.py:65
  33.0 2.1 %collective-permute-start.8 = (f32[16,2048]{1,0:T(8,128)S(1)}, f32[16,2048]{1,0:T(8,128)S(1)}, u32[]{:S(2)}, u32[]{:S(2)}) collective-permute-start(f32[16,2048]{1,0:T(8,128)S(1)} %shard_map.43.mine_ref), channel_id=1, source_target_pairs={{0,8},{4,12},{8,0},{12,4},{16,24},{20,28},{24,16},{28,20},{1,9},{5... | collective-permute-start | bytes 393224 | tf_op jit(solution)/shard_map/ppermute | solution.py:118
  35.1 3.2 %collective-permute-done.10.theirs_ref = f32[16,2048]{1,0:T(8,128)S(1)} collective-permute-done((f32[16,2048]{1,0:T(8,128)S(1)}, f32[16,2048]{1,0:T(8,128)S(1)}, u32[]{:S(2)}, u32[]{:S(2)}) %collective-permute-start.10) | collective-permute-done | bytes 131104 | tf_op jit(solution)/shard_map/ppermute | solution.py:118
  38.3 1.9 %shard_map.45 = (f32[16,4224]{1,0:T(8,128)S(1)}, f32[16,2048]{1,0:T(8,128)S(1)}) custom-call(s32[64,1024]{1,0:T(8,128)S(1)} %bitcast.14, s32[64,1024]{1,0:T(8,128)S(1)} %collective-permute-done.near_ref.l1, s32[32,1024]{1,0:T(8,128)S(1)} %collective-permute-done.6.far0_ref.l2.far_ref, s32[32,1024]{1,0:T(8,128)S(1)} %collective-permute-done.9.leaf_ref.l3.both_ref, ...), custom_call_target="tpu_custom_call" | custom-call | flops 4294967296 | bytes 1048576 | tf_op jit(solution)/shard_map/pallas_call | solution.py:65
  40.3 2.0 %shard_map.46 = (f32[16,4224]{1,0:T(8,128)S(1)}, f32[16,4096]{1,0:T(8,128)S(1)}) custom-call(s32[64,1024]{1,0:T(8,128)S(1)} %bitcast.15, s32[64,1024]{1,0:T(8,128)S(1)} %collective-permute-done.near_ref.l1, s32[32,1024]{1,0:T(8,128)S(1)} %collective-permute-done.1.far1_ref.l2.far_ref, s32[32,1024]{1,0:T(8,128)S(1)} %collective-permute-done.2.leaf_ref.l3.both_ref, ...), custom_call_target="tpu_custom_call" | custom-call | flops 4294967296 | bytes 1048576 | tf_op jit(solution)/shard_map/pallas_call | solution.py:65
  43.9 1.6 %collective-permute-start.17 = (f32[16,2176]{1,0:T(8,128)S(1)}, f32[16,2176]{1,0:T(8,128)S(1)}, u32[]{:S(2)}, u32[]{:S(2)}) collective-permute-start(f32[16,2176]{1,0:T(8,128)S(1)} %slice.71.mine_ref), channel_id=1, source_target_pairs={{0,2},{1,3},{2,0},{3,1},{4,6},{5,7},{6,4},{7,5},{8,10},{9,11},{10,... | collective-permute-start | bytes 417800 | tf_op jit(solution)/shard_map/ppermute | solution.py:118
  47.1 3.5 %collective-permute-done.17.theirs_ref = f32[16,2176]{1,0:T(8,128)S(1)} collective-permute-done((f32[16,2176]{1,0:T(8,128)S(1)}, f32[16,2176]{1,0:T(8,128)S(1)}, u32[]{:S(2)}, u32[]{:S(2)}) %collective-permute-start.17) | collective-permute-done | bytes 139296 | tf_op jit(solution)/shard_map/ppermute | solution.py:118
  50.5 2.7 %shard_map.47 = (f32[16,2304]{1,0:T(8,128)S(1)}, f32[16,2048]{1,0:T(8,128)S(1)}, f32[16,2048]{1,0:T(8,128)S(1)}) custom-call(s32[64,1024]{1,0:T(8,128)S(1)} %bitcast.16, s32[64,1024]{1,0:T(8,128)S(1)} %collective-permute-done.near_ref.l1, f32[16,2176]{1,0:T(8,128)S(1)} %slice.71.mine_ref, f32[16,2176]{1,0:T(8,128)S(1)} %collective-permute-done.17.theirs_ref), custom_call_target="tpu_custom_call" | custom-call | flops 4294967296 | bytes 1048576 | tf_op jit(solution)/shard_map/pallas_call | solution.py:65
  56.4 1.8 %collective-permute-start.18 = (f32[16,2048]{1,0:T(8,128)S(1)}, f32[16,2048]{1,0:T(8,128)S(1)}, u32[]{:S(2)}, u32[]{:S(2)}) collective-permute-start(f32[16,2048]{1,0:T(8,128)S(1)} %shard_map.49.mine_ref), channel_id=1, source_target_pairs={{0,8},{4,12},{8,0},{12,4},{16,24},{20,28},{24,16},{28,20},{1,9},{5... | collective-permute-start | bytes 393224 | tf_op jit(solution)/shard_map/ppermute | solution.py:118
  58.1 2.3 %collective-permute-done.19.theirs_ref = f32[16,2304]{1,0:T(8,128)S(1)} collective-permute-done((f32[16,2304]{1,0:T(8,128)S(1)}, f32[16,2304]{1,0:T(8,128)S(1)}, u32[]{:S(2)}, u32[]{:S(2)}) %collective-permute-start.19) | collective-permute-done | bytes 147488 | tf_op jit(solution)/shard_map/ppermute | solution.py:118
  60.5 2.1 %shard_map.50 = (f32[16,4352]{1,0:T(8,128)S(1)}, f32[16,2304]{1,0:T(8,128)S(1)}) custom-call(s32[64,1024]{1,0:T(8,128)S(1)} %bitcast.17, s32[64,1024]{1,0:T(8,128)S(1)} %collective-permute-done.near_ref.l1, s32[32,1024]{1,0:T(8,128)S(1)} %collective-permute-done.6.far0_ref.l2.far_ref, s32[32,1024]{1,0:T(8,128)S(1)} %collective-permute-done.9.leaf_ref.l3.both_ref, ...), custom_call_target="tpu_custom_call" | custom-call | flops 4294967296 | bytes 1048576 | tf_op jit(solution)/shard_map/pallas_call | solution.py:65
  62.5 2.1 %shard_map.51 = (f32[16,4352]{1,0:T(8,128)S(1)}, f32[16,4352]{1,0:T(8,128)S(1)}) custom-call(s32[64,1024]{1,0:T(8,128)S(1)} %bitcast.18, s32[64,1024]{1,0:T(8,128)S(1)} %collective-permute-done.near_ref.l1, s32[32,1024]{1,0:T(8,128)S(1)} %collective-permute-done.1.far1_ref.l2.far_ref, s32[32,1024]{1,0:T(8,128)S(1)} %collective-permute-done.2.leaf_ref.l3.both_ref, ...), custom_call_target="tpu_custom_call" | custom-call | flops 4294967296 | bytes 1048576 | tf_op jit(solution)/shard_map/pallas_call | solution.py:65
  66.3 1.6 %collective-permute-start.26 = (f32[16,2304]{1,0:T(8,128)S(1)}, f32[16,2304]{1,0:T(8,128)S(1)}, u32[]{:S(2)}, u32[]{:S(2)}) collective-permute-start(f32[16,2304]{1,0:T(8,128)S(1)} %slice.75.mine_ref), channel_id=1, source_target_pairs={{0,2},{1,3},{2,0},{3,1},{4,6},{5,7},{6,4},{7,5},{8,10},{9,11},{10,... | collective-permute-start | bytes 442376 | tf_op jit(solution)/shard_map/ppermute | solution.py:118
  67.9 1.6 %collective-permute-start.21 = (f32[16,2304]{1,0:T(8,128)S(1)}, f32[16,2304]{1,0:T(8,128)S(1)}, u32[]{:S(2)}, u32[]{:S(2)}) collective-permute-start(f32[16,2304]{1,0:T(8,128)S(1)} %pad_maximum_fusion.3), channel_id=1, source_target_pairs={{0,16},{4,20},{8,24},{12,28},{16,0},{20,4},{24,8},{28,12},{1,17},{... | collective-permute-start | bytes 442376 | tf_op jit(solution)/shard_map/ppermute | solution.py:118
  70.1 2.8 %collective-permute-done.26.theirs_ref = f32[16,2304]{1,0:T(8,128)S(1)} collective-permute-done((f32[16,2304]{1,0:T(8,128)S(1)}, f32[16,2304]{1,0:T(8,128)S(1)}, u32[]{:S(2)}, u32[]{:S(2)}) %collective-permute-start.26) | collective-permute-done | bytes 147488 | tf_op jit(solution)/shard_map/ppermute | solution.py:118
  72.9 2.6 %shard_map.52 = (f32[16,2560]{1,0:T(8,128)S(1)}, f32[16,2048]{1,0:T(8,128)S(1)}, f32[16,2048]{1,0:T(8,128)}) custom-call(s32[64,1024]{1,0:T(8,128)S(1)} %bitcast.19, s32[64,1024]{1,0:T(8,128)S(1)} %collective-permute-done.near_ref.l1, f32[16,2304]{1,0:T(8,128)S(1)} %slice.75.mine_ref, f32[16,2304]{1,0:T(8,128)S(1)} %collective-permute-done.26.theirs_ref, ...), custom_call_target="tpu_custom_call" | custom-call | flops 4294967296 | bytes 1048576 | tf_op jit(solution)/shard_map/pallas_call | solution.py:65
  75.4 1.7 %shard_map.53 = (f32[16,2560]{1,0:T(8,128)S(1)}, f32[16,2048]{1,0:T(8,128)}, f8e4m3fn[192,2048]{1,0:T(32,128)(4,1)S(1)}, f32[16,1]{1,0:T(8,128)S(1)}) custom-call(s32[32,1024]{1,0:T(8,128)S(1)} %collective-permute-done.6.far0_ref.l2.far_ref, s32[32,1024]{1,0:T(8,128)S(1)} %collective-permute-done.9.leaf_ref.l3.both_ref, f32[16,2048]{1,0:T(8,128)S(1)} %slice.74.mine_ref, ...), custom_call_target="tpu_custom_call" | custom-call | flops 2147483648 | bytes 1048576 | tf_op jit(solution)/shard_map/pallas_call | solution.py:65
  85.2 1.8 %collective-permute-start.31 = (f32[16,2560]{1,0:T(8,128)S(1)}, f32[16,2560]{1,0:T(8,128)S(1)}, u32[]{:S(2)}, u32[]{:S(2)}) collective-permute-start(f32[16,2560]{1,0:T(8,128)S(1)} %pad_maximum_fusion.2), channel_id=1, source_target_pairs={{0,16},{4,20},{8,24},{12,28},{16,0},{20,4},{24,8},{28,12},{1,17},{... | collective-permute-start | bytes 491528 | tf_op jit(solution)/shard_map/ppermute | solution.py:118
  87.0 5.3 %collective-permute-done.13.refs_3_ = f32[16,2048]{1,0:T(8,128)S(1)} collective-permute-done((f32[16,2048]{1,0:T(8,128)S(1)}, f32[16,2048]{1,0:T(8,128)S(1)}, u32[]{:S(2)}, u32[]{:S(2)}) %collective-permute-start.13) | collective-permute-done | bytes 131104 | tf_op jit(solution)/shard_map/ppermute | solution.py:118
  93.6 1.9 %collective-permute-done.22.refs_8_ = f32[16,2304]{1,0:T(8,128)S(1)} collective-permute-done((f32[16,2304]{1,0:T(8,128)S(1)}, f32[16,2304]{1,0:T(8,128)S(1)}, u32[]{:S(2)}, u32[]{:S(2)}) %collective-permute-start.22) | collective-permute-done | bytes 147488 | tf_op jit(solution)/shard_map/ppermute | solution.py:118
  96.8 6.3 %collective-permute-done.32.refs_15_ = f32[16,2560]{1,0:T(8,128)S(1)} collective-permute-done((f32[16,2560]{1,0:T(8,128)S(1)}, f32[16,2560]{1,0:T(8,128)S(1)}, u32[]{:S(2)}, u32[]{:S(2)}) %collective-permute-start.32) | collective-permute-done | bytes 163872 | tf_op jit(solution)/shard_map/ppermute | solution.py:118
  105.2 1.7 %collective-permute-start.33 = (f32[16,2048]{1,0:T(8,128)S(1)}, f32[16,2048]{1,0:T(8,128)S(1)}, u32[]{:S(2)}, u32[]{:S(2)}) collective-permute-start(f32[16,2048]{1,0:T(8,128)S(1)} %slice.78), channel_id=1, source_target_pairs={{0,8},{4,12},{8,0},{12,4},{16,24},{20,28},{24,16},{28,20},{1,9},{5... | collective-permute-start | bytes 393224 | tf_op jit(solution)/shard_map/ppermute | solution.py:118
  107.3 2.6 %collective-permute-done.30.refs_13_ = f32[16,2048]{1,0:T(8,128)S(1)} collective-permute-done((f32[16,2048]{1,0:T(8,128)S(1)}, f32[16,2048]{1,0:T(8,128)S(1)}, u32[]{:S(2)}, u32[]{:S(2)}) %collective-permute-start.30) | collective-permute-done | bytes 131104 | tf_op jit(solution)/shard_map/ppermute | solution.py:118
  110.2 1.7 %collective-permute-done.34.refs_17_ = f32[16,2048]{1,0:T(8,128)S(1)} collective-permute-done((f32[16,2048]{1,0:T(8,128)S(1)}, f32[16,2048]{1,0:T(8,128)S(1)}, u32[]{:S(2)}, u32[]{:S(2)}) %collective-permute-start.34) | collective-permute-done | bytes 131104 | tf_op jit(solution)/shard_map/ppermute | solution.py:118
  111.9 2.2 %combine.1 = (f32[64,4096]{1,0:T(8,128)}, f32[64,4096]{1,0:T(8,128)}) custom-call(s32[6]{0:T(128)S(1)} %stack.27.place_ref, f32[16,4096]{1,0:T(8,128)S(1)} %get-tuple-element.40.base_ref.refs_0_, f32[16,4096]{1,0:T(8,128)S(1)} %collective-permute-done.11.refs_1_, f32[16,2048]{1,0:T(8,128)S(1)} %collective-permute-done.12.refs_2_, ...), custom_call_target="tpu_custom_call" | custom-call | tf_op jit(solution)/shard_map/combine/pallas_call | solution.py:431
  (81 shorter events, 31.1 us)
Async XLA Ops:
  2.3 7.8 %collective-permute-start.3 = (f32[16,1024]{1,0:T(8,128)S(1)}, f32[16,1024]{1,0:T(8,128)S(1)}, u32[]{:S(2)}, u32[]{:S(2)}) collective-permute-start(f32[16,1024]{1,0:T(8,128)S(1)} %get-tuple-element.31), channel_id=1, source_target_pairs={{0,16},{4,20},{8,24},{12,28},{16,0},{20,4},{24,8},{28,12},{1,17},{... | collective-permute-start | bytes 196616 | tf_op jit(solution)/shard_map/ppermute | solution.py:118
  6.4 20.7 %collective-permute-start.7 = (f32[16,1024]{1,0:T(8,128)S(1)}, f32[16,1024]{1,0:T(8,128)S(1)}, u32[]{:S(2)}, u32[]{:S(2)}) collective-permute-start(f32[16,1024]{1,0:T(8,128)S(1)} %get-tuple-element.33), channel_id=1, source_target_pairs={{0,4},{4,0},{8,12},{12,8},{16,20},{20,16},{24,28},{28,24},{1,5},{5... | collective-permute-start | bytes 196616 | tf_op jit(solution)/shard_map/ppermute | solution.py:118
  7.9 19.2 %collective-permute-start = (s32[64,1024]{1,0:T(8,128)S(1)}, s32[64,1024]{1,0:T(8,128)S(1)}, u32[]{:S(2)}, u32[]{:S(2)}) collective-permute-start(s32[64,1024]{1,0:T(8,128)S(1)} %bitcast.11), channel_id=1, source_target_pairs={{0,4},{4,0},{8,12},{12,8},{16,20},{20,16},{24,28},{28,24},{1,5},{5... | collective-permute-start | bytes 786440 | tf_op jit(solution)/shard_map/ppermute | solution.py:118
  10.1 13.0 %collective-permute-start.6 = (s32[32,1024]{1,0:T(8,128)S(1)}, s32[32,1024]{1,0:T(8,128)S(1)}, u32[]{:S(2)}, u32[]{:S(2)}) collective-permute-start(s32[32,1024]{1,0:T(8,128)S(1)} %get-tuple-element.62), channel_id=1, source_target_pairs={{0,16},{4,20},{8,24},{12,28},{16,0},{20,4},{24,8},{28,12},{1,17},{... | collective-permute-start | bytes 393224 | tf_op jit(solution)/shard_map/ppermute | solution.py:118
  11.7 13.7 %collective-permute-start.1 = (s32[32,1024]{1,0:T(8,128)S(1)}, s32[32,1024]{1,0:T(8,128)S(1)}, u32[]{:S(2)}, u32[]{:S(2)}) collective-permute-start(s32[32,1024]{1,0:T(8,128)S(1)} %get-tuple-element.63), channel_id=1, source_target_pairs={{0,16},{4,20},{8,24},{12,28},{16,0},{20,4},{24,8},{28,12},{1,17},{... | collective-permute-start | bytes 393224 | tf_op jit(solution)/shard_map/ppermute | solution.py:118
  13.1 18.1 %collective-permute-start.5 = (f32[16,1024]{1,0:T(8,128)S(1)}, f32[16,1024]{1,0:T(8,128)S(1)}, u32[]{:S(2)}, u32[]{:S(2)}) collective-permute-start(f32[16,1024]{1,0:T(8,128)S(1)} %get-tuple-element.65), channel_id=1, source_target_pairs={{0,4},{4,0},{8,12},{12,8},{16,20},{20,16},{24,28},{28,24},{1,5},{5... | collective-permute-start | bytes 196616 | tf_op jit(solution)/shard_map/ppermute | solution.py:118
  23.0 8.2 %collective-permute-start.9 = (s32[32,1024]{1,0:T(8,128)S(1)}, s32[32,1024]{1,0:T(8,128)S(1)}, u32[]{:S(2)}, u32[]{:S(2)}) collective-permute-start(s32[32,1024]{1,0:T(8,128)S(1)} %collective-permute-done.6.far0_ref.l2.far_ref), channel_id=1, source_target_pairs={{0,4},{4,0},{8,12},{12,8},{16,20},{20,16},{24,28},{28,24},{1,5},{5... | collective-permute-start | bytes 393224 | tf_op jit(solution)/shard_map/ppermute | solution.py:118
  25.4 6.8 %collective-permute-start.2 = (s32[32,1024]{1,0:T(8,128)S(1)}, s32[32,1024]{1,0:T(8,128)S(1)}, u32[]{:S(2)}, u32[]{:S(2)}) collective-permute-start(s32[32,1024]{1,0:T(8,128)S(1)} %collective-permute-done.1.far1_ref.l2.far_ref), channel_id=1, source_target_pairs={{0,4},{4,0},{8,12},{12,8},{16,20},{20,16},{24,28},{28,24},{1,5},{5... | collective-permute-start | bytes 393224 | tf_op jit(solution)/shard_map/ppermute | solution.py:118
  32.1 6.2 %collective-permute-start.10 = (f32[16,2048]{1,0:T(8,128)S(1)}, f32[16,2048]{1,0:T(8,128)S(1)}, u32[]{:S(2)}, u32[]{:S(2)}) collective-permute-start(f32[16,2048]{1,0:T(8,128)S(1)} %shard_map.44.mine_ref), channel_id=1, source_target_pairs={{0,8},{4,12},{8,0},{12,4},{16,24},{20,28},{24,16},{28,20},{1,9},{5... | collective-permute-start | bytes 393224 | tf_op jit(solution)/shard_map/ppermute | solution.py:118
  33.0 7.2 %collective-permute-start.8 = (f32[16,2048]{1,0:T(8,128)S(1)}, f32[16,2048]{1,0:T(8,128)S(1)}, u32[]{:S(2)}, u32[]{:S(2)}) collective-permute-start(f32[16,2048]{1,0:T(8,128)S(1)} %shard_map.43.mine_ref), channel_id=1, source_target_pairs={{0,8},{4,12},{8,0},{12,4},{16,24},{20,28},{24,16},{28,20},{1,9},{5... | collective-permute-start | bytes 393224 | tf_op jit(solution)/shard_map/ppermute | solution.py:118
  43.9 6.6 %collective-permute-start.17 = (f32[16,2176]{1,0:T(8,128)S(1)}, f32[16,2176]{1,0:T(8,128)S(1)}, u32[]{:S(2)}, u32[]{:S(2)}) collective-permute-start(f32[16,2176]{1,0:T(8,128)S(1)} %slice.71.mine_ref), channel_id=1, source_target_pairs={{0,2},{1,3},{2,0},{3,1},{4,6},{5,7},{6,4},{7,5},{8,10},{9,11},{10,... | collective-permute-start | bytes 417800 | tf_op jit(solution)/shard_map/ppermute | solution.py:118
  45.5 35.6 %collective-permute-start.12 = (f32[16,2048]{1,0:T(8,128)S(1)}, f32[16,2048]{1,0:T(8,128)S(1)}, u32[]{:S(2)}, u32[]{:S(2)}) collective-permute-start(f32[16,2048]{1,0:T(8,128)S(1)} %slice_select_fusion.2), channel_id=1, source_target_pairs={{0,16},{4,20},{8,24},{12,28},{16,0},{20,4},{24,8},{28,12},{1,17},{... | collective-permute-start | bytes 393224 | tf_op jit(solution)/shard_map/ppermute | solution.py:118
  46.5 6.8 %collective-permute-start.16 = (f32[16,2048]{1,0:T(8,128)S(1)}, f32[16,2048]{1,0:T(8,128)S(1)}, u32[]{:S(2)}, u32[]{:S(2)}) collective-permute-start(f32[16,2048]{1,0:T(8,128)S(1)} %slice.70.mine_ref), channel_id=1, source_target_pairs={{0,2},{1,3},{2,0},{3,1},{4,6},{5,7},{6,4},{7,5},{8,10},{9,11},{10,... | collective-permute-start | bytes 393224 | tf_op jit(solution)/shard_map/ppermute | solution.py:118
  54.7 5.7 %collective-permute-start.19 = (f32[16,2304]{1,0:T(8,128)S(1)}, f32[16,2304]{1,0:T(8,128)S(1)}, u32[]{:S(2)}, u32[]{:S(2)}) collective-permute-start(f32[16,2304]{1,0:T(8,128)S(1)} %get-tuple-element.46.mine_ref), channel_id=1, source_target_pairs={{0,8},{4,12},{8,0},{12,4},{16,24},{20,28},{24,16},{28,20},{1,9},{5... | collective-permute-start | bytes 442376 | tf_op jit(solution)/shard_map/ppermute | solution.py:118
  56.4 6.2 %collective-permute-start.18 = (f32[16,2048]{1,0:T(8,128)S(1)}, f32[16,2048]{1,0:T(8,128)S(1)}, u32[]{:S(2)}, u32[]{:S(2)}) collective-permute-start(f32[16,2048]{1,0:T(8,128)S(1)} %shard_map.49.mine_ref), channel_id=1, source_target_pairs={{0,8},{4,12},{8,0},{12,4},{16,24},{20,28},{24,16},{28,20},{1,9},{5... | collective-permute-start | bytes 393224 | tf_op jit(solution)/shard_map/ppermute | solution.py:118
  66.3 6.5 %collective-permute-start.26 = (f32[16,2304]{1,0:T(8,128)S(1)}, f32[16,2304]{1,0:T(8,128)S(1)}, u32[]{:S(2)}, u32[]{:S(2)}) collective-permute-start(f32[16,2304]{1,0:T(8,128)S(1)} %slice.75.mine_ref), channel_id=1, source_target_pairs={{0,2},{1,3},{2,0},{3,1},{4,6},{5,7},{6,4},{7,5},{8,10},{9,11},{10,... | collective-permute-start | bytes 442376 | tf_op jit(solution)/shard_map/ppermute | solution.py:118
  67.9 14.7 %collective-permute-start.21 = (f32[16,2304]{1,0:T(8,128)S(1)}, f32[16,2304]{1,0:T(8,128)S(1)}, u32[]{:S(2)}, u32[]{:S(2)}) collective-permute-start(f32[16,2304]{1,0:T(8,128)S(1)} %pad_maximum_fusion.3), channel_id=1, source_target_pairs={{0,16},{4,20},{8,24},{12,28},{16,0},{20,4},{24,8},{28,12},{1,17},{... | collective-permute-start | bytes 442376 | tf_op jit(solution)/shard_map/ppermute | solution.py:118
  69.5 5.9 %collective-permute-start.25 = (f32[16,2048]{1,0:T(8,128)S(1)}, f32[16,2048]{1,0:T(8,128)S(1)}, u32[]{:S(2)}, u32[]{:S(2)}) collective-permute-start(f32[16,2048]{1,0:T(8,128)S(1)} %slice.74.mine_ref), channel_id=1, source_target_pairs={{0,2},{1,3},{2,0},{3,1},{4,6},{5,7},{6,4},{7,5},{8,10},{9,11},{10,... | collective-permute-start | bytes 393224 | tf_op jit(solution)/shard_map/ppermute | solution.py:118
  77.1 6.6 %collective-permute-start.27 = (f32[16,2560]{1,0:T(8,128)S(1)}, f32[16,2560]{1,0:T(8,128)S(1)}, u32[]{:S(2)}, u32[]{:S(2)}) collective-permute-start(f32[16,2560]{1,0:T(8,128)S(1)} %get-tuple-element.54), channel_id=1, source_target_pairs={{0,8},{4,12},{8,0},{12,4},{16,24},{20,28},{24,16},{28,20},{1,9},{5... | collective-permute-start | bytes 491528 | tf_op jit(solution)/shard_map/ppermute | solution.py:118
  79.1 6.0 %collective-permute-start.29 = (f32[16,2048]{1,0:T(8,128)S(1)}, f32[16,2048]{1,0:T(8,128)S(1)}, u32[]{:S(2)}, u32[]{:S(2)}) collective-permute-start(f32[16,2048]{1,0:T(8,128)S(1)} %shard_map.54), channel_id=1, source_target_pairs={{0,8},{4,12},{8,0},{12,4},{16,24},{20,28},{24,16},{28,20},{1,9},{5... | collective-permute-start | bytes 393224 | tf_op jit(solution)/shard_map/ppermute | solution.py:118
  80.5 23.3 %collective-permute-start.11 = (f32[16,4096]{1,0:T(8,128)S(1)}, f32[16,4096]{1,0:T(8,128)S(1)}, u32[]{:S(2)}, u32[]{:S(2)}) collective-permute-start(f32[16,4096]{1,0:T(8,128)S(1)} %get-tuple-element.40.base_ref.refs_0_), channel_id=1, source_target_pairs={{0,4},{4,0},{8,12},{12,8},{16,20},{20,16},{24,28},{28,24},{1,5},{5... | collective-permute-start | bytes 786440 | tf_op jit(solution)/shard_map/ppermute | solution.py:118
  81.0 11.3 %collective-permute-start.13 = (f32[16,2048]{1,0:T(8,128)S(1)}, f32[16,2048]{1,0:T(8,128)S(1)}, u32[]{:S(2)}, u32[]{:S(2)}) collective-permute-start(f32[16,2048]{1,0:T(8,128)S(1)} %collective-permute-done.12.refs_2_), channel_id=1, source_target_pairs={{0,4},{4,0},{8,12},{12,8},{16,20},{20,16},{24,28},{28,24},{1,5},{5... | collective-permute-start | bytes 393224 | tf_op jit(solution)/shard_map/ppermute | solution.py:118
  82.6 12.9 %collective-permute-start.22 = (f32[16,2304]{1,0:T(8,128)S(1)}, f32[16,2304]{1,0:T(8,128)S(1)}, u32[]{:S(2)}, u32[]{:S(2)}) collective-permute-start(f32[16,2304]{1,0:T(8,128)S(1)} %collective-permute-done.21.refs_7_), channel_id=1, source_target_pairs={{0,4},{4,0},{8,12},{12,8},{16,20},{20,16},{24,28},{28,24},{1,5},{5... | collective-permute-start | bytes 442376 | tf_op jit(solution)/shard_map/ppermute | solution.py:118
  85.2 10.3 %collective-permute-start.31 = (f32[16,2560]{1,0:T(8,128)S(1)}, f32[16,2560]{1,0:T(8,128)S(1)}, u32[]{:S(2)}, u32[]{:S(2)}) collective-permute-start(f32[16,2560]{1,0:T(8,128)S(1)} %pad_maximum_fusion.2), channel_id=1, source_target_pairs={{0,16},{4,20},{8,24},{12,28},{16,0},{20,4},{24,8},{28,12},{1,17},{... | collective-permute-start | bytes 491528 | tf_op jit(solution)/shard_map/ppermute | solution.py:118
  92.3 12.9 %collective-permute-start.14 = (f32[32,2048]{1,0:T(8,128)S(1)}, f32[32,2048]{1,0:T(8,128)S(1)}, u32[]{:S(2)}, u32[]{:S(2)}) collective-permute-start(f32[32,2048]{1,0:T(8,128)S(1)} %pad_maximum_fusion), channel_id=1, source_target_pairs={{0,8},{4,12},{8,0},{12,4},{16,24},{20,28},{24,16},{28,20},{1,9},{5... | collective-permute-start | bytes 786440 | tf_op jit(solution)/shard_map/ppermute | solution.py:118
  92.8 14.1 %collective-permute-start.20 = (f32[16,4352]{1,0:T(8,128)S(1)}, f32[16,4352]{1,0:T(8,128)S(1)}, u32[]{:S(2)}, u32[]{:S(2)}) collective-permute-start(f32[16,4352]{1,0:T(8,128)S(1)} %get-tuple-element.49.refs_5_), channel_id=1, source_target_pairs={{0,4},{4,0},{8,12},{12,8},{16,20},{20,16},{24,28},{28,24},{1,5},{5... | collective-permute-start | bytes 835592 | tf_op jit(solution)/shard_map/ppermute | solution.py:118
  95.5 7.6 %collective-permute-start.32 = (f32[16,2560]{1,0:T(8,128)S(1)}, f32[16,2560]{1,0:T(8,128)S(1)}, u32[]{:S(2)}, u32[]{:S(2)}) collective-permute-start(f32[16,2560]{1,0:T(8,128)S(1)} %collective-permute-done.31.refs_14_), channel_id=1, source_target_pairs={{0,4},{4,0},{8,12},{12,8},{16,20},{20,16},{24,28},{28,24},{1,5},{5... | collective-permute-start | bytes 491528 | tf_op jit(solution)/shard_map/ppermute | solution.py:118
  96.0 11.3 %collective-permute-start.23 = (f32[32,2048]{1,0:T(8,128)S(1)}, f32[32,2048]{1,0:T(8,128)S(1)}, u32[]{:S(2)}, u32[]{:S(2)}) collective-permute-start(f32[32,2048]{1,0:T(8,128)S(1)} %pad_maximum_fusion.1), channel_id=1, source_target_pairs={{0,8},{4,12},{8,0},{12,4},{16,24},{20,28},{24,16},{28,20},{1,9},{5... | collective-permute-start | bytes 786440 | tf_op jit(solution)/shard_map/ppermute | solution.py:118
  103.1 6.7 %collective-permute-start.28 = (f32[16,2560]{1,0:T(8,128)S(1)}, f32[16,2560]{1,0:T(8,128)S(1)}, u32[]{:S(2)}, u32[]{:S(2)}) collective-permute-start(f32[16,2560]{1,0:T(8,128)S(1)} %add.37.refs_10_), channel_id=1, source_target_pairs={{0,4},{4,0},{8,12},{12,8},{16,20},{20,16},{24,28},{28,24},{1,5},{5... | collective-permute-start | bytes 491528 | tf_op jit(solution)/shard_map/ppermute | solution.py:118
  103.9 6.0 %collective-permute-start.30 = (f32[16,2048]{1,0:T(8,128)S(1)}, f32[16,2048]{1,0:T(8,128)S(1)}, u32[]{:S(2)}, u32[]{:S(2)}) collective-permute-start(f32[16,2048]{1,0:T(8,128)S(1)} %get-tuple-element.61.refs_12_), channel_id=1, source_target_pairs={{0,4},{4,0},{8,12},{12,8},{16,20},{20,16},{24,28},{28,24},{1,5},{5... | collective-permute-start | bytes 393224 | tf_op jit(solution)/shard_map/ppermute | solution.py:118
  105.2 5.0 %collective-permute-start.33 = (f32[16,2048]{1,0:T(8,128)S(1)}, f32[16,2048]{1,0:T(8,128)S(1)}, u32[]{:S(2)}, u32[]{:S(2)}) collective-permute-start(f32[16,2048]{1,0:T(8,128)S(1)} %slice.78), channel_id=1, source_target_pairs={{0,8},{4,12},{8,0},{12,4},{16,24},{20,28},{24,16},{28,20},{1,9},{5... | collective-permute-start | bytes 393224 | tf_op jit(solution)/shard_map/ppermute | solution.py:118
  106.9 5.0 %collective-permute-start.34 = (f32[16,2048]{1,0:T(8,128)S(1)}, f32[16,2048]{1,0:T(8,128)S(1)}, u32[]{:S(2)}, u32[]{:S(2)}) collective-permute-start(f32[16,2048]{1,0:T(8,128)S(1)} %slice.79), channel_id=1, source_target_pairs={{0,8},{4,12},{8,0},{12,4},{16,24},{20,28},{24,16},{28,20},{1,9},{5... | collective-permute-start | bytes 393224 | tf_op jit(solution)/shard_map/ppermute | solution.py:118
  (5 other events, 13.4 us)
